TPU v7x, 128 devices: a whole 4x4x4 slice. The times are simulated.
128 devices in a mesh: strip: 128 (over x, y, z, core).
Axes of the slice: x: 4, y: 4, z: 4, core: 2. Of those that a mesh axis runs over, the one named last changes fastest.
Arguments:
- params: float32 [59, 655360], P(None, 'strip'), may hold values from -26 to 26, as said below
- camera: float32 [4, 12], replicated, may hold values from -2 to 2, as said below
- send_index: int32 [16384, 80], P('strip'), may hold values from 0 to 5119, as said below
- send_count: int32 [16384], P('strip'), may hold values from 0 to 80, as said below
- tile_list: int32 [5120, 128], P('strip'), may hold values from 0 to 5119, as said below
- target: float32 [3, 2048, 640], P(None, 'strip'), may hold values from 0 to 1
Outputs:
- param_grads: float32 [59, 655360], P(None, 'strip')
Inputs may be any that keep to these rules, and one draw needn't show every extreme that they name: `send_index`: in row s * 128 + r the first send_count[s * 128 + r] entries are distinct local Gaussian numbers of device s; over all r these live entries name each of device s's 5120 Gaussians exactly once. Later entries are local Gaussian numbers that name nothing sent. `send_count`: for every sender, and for every strip, the counts sum to 5120; the largest count equals 80. `tile_list`: each row holds 128 distinct received numbers of its strip; every number 0 to 5119 of a strip stands in exactly one of the strip's lists. `params`: each Gaussian lies 2 to 6 in front of the camera of the view of the strip that receives it and projects inside the tile whose list holds it; entry 6 of every Gaussian is 1 or more. `camera`: the first nine entries of each row form a rotation matrix.
All inputs are finite; a program needn't handle non-finite values.
Results may differ from a plain program's by a relative error of at most 0.0003.
Values sent between devices are 32-bit elements; how exact they have to be, the bound alone decides.
No kernel may reach another device: no remote copies, remote signals or barrier semaphores. Data moves between devices by JAX's collectives and lax.ppermute only.
A program may use at most 64 MiB of HBM per device.

v0:
```python
import numpy as np

import jax
import jax.numpy as jnp
from jax import lax
from jax.experimental import pallas as pl
from jax.experimental.pallas import tpu as pltpu
from jax.sharding import PartitionSpec as P

VIEWS = 4
ROWS = 40
FEATS = 9
LOG2E = 1.4426950408889634
harmonic_zero = 0.28209479177387814
harmonic_one = 0.4886025119029199
harmonic_two = (
    1.0925484305920792,
    -1.0925484305920792,
    0.31539156525252005,
    -1.0925484305920792,
    0.5462742152960396,
)
harmonic_three = (
    -0.5900435899266435,
    2.890611442640554,
    -0.4570457994644658,
    0.3731763325901154,
    -0.4570457994644658,
    1.445305721320277,
    -0.5900435899266435,
)
light_term = 0.0001
contrast_term = 0.0009
F32 = jnp.float32
BF16 = jnp.bfloat16
SMEM = pl.BlockSpec(memory_space=pltpu.SMEM)
VMEM = pl.BlockSpec(memory_space=pltpu.VMEM)


def iota(shape, axis):
    return lax.broadcasted_iota(jnp.int32, shape, axis)


def dot_nt(a, b):
    return lax.dot_general(a, b, (((1,), (1,)), ((), ())), preferred_element_type=F32)


def rounded(x):
    return x.astype(BF16).astype(F32)


def pick(row, lanes):
    return jnp.take_along_axis(
        jnp.broadcast_to(row, lanes.shape), lanes, axis=1, mode="promise_in_bounds"
    )


def harmonics(along_x, along_y, along_z):
    square_x = along_x * along_x
    square_y = along_y * along_y
    square_z = along_z * along_z
    return [
        harmonic_zero + 0.0 * along_x,
        -harmonic_one * along_y,
        harmonic_one * along_z,
        -harmonic_one * along_x,
        harmonic_two[0] * along_x * along_y,
        harmonic_two[1] * along_y * along_z,
        harmonic_two[2] * (2.0 * square_z - square_x - square_y),
        harmonic_two[3] * along_x * along_z,
        harmonic_two[4] * (square_x - square_y),
        harmonic_three[0] * along_y * (3.0 * square_x - square_y),
        harmonic_three[1] * along_x * along_y * along_z,
        harmonic_three[2] * along_y * (4.0 * square_z - square_x - square_y),
        harmonic_three[3] * along_z * (2.0 * square_z - 3.0 * square_x - 3.0 * square_y),
        harmonic_three[4] * along_x * (4.0 * square_z - square_x - square_y),
        harmonic_three[5] * along_z * (square_x - square_y),
        harmonic_three[6] * along_x * (square_x - 3.0 * square_y),
    ]


def project(params, camera, focal, centre_x, centre_y):
    rotation = [[camera[3 * row + col] for col in range(3)] for row in range(3)]
    mean = [params[axis] for axis in range(3)]
    placed = [
        rotation[row][0] * mean[0]
        + rotation[row][1] * mean[1]
        + rotation[row][2] * mean[2]
        + camera[9 + row]
        for row in range(3)
    ]
    depth = placed[2]
    inverse = 1.0 / depth
    screen_x = focal * placed[0] * inverse + centre_x
    screen_y = focal * placed[1] * inverse + centre_y
    quaternion = params[6:10]
    scale = lax.rsqrt(
        quaternion[0] * quaternion[0]
        + quaternion[1] * quaternion[1]
        + quaternion[2] * quaternion[2]
        + quaternion[3] * quaternion[3]
    )
    real, imag_x, imag_y, imag_z = [part * scale for part in quaternion]
    turn = [
        [
            1.0 - 2.0 * (imag_y * imag_y + imag_z * imag_z),
            2.0 * (imag_x * imag_y - real * imag_z),
            2.0 * (imag_x * imag_z + real * imag_y),
        ],
        [
            2.0 * (imag_x * imag_y + real * imag_z),
            1.0 - 2.0 * (imag_x * imag_x + imag_z * imag_z),
            2.0 * (imag_y * imag_z - real * imag_x),
        ],
        [
            2.0 * (imag_x * imag_z - real * imag_y),
            2.0 * (imag_y * imag_z + real * imag_x),
            1.0 - 2.0 * (imag_x * imag_x + imag_y * imag_y),
        ],
    ]
    scales = [jnp.exp(part) for part in params[3:6]]
    near = focal * inverse
    slant = [-near * placed[0] * inverse, -near * placed[1] * inverse]
    facing = [
        [near * rotation[row][col] + slant[row] * rotation[2][col] for col in range(3)]
        for row in range(2)
    ]
    stretch = [
        [
            (
                facing[row][0] * turn[0][col]
                + facing[row][1] * turn[1][col]
                + facing[row][2] * turn[2][col]
            )
            * scales[col]
            for col in range(3)
        ]
        for row in range(2)
    ]
    cov_xx = (
        stretch[0][0] * stretch[0][0]
        + stretch[0][1] * stretch[0][1]
        + stretch[0][2] * stretch[0][2]
        + 0.3
    )
    cov_xy = (
        stretch[0][0] * stretch[1][0]
        + stretch[0][1] * stretch[1][1]
        + stretch[0][2] * stretch[1][2]
    )
    cov_yy = (
        stretch[1][0] * stretch[1][0]
        + stretch[1][1] * stretch[1][1]
        + stretch[1][2] * stretch[1][2]
        + 0.3
    )
    over = 1.0 / (cov_xx * cov_yy - cov_xy * cov_xy)
    shrink = 1.0 / jnp.sqrt(placed[0] * placed[0] + placed[1] * placed[1] + depth * depth)
    heading = [
        (
            rotation[0][col] * placed[0]
            + rotation[1][col] * placed[1]
            + rotation[2][col] * placed[2]
        )
        * shrink
        for col in range(3)
    ]
    basis = harmonics(heading[0], heading[1], heading[2])
    colour = []
    for channel in range(3):
        total = 0.5 + basis[0] * params[11 + channel]
        for k in range(1, 16):
            total = total + basis[k] * params[11 + 3 * k + channel]
        colour.append(total)
    return [
        screen_x,
        screen_y,
        cov_yy * over,
        -cov_xy * over,
        cov_xx * over,
        colour[0],
        colour[1],
        colour[2],
    ]


def log_sigmoid(logit):
    return jnp.minimum(logit, 0.0) - jnp.log(1.0 + jnp.exp(-jnp.abs(logit)))


def send_views(count_ref, strips):
    per_view = strips // VIEWS
    offset = per_view // 2
    runs = []
    for strip in range(strips):
        view = (strip + offset) % strips // per_view
        if not runs or runs[-1][1] != view:
            runs.append([strip, view])
    return runs


def compact_ints(chunk_ref, count_ref, out_ref, steps):
    lane = iota((1, 128), 1)

    def step(number, carry):
        start, held = carry
        live = count_ref[number]
        shift = start & 127
        row = start >> 7
        chunk = pltpu.roll(chunk_ref[pl.ds(number, 1), :], shift, axis=1)
        held = jnp.where(lane >= shift, chunk, held)
        out_ref[pl.ds(row, 1), :] = held
        held = jnp.where(shift + live >= 128, chunk, held)
        return start + live, held

    lax.fori_loop(0, steps, step, (jnp.int32(0), jnp.zeros((1, 128), jnp.int32)), unroll=4)


def compact_feats(chunk_ref, count_ref, table_ref, steps):
    lane = iota((8, 128), 1)

    def step(number, carry):
        start, held, last = carry
        live = count_ref[number]
        shift = start & 127
        row = start >> 7
        chunk = chunk_ref[number]
        first = pltpu.roll(chunk, 48, axis=1)
        second = pltpu.roll(pltpu.roll(chunk, 96, axis=1), 7, axis=0)
        ninth = jnp.where(lane < 48, first, second)
        chunk = pltpu.roll(chunk, shift, axis=1)
        ninth = pltpu.roll(ninth, shift, axis=1)
        fresh = lane >= shift
        held = jnp.where(fresh, chunk, held)
        last = jnp.where(fresh, ninth, last)
        base = pl.multiple_of(row * 16, 16)
        table_ref[pl.ds(base, 8), :] = held
        table_ref[pl.ds(base + 8, 8), :] = last
        crossed = shift + live >= 128
        held = jnp.where(crossed, chunk, held)
        last = jnp.where(crossed, ninth, last)
        return start + live, held, last

    zero = jnp.zeros((8, 128), F32)
    lax.fori_loop(0, steps, step, (jnp.int32(0), zero, zero), unroll=4)


def expand_feats(table_ref, count_ref, out_ref, steps):
    lane = iota((8, 128), 1)
    sub = iota((8, 128), 0)

    def step(number, start):
        live = count_ref[number]
        shift = start & 127
        base = pl.multiple_of((start >> 7) * 16, 16)
        back = (128 - shift) & 127
        here = lane < 128 - shift
        main = jnp.where(
            here,
            pltpu.roll(table_ref[pl.ds(base, 8), :], back, axis=1),
            pltpu.roll(table_ref[pl.ds(base + 16, 8), :], back, axis=1),
        )
        ninth = jnp.where(
            here,
            pltpu.roll(table_ref[pl.ds(base + 8, 8), :], back, axis=1),
            pltpu.roll(table_ref[pl.ds(base + 24, 8), :], back, axis=1),
        )
        tail = jnp.where(sub == 0, pltpu.roll(ninth, 80, axis=1), pltpu.roll(ninth, 32, axis=1))
        tail = jnp.where(sub < 2, tail, live.astype(F32))
        out_ref[number] = jnp.where(lane < 80, main, tail)
        return start + live

    lax.fori_loop(0, steps, step, jnp.int32(0), unroll=4)


def put_feature(table_ref, block, feature, value):
    table_ref[pl.ds(block * 128 + feature, 8, stride=16), :] = value
    if feature == 8:
        table_ref[pl.ds(block * 128 + 9, 8, stride=16), :] = value


def invert(rows_ref, out_ref):
    high = iota((ROWS, 128), 0)
    low = iota((128, 128), 0)
    lane = iota((ROWS, 128), 1).astype(F32)
    total = jnp.zeros((2 * ROWS, 128), F32)
    for pair in range(ROWS // 2):
        lefts = []
        rights = []
        for row in (2 * pair, 2 * pair + 1):
            number = rows_ref[row : row + 1, :]
            same = high == (number >> 7)
            lefts.append(
                jnp.concatenate([jnp.where(same, float(row), 0.0), jnp.where(same, lane, 0.0)], 0)
            )
            rights.append(jnp.where(low == (number & 127), 1.0, 0.0))
        total = total + dot_nt(
            jnp.concatenate(lefts, 1).astype(BF16), jnp.concatenate(rights, 1).astype(BF16)
        )
    out_ref[...] = (total[:ROWS] * 128.0 + total[ROWS:]).astype(jnp.int32)


def select_camera(camera_ref, place, run_starts):
    values = []
    for entry in range(12):
        value = jnp.full(place.shape, camera_ref[run_starts[0][1], entry], F32)
        for start, view in run_starts[1:]:
            value = jnp.where(place >= start, camera_ref[view, entry], value)
        values.append(value)
    return values


def run_bounds(count_ref, strips):
    runs = send_views(count_ref, strips)
    bounds = [(jnp.int32(0), runs[0][1])]
    for (first, _), (last, view) in zip(runs[:-1], runs[1:]):
        begin = bounds[-1][0]
        total = lax.fori_loop(
            first, last, lambda number, sum_: sum_ + count_ref[number], begin, unroll=True
        )
        bounds.append((total, view))
    return bounds


def owner_kernel(focal, centre_x, centre_y):
    def kernel(
        camera_ref, count_ref, params_ref, index_ref, out_ref, place_ref,
        wide_ref, rows_ref, feats_ref, table_ref,
    ):
        strips = index_ref.shape[0]
        wide_ref[:, 0:80] = index_ref[...]
        compact_ints(wide_ref, count_ref, rows_ref, strips)
        invert(rows_ref, place_ref)
        bounds = run_bounds(count_ref, strips)

        def project_block(block, carry):
            rows = pl.ds(block * 8, 8)
            camera = select_camera(camera_ref, place_ref[rows, :], bounds)
            params = [params_ref[number, rows, :] for number in range(59)]
            feats = project(params, camera, focal, centre_x, centre_y)
            feats.append(log_sigmoid(params[10]))
            for feature in range(FEATS):
                feats_ref[feature, rows, :] = feats[feature]
            return carry

        lax.fori_loop(0, 5, project_block, 0)

        def gather_block(block, carry):
            number = rows_ref[pl.ds(block * 8, 8), :]
            high = number >> 7
            low = number & 127
            got = [jnp.zeros((8, 128), F32)] * FEATS
            for row in range(ROWS):
                same = high == row
                for feature in range(FEATS):
                    value = pick(feats_ref[feature, row : row + 1, :], low)
                    got[feature] = jnp.where(same, value, got[feature])
            for feature in range(FEATS):
                put_feature(table_ref, block, feature, got[feature])
            return carry

        lax.fori_loop(0, 5, gather_block, 0)
        expand_feats(table_ref, count_ref, out_ref, strips)

    return kernel


def entry_basis():
    pixel = np.arange(256)
    x = pixel % 16 - 7.5
    y = pixel // 16 - 7.5
    return np.stack([np.ones(256), x, y, x * x, x * y, y * y]).astype(np.float32)


def swap_tiles(x):
    sub = iota((8, 128), 0)
    group = iota((8, 128), 1) >> 4
    for k in (1, 2, 4):
        up = pltpu.roll(pltpu.roll(x, 8 - k, axis=0), 16 * k, axis=1)
        down = pltpu.roll(pltpu.roll(x, k, axis=0), 128 - 16 * k, axis=1)
        s = (sub & k) != 0
        g = (group & k) != 0
        x = jnp.where(s == g, x, jnp.where(g, up, down))
    return x


def expand_block(lines_ref, row, basis):
    lines = lines_ref[pl.ds(pl.multiple_of(row * 24, 8), 24), :]
    columns = lines.T
    return columns, jnp.dot(columns.astype(BF16), basis, preferred_element_type=F32)


def render_kernel(
    count_ref, top_ref, chunks_ref, list_ref, across_ref, basis_ref,
    image_ref, first_ref, last_ref, lines_ref, entries_ref,
    table_ref, power_ref, column_ref,
):
    compact_feats(chunks_ref, count_ref, table_ref, chunks_ref.shape[0])
    top = top_ref[0]

    def entry_block(block, carry):
        rows = pl.ds(block * 8, 8)
        number = list_ref[rows, :]
        high = number >> 7
        low = number & 127
        got = [jnp.zeros((8, 128), F32)] * FEATS
        for row in range(ROWS):
            same = high == row
            for feature in range(FEATS):
                value = pick(table_ref[row * 16 + feature : row * 16 + feature + 1, :], low)
                got[feature] = jnp.where(same, value, got[feature])
        x = got[0] - across_ref[rows, :]
        y = got[1] - top
        a, b, c = got[2:5]
        for slot, value in enumerate((x, y, a, b, c)):
            entries_ref[slot, rows, :] = value
        terms = [
            got[8] - 0.5 * (a * x * x + c * y * y) - b * x * y,
            a * x + b * y,
            c * y + b * x,
            -0.5 * a,
            -b,
            -0.5 * c,
        ]
        for slot, term in enumerate(terms):
            term = term * LOG2E
            for part in range(3):
                piece = rounded(term)
                lines_ref[pl.ds(block * 192 + slot * 3 + part, 8, stride=24), :] = piece
                term = term - piece
        for channel in range(3):
            lines_ref[pl.ds(block * 192 + 18 + channel, 8, stride=24), :] = got[5 + channel]
            lines_ref[pl.ds(block * 192 + 21 + channel, 8, stride=24), :] = jnp.zeros((8, 128), F32)
        return carry

    lax.fori_loop(0, 5, entry_block, 0)
    basis = basis_ref[...]

    def blend(turn, carry):
        through = list(carry[0:10])
        shown = list(carry[10:40])
        for part in range(5):
            columns, power = expand_block(lines_ref, turn * 5 + part, basis)
            power_ref[part * 128 : part * 128 + 128, :] = power
            column_ref[part * 128 : part * 128 + 128, 0:24] = columns
        for entry in range(16):
            for group in range(5):
                at = (entry * 5 + group) * 8
                columns = column_ref[at : at + 8, :]
                colour = [
                    jnp.broadcast_to(columns[:, 18 + channel : 19 + channel], (8, 128))
                    for channel in range(3)
                ]
                for half in range(2):
                    slot = group * 2 + half
                    alpha = jnp.exp2(power_ref[at : at + 8, half * 128 : half * 128 + 128])
                    weight = alpha * through[slot]
                    through[slot] = through[slot] - weight
                    for channel in range(3):
                        shown[slot * 3 + channel] = (
                            shown[slot * 3 + channel] + weight * colour[channel]
                        )
        return tuple(through + shown)

    one = jnp.ones((8, 128), F32)
    zero = jnp.zeros((8, 128), F32)
    final = lax.fori_loop(0, 8, blend, (one,) * 10 + (zero,) * 30)
    for group in range(5):
        for channel in range(3):
            for half in range(2):
                image_ref[channel, group, half * 8 : half * 8 + 8, :] = swap_tiles(
                    final[10 + (group * 2 + half) * 3 + channel]
                )
            at = (channel * 5 + group) * 10
            first_ref[at : at + 10, :] = image_ref[channel, group, 0:10, :]
            last_ref[at : at + 10, :] = image_ref[channel, group, 6:16, :]


def window_weights():
    offsets = np.arange(11, dtype=np.float64) - 5.0
    raw = np.exp(-offsets * offsets / 4.5)
    return [float(value) for value in raw / raw.sum()]


WINDOW = window_weights()


def tap_sum(load):
    total = WINDOW[5] * load(5)
    for k in range(5):
        total = total + WINDOW[k] * (load(k) + load(10 - k))
    return total


def down_rows(field_ref, slot, out_ref):
    for tile in range(5):
        for channel in range(3):
            base = channel * 40
            out_ref[base : base + 32, :] = tap_sum(
                lambda k: field_ref[tile, base + k : base + k + 32, :]
            )
        yield tile, out_ref[...].T


def extend(ext_ref, own, above, below, keep_above, keep_below):
    for tile in range(5):
        for channel in range(3):
            base = channel * 40
            ext_ref[tile, base : base + 10, :] = above(channel, tile) * keep_above
            ext_ref[tile, base + 10 : base + 26, :] = own(channel, tile)
            ext_ref[tile, base + 26 : base + 36, :] = below(channel, tile) * keep_below
            ext_ref[tile, base + 36 : base + 40, :] = jnp.zeros((4, 128), F32)
        ext_ref[tile, 120:128, :] = jnp.zeros((8, 128), F32)


def clear_ends(ref, slot):
    ref[slot, 0:8, :] = jnp.zeros((8, 128), F32)
    ref[slot, 648:656, :] = jnp.zeros((8, 128), F32)


def truth_kernel(
    keep_ref, own_ref, above_ref, below_ref, ext_ref, mean_ref, power_ref,
    field_ref, rows_ref, cols_ref,
):
    lanes = lambda tile: slice(tile * 128, tile * 128 + 128)
    extend(
        ext_ref,
        lambda channel, tile: own_ref[channel, :, lanes(tile)],
        lambda channel, tile: above_ref[channel, :, lanes(tile)],
        lambda channel, tile: below_ref[channel, :, lanes(tile)],
        keep_ref[0],
        keep_ref[1],
    )
    rows_ref[...] = jnp.zeros((128, 128), F32)
    for tile in range(5):
        field_ref[tile] = ext_ref[tile] * ext_ref[tile]
    for slot, (source, out_ref) in enumerate(((ext_ref, mean_ref), (field_ref, power_ref))):
        clear_ends(cols_ref, slot)
        for tile, turned in down_rows(source, slot, rows_ref):
            cols_ref[slot, 8 + tile * 128 : 136 + tile * 128, :] = turned

        def columns(step, carry, slot=slot, out_ref=out_ref):
            base = step * 64
            out_ref[pl.ds(base, 64), :] = tap_sum(
                lambda k: cols_ref[slot, pl.ds(base + 3 + k, 64), :]
            )
            return carry

        lax.fori_loop(0, 10, columns, 0)


def invert_kernel(list_ref, out_ref):
    invert(list_ref, out_ref)


def gradient_kernel(
    count_ref, keep_ref, image_ref, above_ref, below_ref, truth_ref, mean_y_ref, power_y_ref,
    lines_ref, entries_ref, place_ref, basis_ref, moment_ref,
    out_ref,
    ext_ref, square_ref, cross_ref, rows_ref, cols_ref, parts_ref,
    alpha_ref, weight_ref, column_ref, power_ref, light_ref, split_ref,
    sums_ref, tint_ref, feats_ref, table_ref,
):
    keep_above = keep_ref[0]
    keep_below = keep_ref[1]
    extend(
        ext_ref,
        lambda channel, tile: image_ref[channel, tile],
        lambda channel, tile: above_ref[(channel * 5 + tile) * 10 : (channel * 5 + tile) * 10 + 10, :],
        lambda channel, tile: below_ref[(channel * 5 + tile) * 10 : (channel * 5 + tile) * 10 + 10, :],
        keep_above,
        keep_below,
    )
    for tile in range(5):
        square_ref[tile] = ext_ref[tile] * ext_ref[tile]
        cross_ref[tile] = ext_ref[tile] * truth_ref[tile]
    rows_ref[...] = jnp.zeros((128, 128), F32)
    for slot, source in enumerate((ext_ref, square_ref, cross_ref)):
        clear_ends(cols_ref, slot)
        clear_ends(parts_ref, slot)
        for tile, turned in down_rows(source, slot, rows_ref):
            cols_ref[slot, 8 + tile * 128 : 136 + tile * 128, :] = turned
    lane = iota((8, 128), 1)
    row = lane - jnp.where(lane >= 80, 80, jnp.where(lane >= 40, 40, 0))
    live = jnp.where(row < 5, keep_above, jnp.where(row >= 21, keep_below, 1.0))
    live = jnp.where((row < 26) & (lane < 120), live, 0.0)[0:1, :]

    def similarity(step, carry):
        base = step * 32
        mean_x, power_x, cross = [
            tap_sum(lambda k: cols_ref[slot, pl.ds(base + 3 + k, 32), :]) for slot in range(3)
        ]
        mean_y = mean_y_ref[pl.ds(base, 32), :]
        power_y = power_y_ref[pl.ds(base, 32), :]
        both = mean_x * mean_y
        squares = mean_x * mean_x + mean_y * mean_y
        light_up = 2.0 * both + light_term
        light_down = squares + light_term
        sharp_up = 2.0 * (cross - both) + contrast_term
        sharp_down = power_x + power_y - squares + contrast_term
        over = 1.0 / (light_down * sharp_down)
        score = light_up * sharp_up * over
        scale = live * over
        cross_grad = -2.0 * light_up * scale
        power_grad = score * light_down * scale
        mean_grad = (
            -2.0 * mean_y * (sharp_up - light_up) + 2.0 * mean_x * score * (sharp_down - light_down)
        ) * scale
        at = pl.ds(base + 8, 32)
        parts_ref[0, at, :] = mean_grad
        parts_ref[1, at, :] = power_grad
        parts_ref[2, at, :] = cross_grad
        return carry

    lax.fori_loop(0, 20, similarity, 0)
    for tile in range(5):
        for slot in range(3):
            turned = tap_sum(
                lambda k: parts_ref[slot, tile * 128 + 3 + k : tile * 128 + 131 + k, :]
            ).T
            (square_ref, cross_ref, cols_ref)[slot][0, 0:128, :] = turned
        for channel in range(3):
            base = channel * 40
            down = [
                tap_sum(lambda k: (square_ref, cross_ref, cols_ref)[slot][0, base + k : base + k + 16, :])
                for slot in range(3)
            ]
            own = image_ref[channel, tile]
            truth = truth_ref[tile, base + 10 : base + 26, :]
            pull = down[0] + 2.0 * own * down[1] + truth * down[2]
            for half in range(2):
                value = swap_tiles(pull[half * 8 : half * 8 + 8])
                light_ref[tile * 6 + half * 3 + channel] = value
                for part in range(3):
                    piece = rounded(value)
                    split_ref[half, pl.ds(tile * 128 + channel * 3 + part, 8, stride=16), :] = piece
                    value = value - piece
    basis = basis_ref[...]

    def forward(turn, carry):
        through = list(carry)
        for part in range(5):
            columns, power = expand_block(lines_ref, turn * 5 + part, basis)
            power_ref[part * 128 : part * 128 + 128, :] = power
            at = pl.multiple_of(turn * 640 + part * 128, 128)
            column_ref[pl.ds(at, 128), 0:24] = columns
        for entry in range(16):
            for group in range(5):
                at = (entry * 5 + group) * 8
                for half in range(2):
                    slot = group * 2 + half
                    lanes = slice(half * 128, half * 128 + 128)
                    alpha = jnp.exp2(power_ref[at : at + 8, lanes])
                    weight = alpha * through[slot]
                    through[slot] = through[slot] - weight
                    alpha_ref[half, pl.ds(turn * 640 + at, 8), :] = alpha
                    weight_ref[half, pl.ds(turn * 640 + at, 8), :] = weight
        return tuple(through)

    lax.fori_loop(0, 8, forward, (jnp.ones((8, 128), F32),) * 10)
    moments = moment_ref[...]

    def backward(count, carry):
        turn = 7 - count
        behind = list(carry)
        for entry in range(15, -1, -1):
            for group in range(5):
                at = (entry * 5 + group) * 8
                columns = column_ref[pl.ds(turn * 640 + at, 8), :]
                colour = [
                    jnp.broadcast_to(columns[:, 18 + channel : 19 + channel], (8, 128))
                    for channel in range(3)
                ]
                for half in range(2):
                    slot = group * 2 + half
                    lanes = slice(half * 128, half * 128 + 128)
                    light = group * 6 + half * 3
                    value = (
                        colour[0] * light_ref[light]
                        + colour[1] * light_ref[light + 1]
                        + colour[2] * light_ref[light + 2]
                    )
                    delta = value - behind[slot]
                    alpha = alpha_ref[half, pl.ds(turn * 640 + at, 8), :]
                    behind[slot] = behind[slot] + alpha * delta
                    power_ref[at : at + 8, lanes] = (
                        weight_ref[half, pl.ds(turn * 640 + at, 8), :] * delta
                    )
        for part in range(5):
            pull = power_ref[part * 128 : part * 128 + 128, :]
            coarse = pull.astype(BF16)
            fine = (pull - coarse.astype(F32)).astype(BF16)
            total = dot_nt(moments, coarse) + dot_nt(moments, fine)
            sums_ref[pl.ds(pl.multiple_of((turn * 5 + part) * 8, 8), 8), :] = total[0:8]
        return tuple(behind)

    lax.fori_loop(0, 8, backward, (jnp.zeros((8, 128), F32),) * 10)

    def tints(tile, carry):
        at = pl.ds(pl.multiple_of(tile * 16, 16), 16)
        total = jnp.zeros((16, 128), F32)
        for half in range(2):
            weight = weight_ref[half, pl.ds(tile, 128, stride=ROWS), :]
            coarse = weight.astype(BF16)
            fine = (weight - coarse.astype(F32)).astype(BF16)
            light = split_ref[half, at, :].astype(BF16)
            total = total + dot_nt(light, coarse) + dot_nt(light, fine)
        tint_ref[at, :] = total
        return carry

    split_rows(split_ref)
    lax.fori_loop(0, ROWS, tints, 0)

    def entry_grads(block, carry):
        rows = pl.ds(block * 8, 8)
        zeroth, by_x, by_y, by_xx, by_xy, by_yy = [
            sums_ref[pl.ds(block * 64 + slot, 8, stride=8), :] for slot in range(6)
        ]
        x, y, a, b, c = [entries_ref[slot, rows, :] for slot in range(5)]
        off_x = by_x - x * zeroth
        off_y = by_y - y * zeroth
        feats_ref[0, rows, :] = a * off_x + b * off_y
        feats_ref[1, rows, :] = c * off_y + b * off_x
        feats_ref[2, rows, :] = -0.5 * (by_xx - x * (by_x + off_x))
        feats_ref[3, rows, :] = x * by_y + y * off_x - by_xy
        feats_ref[4, rows, :] = -0.5 * (by_yy - y * (by_y + off_y))
        feats_ref[8, rows, :] = zeroth
        for channel in range(3):
            feats_ref[5 + channel, rows, :] = (
                tint_ref[pl.ds(block * 128 + channel * 3, 8, stride=16), :]
                + tint_ref[pl.ds(block * 128 + channel * 3 + 1, 8, stride=16), :]
                + tint_ref[pl.ds(block * 128 + channel * 3 + 2, 8, stride=16), :]
            )
        return carry

    lax.fori_loop(0, 5, entry_grads, 0)

    def gather_block(block, carry):
        place = place_ref[pl.ds(block * 8, 8), :]
        tile = place >> 7
        entry = place & 127
        other = entry * ROWS + tile
        high = other >> 7
        low = other & 127
        got = [jnp.zeros((8, 128), F32)] * FEATS
        for row in range(ROWS):
            same = high == row
            match = tile == row
            for feature in range(FEATS):
                line = feats_ref[feature, row : row + 1, :]
                if 5 <= feature < 8:
                    got[feature] = jnp.where(match, pick(line, entry), got[feature])
                else:
                    got[feature] = jnp.where(same, pick(line, low), got[feature])
        for feature in range(FEATS):
            put_feature(table_ref, block, feature, got[feature])
        return carry

    lax.fori_loop(0, 5, gather_block, 0)
    expand_feats(table_ref, count_ref, out_ref, out_ref.shape[0])


def split_rows(split_ref):
    for row in range(9, 16):
        for half in range(2):
            split_ref[half, pl.ds(row, ROWS, stride=16), :] = jnp.zeros((ROWS, 128), F32)


def pull_kernel(focal, centre_x, centre_y):
    def kernel(camera_ref, count_ref, params_ref, place_ref, chunks_ref, out_ref, table_ref):
        strips = chunks_ref.shape[0]
        compact_feats(chunks_ref, count_ref, table_ref, strips)
        bounds = run_bounds(count_ref, strips)

        def block_grads(block, carry):
            rows = pl.ds(block * 8, 8)
            place = place_ref[rows, :]
            high = place >> 7
            low = place & 127
            got = [jnp.zeros((8, 128), F32)] * FEATS
            for row in range(ROWS):
                same = high == row
                for feature in range(FEATS):
                    value = pick(table_ref[row * 16 + feature : row * 16 + feature + 1, :], low)
                    got[feature] = jnp.where(same, value, got[feature])
            camera = select_camera(camera_ref, place, bounds)
            params = [params_ref[number, rows, :] for number in range(59)]
            ignored, pull = jax.vjp(
                lambda values: project(values, camera, focal, centre_x, centre_y), params
            )
            for number, grad in enumerate(pull(got[:8])[0]):
                if number == 10:
                    grad = got[8] / (1.0 + jnp.exp(params[10]))
                out_ref[number, rows, :] = grad
            return carry

        lax.fori_loop(0, 5, block_grads, 0)

    return kernel


def shape(*dims, dtype=F32):
    return jax.ShapeDtypeStruct(dims, dtype)


def per_device(params, camera, send_index, send_count, tile_list, target):
    strips = lax.axis_size("strip")
    index = lax.axis_index("strip")
    per_view = strips // VIEWS
    offset = per_view // 2
    position = (index + offset) % strips
    rows_strip = target.shape[1]
    width = target.shape[2]
    focal = 0.5 * width
    centre_y = 0.5 * rows_strip * per_view
    top = ((position % per_view) * rows_strip + rows_strip // 2).astype(F32).reshape(1)
    keep = jnp.stack([position % per_view != 0, position % per_view != per_view - 1]).astype(F32)
    ahead = [(i, (i + 1) % strips) for i in range(strips)]
    behind = [((i + 1) % strips, i) for i in range(strips)]
    blocks = params.reshape(59, ROWS, 128)

    chunks, place = pl.pallas_call(
        owner_kernel(focal, 0.5 * width, centre_y),
        out_shape=(shape(strips, 8, 128), shape(ROWS, 128, dtype=jnp.int32)),
        in_specs=[SMEM, SMEM, VMEM, VMEM],
        scratch_shapes=[
            pltpu.VMEM((strips, 128), jnp.int32),
            pltpu.VMEM((ROWS + 8, 128), jnp.int32),
            pltpu.VMEM((FEATS, ROWS, 128), F32),
            pltpu.VMEM(((ROWS + 2) * 16, 128), F32),
        ],
        name="owner",
    )(camera, send_count, blocks, send_index)
    arrived = lax.all_to_all(chunks, "strip", split_axis=0, concat_axis=0, tiled=True)
    counts = arrived[:, 2, 80].astype(jnp.int32)

    truth_above = lax.ppermute(target[:, 6:16, :], "strip", ahead)
    truth_below = lax.ppermute(target[:, 0:10, :], "strip", behind)
    truth, mean_y, power_y = pl.pallas_call(
        truth_kernel,
        out_shape=(shape(5, 128, 128), shape(640, 128), shape(640, 128)),
        in_specs=[SMEM, VMEM, VMEM, VMEM],
        scratch_shapes=[
            pltpu.VMEM((5, 128, 128), F32),
            pltpu.VMEM((128, 128), F32),
            pltpu.VMEM((2, 656, 128), F32),
        ],
        name="truth",
    )(keep, target, truth_above, truth_below)
    listed = pl.pallas_call(
        invert_kernel, out_shape=shape(ROWS, 128, dtype=jnp.int32), name="listed"
    )(tile_list)

    flat_list = tile_list.T.reshape(ROWS, 128)
    across = jnp.asarray(
        (np.arange(ROWS * 128) % ROWS * 16 + 8).astype(np.float32).reshape(ROWS, 128)
    )
    rows = entry_basis()
    basis = np.zeros((24, 256), np.float32)
    basis[0:18] = np.repeat(rows, 3, axis=0)
    moment = np.zeros((16, 256), np.float32)
    moment[0:6] = rows
    basis = jnp.asarray(basis, BF16)
    moment = jnp.asarray(moment, BF16)
    image, first, last, lines, entries = pl.pallas_call(
        render_kernel,
        out_shape=(
            shape(3, 5, 16, 128),
            shape(150, 128),
            shape(150, 128),
            shape(ROWS * 24, 128),
            shape(5, ROWS, 128),
        ),
        in_specs=[SMEM, SMEM, VMEM, VMEM, VMEM, VMEM],
        scratch_shapes=[
            pltpu.VMEM(((ROWS + 2) * 16, 128), F32),
            pltpu.VMEM((640, 256), F32),
            pltpu.VMEM((640, 128), F32),
        ],
        name="render",
    )(counts, top, arrived, flat_list, across, basis)
    above = lax.ppermute(last, "strip", ahead)
    below = lax.ppermute(first, "strip", behind)
    grads = pl.pallas_call(
        gradient_kernel,
        out_shape=shape(strips, 8, 128),
        in_specs=[SMEM, SMEM] + [VMEM] * 11,
        scratch_shapes=[
            pltpu.VMEM((5, 128, 128), F32),
            pltpu.VMEM((5, 128, 128), F32),
            pltpu.VMEM((5, 128, 128), F32),
            pltpu.VMEM((128, 128), F32),
            pltpu.VMEM((3, 656, 128), F32),
            pltpu.VMEM((3, 656, 128), F32),
            pltpu.VMEM((2, 5120, 128), F32),
            pltpu.VMEM((2, 5120, 128), F32),
            pltpu.VMEM((5120, 128), F32),
            pltpu.VMEM((640, 256), F32),
            pltpu.VMEM((30, 8, 128), F32),
            pltpu.VMEM((2, ROWS * 16, 128), F32),
            pltpu.VMEM((ROWS * 8, 128), F32),
            pltpu.VMEM((ROWS * 16, 128), F32),
            pltpu.VMEM((FEATS, ROWS, 128), F32),
            pltpu.VMEM(((ROWS + 2) * 16, 128), F32),
        ],
        name="gradient",
    )(
        counts, keep, image, above, below, truth, mean_y, power_y,
        lines, entries, listed, basis, moment,
    )
    returned = lax.all_to_all(grads, "strip", split_axis=0, concat_axis=0, tiled=True)
    result = pl.pallas_call(
        pull_kernel(focal, 0.5 * width, centre_y),
        out_shape=shape(59, ROWS, 128),
        in_specs=[SMEM, SMEM, VMEM, VMEM, VMEM],
        scratch_shapes=[pltpu.VMEM(((ROWS + 2) * 16, 128), F32)],
        name="pull",
    )(camera, send_count, blocks, place, returned)
    return result.reshape(59, ROWS * 128)


def solution(mesh):
    return jax.shard_map(
        per_device,
        mesh=mesh,
        in_specs=(
            P(None, "strip"),
            P(),
            P("strip", None),
            P("strip"),
            P("strip", None),
            P(None, "strip", None),
        ),
        out_specs=P(None, "strip"),
        check_vma=False,
    )
```

profile of v0, /device:TPU:1, one launch (start us, length us, event | category | flops | bytes accessed | tf_op | source)
XLA Modules:
  0.0 134.5 jit_solution(4020650893303634746)
XLA Ops:
  0.0 1.5 %copy.14 = f32[8,8,40,128]{3,2,1,0:T(8,128)S(1)} copy(f32[8,8,40,128]{3,1,2,0:T(8,128)} %bitcast.12) | data formatting | bytes 2621440
  1.6 0.0 copy-start.7
  1.6 1.1 slice.13.params_ref
  2.7 0.0 copy-done.7
  2.7 0.7 copy.12.index_ref
  3.4 12.5 %owner.1 = (f32[128,8,128]{2,1,0:T(8,128)}, s32[40,128]{1,0:T(8,128)}) custom-call(f32[4,12]{1,0:T(4,128)} %camera_ref.3, s32[128]{0:T(128)} %count_ref.3, f32[59,40,128]{2,1,0:T(8,128)} %slice.13.params_ref, s32[128,80]{1,0:T(8,128)} %copy.12.index_ref), custom_call_target="tpu_custom_call" | custom-call | tf_op jit(solution)/shard_map/owner/pallas_call | solution.py:822
  15.9 11.5 %all-to-all-start = ((f32[128,8,128]{2,1,0:T(8,128)}), f32[128,8,128]{2,1,0:T(8,128)S(1)}, u32[]{:S(2)}, u32[]{:S(2)}) async-start(f32[128,8,128]{2,1,0:T(8,128)} %get-tuple-element.16), calls=%async_computation | async-start | bytes 1048576 | tf_op jit(solution)/shard_map/all_to_all | solution.py:834
  27.5 1.8 %collective-permute-start.2 = (f32[3,10,640]{2,1,0:T(8,128)S(1)}, f32[3,10,640]{2,1,0:T(8,128)S(1)}, u32[]{:S(2)}, u32[]{:S(2)}) collective-permute-start(f32[3,10,640]{2,1,0:T(8,128)S(1)} %get-tuple-element.26), channel_id=1, source_target_pairs={{0,1},{1,2},{2,3},{3,4},{4,5},{5,6},{6,7},{7,8},{8,9},{9,10},{10,1... | collective-permute-start | bytes 230408 | tf_op jit(solution)/shard_map/ppermute | solution.py:837
  29.3 0.0 collective-permute-start.3
  29.3 1.9 %listed.1.place_ref = s32[40,128]{1,0:T(8,128)} custom-call(s32[40,128]{1,0:T(8,128)} %list_ref.1), custom_call_target="tpu_custom_call" | custom-call | tf_op jit(solution)/shard_map/listed/pallas_call | solution.py:850
  31.2 0.1 copy.13
  31.3 0.7 reshape.15.list_ref
  32.0 9.3 %all-to-all-done.chunks_ref = f32[128,8,128]{2,1,0:T(8,128)S(1)} async-done(((f32[128,8,128]{2,1,0:T(8,128)}), f32[128,8,128]{2,1,0:T(8,128)S(1)}, u32[]{:S(2)}, u32[]{:S(2)}) %all-to-all-start) | async-done | bytes 524320 | tf_op jit(solution)/shard_map/all_to_all | solution.py:834
  41.3 3.1 %fusion.count_ref = s32[128]{0:T(128)} fusion(f32[128,8,128]{2,1,0:T(8,128)S(1)} %all-to-all-done.chunks_ref), kind=kLoop, calls=%fused_computation.1 | loop fusion | flops 128 | bytes 1024 | tf_op jit(solution)/shard_map/convert_element_type | solution.py:835
  44.5 14.0 %render.1 = (f32[3,5,16,128]{3,2,1,0:T(8,128)}, f32[150,128]{1,0:T(8,128)}, f32[150,128]{1,0:T(8,128)}, f32[960,128]{1,0:T(8,128)}, f32[5,40,128]{2,1,0:T(8,128)}) custom-call(s32[128]{0:T(128)} %fusion.count_ref, f32[1]{0:T(128)} %bitcast.2.top_ref, f32[128,8,128]{2,1,0:T(8,128)} %copy-done, s32[40,128]{1,0:T(8,128)} %reshape.15.list_ref, ...), custom_call_target="tpu_custom_call" | custom-call | tf_op jit(solution)/shard_map/render/pallas_call | solution.py:865
  58.5 1.2 collective-permute-start
  59.7 0.0 collective-permute-start.1
  59.7 0.7 add_convert_fusion.keep_ref
  60.4 0.0 collective-permute-done.2.above_ref
  60.4 0.0 collective-permute-done.3.below_ref
  60.4 0.7 copy-done.2
  61.0 0.6 copy-done.3
  61.7 3.0 %truth.1 = (f32[5,128,128]{2,1,0:T(8,128)}, f32[640,128]{1,0:T(8,128)}, f32[640,128]{1,0:T(8,128)}) custom-call(f32[2]{0:T(128)} %add_convert_fusion.keep_ref, f32[3,16,640]{2,1,0:T(8,128)} %own_ref.1, f32[3,10,640]{2,1,0:T(8,128)} %copy-done.2, f32[3,10,640]{2,1,0:T(8,128)} %copy-done.3), custom_call_target="tpu_custom_call" | custom-call | tf_op jit(solution)/shard_map/truth/pallas_call | solution.py:839
  64.7 0.0 collective-permute-done.above_ref
  64.7 0.0 collective-permute-done.1.below_ref
  64.7 0.6 copy-done.5
  65.3 0.0 copy-done.6
  65.3 30.9 %gradient.1 = f32[128,8,128]{2,1,0:T(8,128)} custom-call(s32[128]{0:T(128)} %fusion.count_ref, f32[2]{0:T(128)} %add_convert_fusion.keep_ref, f32[3,5,16,128]{3,2,1,0:T(8,128)} %get-tuple-element.17.image_ref, f32[150,128]{1,0:T(8,128)} %copy-done.5, f32[150,128]{1,0:T(8,128)} %copy-done.6, f32[5,128,128]{2,1,0:T(8,128)} %get-tuple-element.20.truth_ref, ...), custom_call_target="tpu_custom_call" | custom-call | tf_op jit(solution)/shard_map/gradient/pallas_call | solution.py:884
  96.2 25.9 %all_to_all.10.chunks_ref = f32[128,8,128]{2,1,0:T(8,128)} all-to-all(f32[128,8,128]{2,1,0:T(8,128)} %gradient.1), channel_id=1, replica_groups=mesh['strip'=128] {'strip'}, dimensions={0} | all-to-all | bytes 1048576 | tf_op jit(solution)/shard_map/all_to_all | solution.py:911
  122.1 9.8 %pull.1 = f32[59,40,128]{2,1,0:T(8,128)} custom-call(f32[4,12]{1,0:T(4,128)} %camera_ref.3, s32[128]{0:T(128)} %count_ref.3, f32[59,40,128]{2,1,0:T(8,128)} %slice.13.params_ref, s32[40,128]{1,0:T(8,128)} %get-tuple-element.15.place_ref, f32[128,8,128]{2,1,0:T(8,128)} %all_to_all.10.chunks_ref), custom_call_target="tpu_custom_call" | custom-call | tf_op jit(solution)/shard_map/pull/pallas_call | solution.py:912
  131.9 1.4 %pad.2 = f32[64,40,128]{2,1,0:T(8,128)S(1)} pad(f32[59,40,128]{2,1,0:T(8,128)} %pull.1, f32[]{:T(128)} %constant.50), padding=0_5x0_0x0_0 | pad | bytes 2519044
  133.2 1.3 copy.15
  (11 shorter events, 0.0 us)
Async XLA Ops:
  1.6 1.1 copy-start.7
  2.7 24.8 %copy-start.1 = (f32[3,16,640]{2,1,0:T(8,128)S(1)}, f32[3,16,640]{2,1,0:T(8,128)}, u32[]{:S(2)}) copy-start(f32[3,16,640]{2,1,0:T(8,128)} %own_ref.1) | copy-start | bytes 368644
  3.4 27.8 %copy-start.4 = (s32[40,128]{1,0:T(8,128)S(1)}, s32[40,128]{1,0:T(8,128)}, u32[]{:S(2)}) copy-start(s32[40,128]{1,0:T(8,128)} %list_ref.1) | copy-start | bytes 61444
  15.9 25.4 %all-to-all-start = ((f32[128,8,128]{2,1,0:T(8,128)}), f32[128,8,128]{2,1,0:T(8,128)S(1)}, u32[]{:S(2)}, u32[]{:S(2)}) async-start(f32[128,8,128]{2,1,0:T(8,128)} %get-tuple-element.16), calls=%async_computation | async-start | bytes 1048576 | tf_op jit(solution)/shard_map/all_to_all | solution.py:834
  27.5 32.9 %collective-permute-start.2 = (f32[3,10,640]{2,1,0:T(8,128)S(1)}, f32[3,10,640]{2,1,0:T(8,128)S(1)}, u32[]{:S(2)}, u32[]{:S(2)}) collective-permute-start(f32[3,10,640]{2,1,0:T(8,128)S(1)} %get-tuple-element.26), channel_id=1, source_target_pairs={{0,1},{1,2},{2,3},{3,4},{4,5},{5,6},{6,7},{7,8},{8,9},{9,10},{10,1... | collective-permute-start | bytes 230408 | tf_op jit(solution)/shard_map/ppermute | solution.py:837
  29.3 31.1 %collective-permute-start.3 = (f32[3,10,640]{2,1,0:T(8,128)S(1)}, f32[3,10,640]{2,1,0:T(8,128)S(1)}, u32[]{:S(2)}, u32[]{:S(2)}) collective-permute-start(f32[3,10,640]{2,1,0:T(8,128)S(1)} %get-tuple-element.25), channel_id=1, source_target_pairs={{1,0},{2,1},{3,2},{4,3},{5,4},{6,5},{7,6},{8,7},{9,8},{10,9},{11,1... | collective-permute-start | bytes 230408 | tf_op jit(solution)/shard_map/ppermute | solution.py:838
  41.3 3.1 %copy-start = (f32[128,8,128]{2,1,0:T(8,128)}, f32[128,8,128]{2,1,0:T(8,128)S(1)}, u32[]{:S(2)}) copy-start(f32[128,8,128]{2,1,0:T(8,128)S(1)} %all-to-all-done.chunks_ref) | copy-start | bytes 1572868
  58.5 6.1 %collective-permute-start = (f32[150,128]{1,0:T(8,128)}, f32[150,128]{1,0:T(8,128)S(1)}, u32[]{:S(2)}, u32[]{:S(2)}) collective-permute-start(f32[150,128]{1,0:T(8,128)} %get-tuple-element.18), channel_id=1, source_target_pairs={{0,1},{1,2},{2,3},{3,4},{4,5},{5,6},{6,7},{7,8},{8,9},{9,10},{10,1... | collective-permute-start | bytes 230408 | tf_op jit(solution)/shard_map/ppermute | solution.py:882
  59.7 4.9 %collective-permute-start.1 = (f32[150,128]{1,0:T(8,128)}, f32[150,128]{1,0:T(8,128)S(1)}, u32[]{:S(2)}, u32[]{:S(2)}) collective-permute-start(f32[150,128]{1,0:T(8,128)} %get-tuple-element.19), channel_id=1, source_target_pairs={{1,0},{2,1},{3,2},{4,3},{5,4},{6,5},{7,6},{8,7},{9,8},{10,9},{11,1... | collective-permute-start | bytes 230408 | tf_op jit(solution)/shard_map/ppermute | solution.py:883
  60.4 0.7 copy-start.2
  61.0 0.6 copy-start.3
  64.7 0.6 copy-start.5
  64.7 0.7 copy-start.6
where the time goes:
time: 135 us
  Pallas kernels  72.1 us (53%)
  blocking collectives  25.9 us (19%)
  starting transfers between devices  14.5 us (11%)
  waiting for transfers between devices  9.32 us (7%)
  local copies, waits for them, and re-layouts  8.8 us (7%)
  other arithmetic  3.79 us (3%)
    pallas_call x1, Pallas kernels, per_device(): pl.pallas_call(gradient_kernel, out_shape=shape(strips, 8, 128), in_specs...  30.9 us
    all_to_all x1, blocking collectives, per_device(): lax.all_to_all(grads, 'strip', split_axis=0, concat_axis=0, tiled=True)  25.9 us
    pallas_call x1, Pallas kernels, per_device(): pl.pallas_call(render_kernel, out_shape=(shape(3, 5, 16, 128), shape(150,...  14 us
    pallas_call x1, Pallas kernels, per_device(): pl.pallas_call(owner_kernel(focal, 0.5 * width, centre_y), out_shape=(sha...  12.5 us
    all_to_all x1, starting transfers between devices, per_device(): lax.all_to_all(chunks, 'strip', split_axis=0, concat_axis=0, tiled=True)  11.5 us
    pallas_call x1, Pallas kernels, per_device(): pl.pallas_call(pull_kernel(focal, 0.5 * width, centre_y), out_shape=shape...  9.79 us
    all_to_all x1, waiting for transfers between devices, per_device(): lax.all_to_all(chunks, 'strip', split_axis=0, concat_axis=0, tiled=True)  9.31 us
    unnamed x20, local copies, waits for them, and re-layouts  6.88 us
  transfers between devices with their start and end apart: 5, of which 1 were waited for; matrix products, arithmetic and copies ran while one was open for 3% of the time, Pallas kernels for 14%

commit v1 on v0

--- a/solution.py
+++ b/solution.py
@@ -35,6 +35,7 @@
 BF16 = jnp.bfloat16
 SMEM = pl.BlockSpec(memory_space=pltpu.SMEM)
 VMEM = pl.BlockSpec(memory_space=pltpu.VMEM)
+ANY = pl.BlockSpec(memory_space=pl.ANY)
 
 
 def iota(shape, axis):
@@ -213,36 +214,41 @@
         held = jnp.where(shift + live >= 128, chunk, held)
         return start + live, held
 
-    lax.fori_loop(0, steps, step, (jnp.int32(0), jnp.zeros((1, 128), jnp.int32)), unroll=4)
-
-
-def compact_feats(chunk_ref, count_ref, table_ref, steps):
+    lax.fori_loop(0, steps, step, (jnp.int32(0), jnp.zeros((1, 128), jnp.int32)), unroll=16)
+
+
+def compact_feats(chunk_ref, count_of, table_ref, steps):
     lane = iota((8, 128), 1)
 
     def step(number, carry):
         start, held, last = carry
-        live = count_ref[number]
+        if isinstance(number, int) and number == steps - 1:
+            chunk = pltpu.roll(chunk_ref[number * 6 - 2 : number * 6 + 6, :], 6, axis=0)
+        else:
+            chunk = chunk_ref[pl.ds(number * 6, 8), :]
+        live = count_of(number, chunk)
         shift = start & 127
         row = start >> 7
-        chunk = chunk_ref[number]
         first = pltpu.roll(chunk, 48, axis=1)
         second = pltpu.roll(pltpu.roll(chunk, 96, axis=1), 7, axis=0)
-        ninth = jnp.where(lane < 48, first, second)
+        rest = jnp.where(lane < 48, first, second)
         chunk = pltpu.roll(chunk, shift, axis=1)
-        ninth = pltpu.roll(ninth, shift, axis=1)
+        rest = pltpu.roll(rest, shift, axis=1)
         fresh = lane >= shift
         held = jnp.where(fresh, chunk, held)
-        last = jnp.where(fresh, ninth, last)
+        last = jnp.where(fresh, rest, last)
         base = pl.multiple_of(row * 16, 16)
         table_ref[pl.ds(base, 8), :] = held
         table_ref[pl.ds(base + 8, 8), :] = last
         crossed = shift + live >= 128
         held = jnp.where(crossed, chunk, held)
-        last = jnp.where(crossed, ninth, last)
+        last = jnp.where(crossed, rest, last)
         return start + live, held, last
 
     zero = jnp.zeros((8, 128), F32)
-    lax.fori_loop(0, steps, step, (jnp.int32(0), zero, zero), unroll=4)
+    carry = lax.fori_loop(0, steps - 16, step, (jnp.int32(0), zero, zero), unroll=16)
+    for number in range(steps - 16, steps):
+        carry = step(number, carry)
 
 
 def expand_feats(table_ref, count_ref, out_ref, steps):
@@ -260,23 +266,49 @@
             pltpu.roll(table_ref[pl.ds(base, 8), :], back, axis=1),
             pltpu.roll(table_ref[pl.ds(base + 16, 8), :], back, axis=1),
         )
-        ninth = jnp.where(
+        rest = jnp.where(
             here,
             pltpu.roll(table_ref[pl.ds(base + 8, 8), :], back, axis=1),
             pltpu.roll(table_ref[pl.ds(base + 24, 8), :], back, axis=1),
         )
-        tail = jnp.where(sub == 0, pltpu.roll(ninth, 80, axis=1), pltpu.roll(ninth, 32, axis=1))
-        tail = jnp.where(sub < 2, tail, live.astype(F32))
-        out_ref[number] = jnp.where(lane < 80, main, tail)
+        tail = jnp.where(
+            (sub & 1) == 0, pltpu.roll(rest, 80, axis=1), pltpu.roll(rest, 32, axis=1)
+        )
+        tail = jnp.where((sub == 1) & (lane == 127), live.astype(F32), tail)
+        out_ref[pl.ds(number * 6, 6), :] = jnp.where(lane < 80, main, tail)[0:6]
         return start + live
 
-    lax.fori_loop(0, steps, step, jnp.int32(0), unroll=4)
+    lax.fori_loop(0, steps, step, jnp.int32(0), unroll=16)
+
+
+def line_of(feature):
+    return feature if feature < 6 else 8 + 2 * (feature - 6)
 
 
 def put_feature(table_ref, block, feature, value):
-    table_ref[pl.ds(block * 128 + feature, 8, stride=16), :] = value
-    if feature == 8:
-        table_ref[pl.ds(block * 128 + 9, 8, stride=16), :] = value
+    line = line_of(feature)
+    table_ref[pl.ds(block * 128 + line, 8, stride=16), :] = value
+    if feature >= 6:
+        table_ref[pl.ds(block * 128 + line + 1, 8, stride=16), :] = value
+
+
+def table_line(table_ref, row, feature):
+    line = row * 16 + line_of(feature)
+    return table_ref[line : line + 1, :]
+
+
+def fetch_params(params_ref, local_ref, sems):
+    copies = [
+        pltpu.make_async_copy(
+            params_ref.at[:, pl.ds(tile * 128, 128)],
+            local_ref.at[pl.ds(tile * 64, 59), :],
+            sems.at[tile],
+        )
+        for tile in range(ROWS)
+    ]
+    for copy in copies:
+        copy.start()
+    return copies
 
 
 def invert(rows_ref, out_ref):
@@ -325,18 +357,25 @@
 def owner_kernel(focal, centre_x, centre_y):
     def kernel(
         camera_ref, count_ref, params_ref, index_ref, out_ref, place_ref,
-        wide_ref, rows_ref, feats_ref, table_ref,
+        wide_ref, rows_ref, feats_ref, table_ref, local_ref, sems,
     ):
-        strips = index_ref.shape[0]
-        wide_ref[:, 0:80] = index_ref[...]
+        copies = fetch_params(params_ref, local_ref, sems)
+        strips = index_ref.shape[1]
+        wide_ref[...] = jnp.concatenate(
+            [index_ref[...], jnp.zeros((128 - index_ref.shape[0], strips), jnp.int32)], 0
+        ).T
         compact_ints(wide_ref, count_ref, rows_ref, strips)
         invert(rows_ref, place_ref)
         bounds = run_bounds(count_ref, strips)
+        for copy in copies:
+            copy.wait()
 
         def project_block(block, carry):
             rows = pl.ds(block * 8, 8)
             camera = select_camera(camera_ref, place_ref[rows, :], bounds)
-            params = [params_ref[number, rows, :] for number in range(59)]
+            params = [
+                local_ref[pl.ds(block * 512 + number, 8, stride=64), :] for number in range(59)
+            ]
             feats = project(params, camera, focal, centre_x, centre_y)
             feats.append(log_sigmoid(params[10]))
             for feature in range(FEATS):
@@ -384,18 +423,24 @@
     return x
 
 
-def expand_block(lines_ref, row, basis):
-    lines = lines_ref[pl.ds(pl.multiple_of(row * 24, 8), 24), :]
-    columns = lines.T
-    return columns, jnp.dot(columns.astype(BF16), basis, preferred_element_type=F32)
+def coarse_fine(x):
+    coarse = x.astype(BF16)
+    return coarse, (x - coarse.astype(F32)).astype(BF16)
 
 
 def render_kernel(
-    count_ref, top_ref, chunks_ref, list_ref, across_ref, basis_ref,
-    image_ref, first_ref, last_ref, lines_ref, entries_ref,
-    table_ref, power_ref, column_ref,
+    top_ref, chunks_ref, list_ref, tiles_ref, across_ref, basis_ref,
+    image_ref, first_ref, last_ref, entries_ref, colour_ref, count_ref, alphas_ref, weights_ref,
+    table_ref, lines_ref, power_a, power_b, alpha_ref, weight_ref, tint_ref, shown_ref, sems,
 ):
-    compact_feats(chunks_ref, count_ref, table_ref, chunks_ref.shape[0])
+    strips = chunks_ref.shape[0] // 6
+
+    def count_of(number, chunk):
+        live = chunk[1, 127].astype(jnp.int32)
+        count_ref[number] = live
+        return live
+
+    compact_feats(chunks_ref, count_of, table_ref, strips)
     top = top_ref[0]
 
     def entry_block(block, carry):
@@ -403,12 +448,19 @@
         number = list_ref[rows, :]
         high = number >> 7
         low = number & 127
+        other = tiles_ref[rows, :]
+        other_high = other >> 7
+        other_low = other & 127
         got = [jnp.zeros((8, 128), F32)] * FEATS
         for row in range(ROWS):
             same = high == row
+            match = other_high == row
             for feature in range(FEATS):
-                value = pick(table_ref[row * 16 + feature : row * 16 + feature + 1, :], low)
-                got[feature] = jnp.where(same, value, got[feature])
+                line = table_line(table_ref, row, feature)
+                if 5 <= feature < 8:
+                    got[feature] = jnp.where(match, pick(line, other_low), got[feature])
+                else:
+                    got[feature] = jnp.where(same, pick(line, low), got[feature])
         x = got[0] - across_ref[rows, :]
         y = got[1] - top
         a, b, c = got[2:5]
@@ -428,52 +480,95 @@
                 piece = rounded(term)
                 lines_ref[pl.ds(block * 192 + slot * 3 + part, 8, stride=24), :] = piece
                 term = term - piece
+        for slot in range(18, 24):
+            lines_ref[pl.ds(block * 192 + slot, 8, stride=24), :] = jnp.zeros((8, 128), F32)
         for channel in range(3):
-            lines_ref[pl.ds(block * 192 + 18 + channel, 8, stride=24), :] = got[5 + channel]
-            lines_ref[pl.ds(block * 192 + 21 + channel, 8, stride=24), :] = jnp.zeros((8, 128), F32)
+            value = got[5 + channel]
+            colour_ref[channel, rows, :] = value
+            for part in range(3):
+                piece = rounded(value)
+                tint_ref[pl.ds(block * 128 + channel * 3 + part, 8, stride=16), :] = piece
+                value = value - piece
         return carry
 
     lax.fori_loop(0, 5, entry_block, 0)
     basis = basis_ref[...]
 
-    def blend(turn, carry):
-        through = list(carry[0:10])
-        shown = list(carry[10:40])
+    def powers(turn, power_ref):
         for part in range(5):
-            columns, power = expand_block(lines_ref, turn * 5 + part, basis)
-            power_ref[part * 128 : part * 128 + 128, :] = power
-            column_ref[part * 128 : part * 128 + 128, 0:24] = columns
+            lines = lines_ref[pl.ds(pl.multiple_of((turn * 5 + part) * 24, 8), 24), :]
+            power_ref[part * 128 : part * 128 + 128, :] = jnp.dot(
+                lines.T.astype(BF16), basis, preferred_element_type=F32
+            )
+
+    def copies(turn):
+        rows = pl.ds(turn * 640, 640)
+        found = []
+        for half in range(2):
+            for slot, (near, far) in enumerate(((alpha_ref, alphas_ref), (weight_ref, weights_ref))):
+                found.append(
+                    pltpu.make_async_copy(
+                        near.at[half, rows, :],
+                        far.at[half, rows, :],
+                        sems.at[turn * 4 + slot * 2 + half],
+                    )
+                )
+        return found
+
+    def scan(turn, power_ref, through):
+        through = list(through)
         for entry in range(16):
             for group in range(5):
                 at = (entry * 5 + group) * 8
-                columns = column_ref[at : at + 8, :]
-                colour = [
-                    jnp.broadcast_to(columns[:, 18 + channel : 19 + channel], (8, 128))
-                    for channel in range(3)
-                ]
                 for half in range(2):
                     slot = group * 2 + half
                     alpha = jnp.exp2(power_ref[at : at + 8, half * 128 : half * 128 + 128])
                     weight = alpha * through[slot]
                     through[slot] = through[slot] - weight
-                    for channel in range(3):
-                        shown[slot * 3 + channel] = (
-                            shown[slot * 3 + channel] + weight * colour[channel]
-                        )
-        return tuple(through + shown)
-
-    one = jnp.ones((8, 128), F32)
-    zero = jnp.zeros((8, 128), F32)
-    final = lax.fori_loop(0, 8, blend, (one,) * 10 + (zero,) * 30)
+                    alpha_ref[half, pl.ds(turn * 640 + at, 8), :] = alpha
+                    weight_ref[half, pl.ds(turn * 640 + at, 8), :] = weight
+        return tuple(through)
+
+    def blend(pair, through):
+        powers(2 * pair + 1, power_b)
+        through = scan(2 * pair, power_a, through)
+        powers(jnp.minimum(2 * pair + 2, 7), power_a)
+        through = scan(2 * pair + 1, power_b, through)
+        for turn in (2 * pair, 2 * pair + 1):
+            for copy in copies(turn):
+                copy.start()
+        return through
+
+    powers(0, power_a)
+    lax.fori_loop(0, 4, blend, (jnp.ones((8, 128), F32),) * 10)
+
+    def tints(tile, carry):
+        tint = tint_ref[pl.ds(pl.multiple_of(tile * 16, 16), 16), :].astype(BF16)
+        for half in range(2):
+            coarse, fine = coarse_fine(weight_ref[half, pl.ds(tile, 128, stride=ROWS), :])
+            total = jnp.dot(tint, coarse, preferred_element_type=F32) + jnp.dot(
+                tint, fine, preferred_element_type=F32
+            )
+            shown_ref[half, pl.ds(pl.multiple_of(tile * 16, 16), 16), :] = total
+        return carry
+
+    lax.fori_loop(0, ROWS, tints, 0, unroll=4)
     for group in range(5):
         for channel in range(3):
             for half in range(2):
+                parts = [
+                    shown_ref[half, pl.ds(group * 128 + channel * 3 + part, 8, stride=16), :]
+                    for part in range(3)
+                ]
                 image_ref[channel, group, half * 8 : half * 8 + 8, :] = swap_tiles(
-                    final[10 + (group * 2 + half) * 3 + channel]
+                    parts[0] + parts[1] + parts[2]
                 )
             at = (channel * 5 + group) * 10
             first_ref[at : at + 10, :] = image_ref[channel, group, 0:10, :]
             last_ref[at : at + 10, :] = image_ref[channel, group, 6:16, :]
+    for turn in range(8):
+        for copy in copies(turn):
+            copy.wait()
 
 
 def window_weights():
@@ -555,12 +650,19 @@
 
 def gradient_kernel(
     count_ref, keep_ref, image_ref, above_ref, below_ref, truth_ref, mean_y_ref, power_y_ref,
-    lines_ref, entries_ref, place_ref, basis_ref, moment_ref,
+    entries_ref, colour_ref, place_ref, moment_ref, alphas_ref, weights_ref,
     out_ref,
     ext_ref, square_ref, cross_ref, rows_ref, cols_ref, parts_ref,
-    alpha_ref, weight_ref, column_ref, power_ref, light_ref, split_ref,
-    sums_ref, tint_ref, feats_ref, table_ref,
+    alpha_ref, weight_ref, pull_a, pull_b, light_ref, split_ref,
+    sums_ref, tint_ref, feats_ref, table_ref, sems,
 ):
+    copies = [
+        pltpu.make_async_copy(far.at[half], near.at[half], sems.at[slot * 2 + half])
+        for slot, (far, near) in enumerate(((alphas_ref, alpha_ref), (weights_ref, weight_ref)))
+        for half in range(2)
+    ]
+    for copy in copies:
+        copy.start()
     keep_above = keep_ref[0]
     keep_below = keep_ref[1]
     extend(
@@ -635,45 +737,31 @@
                     piece = rounded(value)
                     split_ref[half, pl.ds(tile * 128 + channel * 3 + part, 8, stride=16), :] = piece
                     value = value - piece
-    basis = basis_ref[...]
-
-    def forward(turn, carry):
-        through = list(carry)
-        for part in range(5):
-            columns, power = expand_block(lines_ref, turn * 5 + part, basis)
-            power_ref[part * 128 : part * 128 + 128, :] = power
-            at = pl.multiple_of(turn * 640 + part * 128, 128)
-            column_ref[pl.ds(at, 128), 0:24] = columns
-        for entry in range(16):
-            for group in range(5):
-                at = (entry * 5 + group) * 8
-                for half in range(2):
-                    slot = group * 2 + half
-                    lanes = slice(half * 128, half * 128 + 128)
-                    alpha = jnp.exp2(power_ref[at : at + 8, lanes])
-                    weight = alpha * through[slot]
-                    through[slot] = through[slot] - weight
-                    alpha_ref[half, pl.ds(turn * 640 + at, 8), :] = alpha
-                    weight_ref[half, pl.ds(turn * 640 + at, 8), :] = weight
-        return tuple(through)
-
-    lax.fori_loop(0, 8, forward, (jnp.ones((8, 128), F32),) * 10)
+    for copy in copies:
+        copy.wait()
     moments = moment_ref[...]
 
-    def backward(count, carry):
-        turn = 7 - count
-        behind = list(carry)
+    def scan(turn, pull_ref, behind):
+        behind = list(behind)
+        turned = [
+            [
+                pltpu.roll(
+                    colour_ref[channel, group * 8 : group * 8 + 8, :], 128 - turn * 16 & 127, axis=1
+                )
+                for channel in range(3)
+            ]
+            for group in range(5)
+        ]
         for entry in range(15, -1, -1):
             for group in range(5):
                 at = (entry * 5 + group) * 8
-                columns = column_ref[pl.ds(turn * 640 + at, 8), :]
+                rows = pl.ds(turn * 640 + at, 8)
                 colour = [
-                    jnp.broadcast_to(columns[:, 18 + channel : 19 + channel], (8, 128))
+                    jnp.broadcast_to(turned[group][channel][:, entry : entry + 1], (8, 128))
                     for channel in range(3)
                 ]
                 for half in range(2):
                     slot = group * 2 + half
-                    lanes = slice(half * 128, half * 128 + 128)
                     light = group * 6 + half * 3
                     value = (
                         colour[0] * light_ref[light]
@@ -681,35 +769,40 @@
                         + colour[2] * light_ref[light + 2]
                     )
                     delta = value - behind[slot]
-                    alpha = alpha_ref[half, pl.ds(turn * 640 + at, 8), :]
-                    behind[slot] = behind[slot] + alpha * delta
-                    power_ref[at : at + 8, lanes] = (
-                        weight_ref[half, pl.ds(turn * 640 + at, 8), :] * delta
+                    behind[slot] = behind[slot] + alpha_ref[half, rows, :] * delta
+                    pull_ref[at : at + 8, half * 128 : half * 128 + 128] = (
+                        weight_ref[half, rows, :] * delta
                     )
+        return tuple(behind)
+
+    def reduce(turn, pull_ref):
         for part in range(5):
-            pull = power_ref[part * 128 : part * 128 + 128, :]
-            coarse = pull.astype(BF16)
-            fine = (pull - coarse.astype(F32)).astype(BF16)
+            coarse, fine = coarse_fine(pull_ref[part * 128 : part * 128 + 128, :])
             total = dot_nt(moments, coarse) + dot_nt(moments, fine)
             sums_ref[pl.ds(pl.multiple_of((turn * 5 + part) * 8, 8), 8), :] = total[0:8]
-        return tuple(behind)
-
-    lax.fori_loop(0, 8, backward, (jnp.zeros((8, 128), F32),) * 10)
+
+    def backward(count, behind):
+        turn = 7 - 2 * count
+        reduce(turn + 1, pull_b)
+        behind = scan(turn, pull_a, behind)
+        reduce(turn, pull_a)
+        return scan(turn - 1, pull_b, behind)
+
+    pull_b[...] = jnp.zeros((640, 256), F32)
+    lax.fori_loop(0, 4, backward, (jnp.zeros((8, 128), F32),) * 10)
+    reduce(0, pull_b)
 
     def tints(tile, carry):
         at = pl.ds(pl.multiple_of(tile * 16, 16), 16)
         total = jnp.zeros((16, 128), F32)
         for half in range(2):
-            weight = weight_ref[half, pl.ds(tile, 128, stride=ROWS), :]
-            coarse = weight.astype(BF16)
-            fine = (weight - coarse.astype(F32)).astype(BF16)
+            coarse, fine = coarse_fine(weight_ref[half, pl.ds(tile, 128, stride=ROWS), :])
             light = split_ref[half, at, :].astype(BF16)
             total = total + dot_nt(light, coarse) + dot_nt(light, fine)
         tint_ref[at, :] = total
         return carry
 
-    split_rows(split_ref)
-    lax.fori_loop(0, ROWS, tints, 0)
+    lax.fori_loop(0, ROWS, tints, 0, unroll=4)
 
     def entry_grads(block, carry):
         rows = pl.ds(block * 8, 8)
@@ -757,19 +850,17 @@
         return carry
 
     lax.fori_loop(0, 5, gather_block, 0)
-    expand_feats(table_ref, count_ref, out_ref, out_ref.shape[0])
-
-
-def split_rows(split_ref):
-    for row in range(9, 16):
-        for half in range(2):
-            split_ref[half, pl.ds(row, ROWS, stride=16), :] = jnp.zeros((ROWS, 128), F32)
+    expand_feats(table_ref, count_ref, out_ref, out_ref.shape[0] // 6)
 
 
 def pull_kernel(focal, centre_x, centre_y):
-    def kernel(camera_ref, count_ref, params_ref, place_ref, chunks_ref, out_ref, table_ref):
-        strips = chunks_ref.shape[0]
-        compact_feats(chunks_ref, count_ref, table_ref, strips)
+    def kernel(
+        camera_ref, count_ref, params_ref, place_ref, chunks_ref, out_ref,
+        table_ref, local_ref, grads_ref, sems, out_sems,
+    ):
+        copies = fetch_params(params_ref, local_ref, sems)
+        strips = chunks_ref.shape[0] // 6
+        compact_feats(chunks_ref, lambda number, chunk: count_ref[number], table_ref, strips)
         bounds = run_bounds(count_ref, strips)
 
         def block_grads(block, carry):
@@ -781,26 +872,47 @@
             for row in range(ROWS):
                 same = high == row
                 for feature in range(FEATS):
-                    value = pick(table_ref[row * 16 + feature : row * 16 + feature + 1, :], low)
+                    value = pick(table_line(table_ref, row, feature), low)
                     got[feature] = jnp.where(same, value, got[feature])
             camera = select_camera(camera_ref, place, bounds)
-            params = [params_ref[number, rows, :] for number in range(59)]
+            params = [
+                local_ref[pl.ds(block * 512 + number, 8, stride=64), :] for number in range(59)
+            ]
             ignored, pull = jax.vjp(
                 lambda values: project(values, camera, focal, centre_x, centre_y), params
             )
             for number, grad in enumerate(pull(got[:8])[0]):
                 if number == 10:
                     grad = got[8] / (1.0 + jnp.exp(params[10]))
-                out_ref[number, rows, :] = grad
+                grads_ref[pl.ds(block * 512 + number, 8, stride=64), :] = grad
+            for tile in range(8):
+                result(block * 8 + tile).start()
             return carry
 
+        def result(tile):
+            return pltpu.make_async_copy(
+                grads_ref.at[pl.ds(pl.multiple_of(tile * 64, 64), 59), :],
+                out_ref.at[:, pl.ds(pl.multiple_of(tile * 128, 128), 128)],
+                out_sems.at[tile],
+            )
+
+        for copy in copies:
+            copy.wait()
         lax.fori_loop(0, 5, block_grads, 0)
+        for tile in range(ROWS):
+            result(tile).wait()
 
     return kernel
 
 
 def shape(*dims, dtype=F32):
     return jax.ShapeDtypeStruct(dims, dtype)
+
+
+def exchange(chunks, strips):
+    sent = chunks.reshape(strips, 1, 768)
+    got = lax.all_to_all(sent, "strip", split_axis=0, concat_axis=0, tiled=True)
+    return got.reshape(strips * 6, 128)
 
 
 def per_device(params, camera, send_index, send_count, tile_list, target):
@@ -817,22 +929,22 @@
     keep = jnp.stack([position % per_view != 0, position % per_view != per_view - 1]).astype(F32)
     ahead = [(i, (i + 1) % strips) for i in range(strips)]
     behind = [((i + 1) % strips, i) for i in range(strips)]
-    blocks = params.reshape(59, ROWS, 128)
 
     chunks, place = pl.pallas_call(
         owner_kernel(focal, 0.5 * width, centre_y),
-        out_shape=(shape(strips, 8, 128), shape(ROWS, 128, dtype=jnp.int32)),
-        in_specs=[SMEM, SMEM, VMEM, VMEM],
+        out_shape=(shape(strips * 6, 128), shape(ROWS, 128, dtype=jnp.int32)),
+        in_specs=[SMEM, SMEM, ANY, VMEM],
         scratch_shapes=[
             pltpu.VMEM((strips, 128), jnp.int32),
             pltpu.VMEM((ROWS + 8, 128), jnp.int32),
             pltpu.VMEM((FEATS, ROWS, 128), F32),
             pltpu.VMEM(((ROWS + 2) * 16, 128), F32),
+            pltpu.VMEM((ROWS * 64, 128), F32),
+            pltpu.SemaphoreType.DMA((ROWS,)),
         ],
         name="owner",
-    )(camera, send_count, blocks, send_index)
-    arrived = lax.all_to_all(chunks, "strip", split_axis=0, concat_axis=0, tiled=True)
-    counts = arrived[:, 2, 80].astype(jnp.int32)
+    )(camera, send_count, params, send_index.T)
+    arrived = exchange(chunks, strips)
 
     truth_above = lax.ppermute(target[:, 6:16, :], "strip", ahead)
     truth_below = lax.ppermute(target[:, 0:10, :], "strip", behind)
@@ -862,29 +974,39 @@
     moment[0:6] = rows
     basis = jnp.asarray(basis, BF16)
     moment = jnp.asarray(moment, BF16)
-    image, first, last, lines, entries = pl.pallas_call(
+    image, first, last, entries, colour, counts, alphas, weights = pl.pallas_call(
         render_kernel,
         out_shape=(
             shape(3, 5, 16, 128),
             shape(150, 128),
             shape(150, 128),
-            shape(ROWS * 24, 128),
             shape(5, ROWS, 128),
+            shape(3, ROWS, 128),
+            shape(strips, dtype=jnp.int32),
+            shape(2, 5120, 128),
+            shape(2, 5120, 128),
         ),
-        in_specs=[SMEM, SMEM, VMEM, VMEM, VMEM, VMEM],
+        in_specs=[SMEM, VMEM, VMEM, VMEM, VMEM, VMEM],
+        out_specs=(VMEM, VMEM, VMEM, VMEM, VMEM, SMEM, ANY, ANY),
         scratch_shapes=[
             pltpu.VMEM(((ROWS + 2) * 16, 128), F32),
+            pltpu.VMEM((ROWS * 24, 128), F32),
             pltpu.VMEM((640, 256), F32),
-            pltpu.VMEM((640, 128), F32),
+            pltpu.VMEM((640, 256), F32),
+            pltpu.VMEM((2, 5120, 128), F32),
+            pltpu.VMEM((2, 5120, 128), F32),
+            pltpu.VMEM((ROWS * 16, 128), F32),
+            pltpu.VMEM((2, ROWS * 16, 128), F32),
+            pltpu.SemaphoreType.DMA((32,)),
         ],
         name="render",
-    )(counts, top, arrived, flat_list, across, basis)
+    )(top, arrived, flat_list, tile_list, across, basis)
     above = lax.ppermute(last, "strip", ahead)
     below = lax.ppermute(first, "strip", behind)
     grads = pl.pallas_call(
         gradient_kernel,
-        out_shape=shape(strips, 8, 128),
-        in_specs=[SMEM, SMEM] + [VMEM] * 11,
+        out_shape=shape(strips * 6, 128),
+        in_specs=[SMEM, SMEM] + [VMEM] * 10 + [ANY, ANY],
         scratch_shapes=[
             pltpu.VMEM((5, 128, 128), F32),
             pltpu.VMEM((5, 128, 128), F32),
@@ -894,29 +1016,36 @@
             pltpu.VMEM((3, 656, 128), F32),
             pltpu.VMEM((2, 5120, 128), F32),
             pltpu.VMEM((2, 5120, 128), F32),
-            pltpu.VMEM((5120, 128), F32),
+            pltpu.VMEM((640, 256), F32),
             pltpu.VMEM((640, 256), F32),
             pltpu.VMEM((30, 8, 128), F32),
             pltpu.VMEM((2, ROWS * 16, 128), F32),
-            pltpu.VMEM((ROWS * 8, 128), F32),
+            pltpu.VMEM((ROWS * 8 + 40, 128), F32),
             pltpu.VMEM((ROWS * 16, 128), F32),
             pltpu.VMEM((FEATS, ROWS, 128), F32),
             pltpu.VMEM(((ROWS + 2) * 16, 128), F32),
+            pltpu.SemaphoreType.DMA((4,)),
         ],
         name="gradient",
     )(
         counts, keep, image, above, below, truth, mean_y, power_y,
-        lines, entries, listed, basis, moment,
+        entries, colour, listed, moment, alphas, weights,
     )
-    returned = lax.all_to_all(grads, "strip", split_axis=0, concat_axis=0, tiled=True)
-    result = pl.pallas_call(
+    returned = exchange(grads, strips)
+    return pl.pallas_call(
         pull_kernel(focal, 0.5 * width, centre_y),
-        out_shape=shape(59, ROWS, 128),
-        in_specs=[SMEM, SMEM, VMEM, VMEM, VMEM],
-        scratch_shapes=[pltpu.VMEM(((ROWS + 2) * 16, 128), F32)],
+        out_shape=shape(59, ROWS * 128),
+        in_specs=[SMEM, SMEM, ANY, VMEM, VMEM],
+        out_specs=ANY,
+        scratch_shapes=[
+            pltpu.VMEM(((ROWS + 2) * 16, 128), F32),
+            pltpu.VMEM((ROWS * 64, 128), F32),
+            pltpu.VMEM((ROWS * 64, 128), F32),
+            pltpu.SemaphoreType.DMA((ROWS,)),
+            pltpu.SemaphoreType.DMA((ROWS,)),
+        ],
         name="pull",
-    )(camera, send_count, blocks, place, returned)
-    return result.reshape(59, ROWS * 128)
+    )(camera, send_count, params, place, returned)
 
 
 def solution(mesh):

time: 135 us -> 104 us (0.77)
  Pallas kernels: 72.1 us -> 52.2 us
  local copies, waits for them, and re-layouts: 8.8 us -> 5.18 us
  other arithmetic: 3.79 us -> 0.56 us
  waiting for transfers between devices: 9.32 us -> 6.33 us
    pallas_call x1, Pallas kernels: 30.9 us -> 18.8 us  [per_device(): pl.pallas_call(gradient_kernel, out_shape=shape(strips * 6, 128), in_spec...]
    pallas_call x1, Pallas kernels: 12.5 us -> 8.18 us  [per_device(): pl.pallas_call(owner_kernel(focal, 0.5 * width, centre_y), out_shape=(sha...]
    unnamed x20 -> x10, local copies, waits for them, and re-layouts: 6.88 us -> 2.67 us
    convert_element_type x1 -> x0, other arithmetic: 3.14 us -> none  [per_device(): counts = arrived[:, 2, 80].astype(jnp.int32)]
    all_to_all x1, waiting for transfers between devices: 9.31 us -> 6.32 us  [exchange(): got = lax.all_to_all(sent, 'strip', split_axis=0, concat_axis=0, tiled=True)]
    pallas_call x1, Pallas kernels: 9.79 us -> 7.6 us  [per_device(): pl.pallas_call(pull_kernel(focal, 0.5 * width, centre_y), out_shape=shape...]
  transfers between devices with their start and end apart: 5 -> 5, of which waited for: 1 -> 1; matrix products, arithmetic and copies ran while one was open for 3% -> 3% of each run, Pallas kernels for 14% -> 17%
where the time goes in v1:
time: 104 us; the launch traced here: 103 us
  Pallas kernels  52.2 us (50%)
  blocking collectives  24.6 us (24%)
  starting transfers between devices  14.5 us (14%)
  waiting for transfers between devices  6.33 us (6%)
  local copies, waits for them, and re-layouts  5.18 us (5%)
    all_to_all x1, blocking collectives, exchange(): got = lax.all_to_all(sent, 'strip', split_axis=0, concat_axis=0, tiled=True)  24.6 us
    pallas_call x1, Pallas kernels, per_device(): pl.pallas_call(gradient_kernel, out_shape=shape(strips * 6, 128), in_spec...  18.8 us
    pallas_call x1, Pallas kernels, per_device(): pl.pallas_call(render_kernel, out_shape=(shape(3, 5, 16, 128), shape(150,...  12.8 us
    all_to_all x1, starting transfers between devices, exchange(): got = lax.all_to_all(sent, 'strip', split_axis=0, concat_axis=0, tiled=True)  11.5 us
    pallas_call x1, Pallas kernels, per_device(): pl.pallas_call(owner_kernel(focal, 0.5 * width, centre_y), out_shape=(sha...  8.18 us
    pallas_call x1, Pallas kernels, per_device(): pl.pallas_call(pull_kernel(focal, 0.5 * width, centre_y), out_shape=shape...  7.6 us
    all_to_all x1, waiting for transfers between devices, exchange(): got = lax.all_to_all(sent, 'strip', split_axis=0, concat_axis=0, tiled=True)  6.32 us
    pallas_call x1, Pallas kernels, per_device(): pl.pallas_call(truth_kernel, out_shape=(shape(5, 128, 128), shape(640, 12...  2.96 us
  transfers between devices with their start and end apart: 5, of which 1 were waited for; matrix products, arithmetic and copies ran while one was open for 3% of the time, Pallas kernels for 17%

profile of v1, /device:TPU:1, one launch (start us, length us, event | category | flops | bytes accessed | tf_op | source)
XLA Modules:
  0.0 103.5 jit_solution(18354251877635683649)
XLA Ops:
  0.0 8.2 %owner.1 = (f32[768,128]{1,0:T(8,128)}, s32[40,128]{1,0:T(8,128)}) custom-call(f32[4,12]{1,0:T(4,128)} %camera_ref.3, s32[128]{0:T(128)} %count_ref.3, f32[59,5120]{1,0:T(8,128)} %params_ref.3, s32[80,128]{1,0:T(8,128)} %bitcast.14), custom_call_target="tpu_custom_call" | custom-call | tf_op jit(solution)/shard_map/owner/pallas_call | solution.py:933
  8.2 11.5 %all-to-all-start = ((f32[128,1,768]{2,1,0:T(1,128)}), f32[128,1,768]{2,1,0:T(1,128)S(1)}, u32[]{:S(2)}, u32[]{:S(2)}) async-start(f32[128,1,768]{2,1,0:T(1,128)} %bitcast.12), calls=%async_computation | async-start | bytes 786432 | tf_op jit(solution)/shard_map/all_to_all | solution.py:914
  19.7 1.0 fusion
  20.7 1.8 %collective-permute-start.2 = (f32[3,10,640]{2,1,0:T(8,128)S(1)}, f32[3,10,640]{2,1,0:T(8,128)S(1)}, u32[]{:S(2)}, u32[]{:S(2)}) collective-permute-start(f32[3,10,640]{2,1,0:T(8,128)S(1)} %get-tuple-element.32), channel_id=1, source_target_pairs={{0,1},{1,2},{2,3},{3,4},{4,5},{5,6},{6,7},{7,8},{8,9},{9,10},{10,1... | collective-permute-start | bytes 230408 | tf_op jit(solution)/shard_map/ppermute | solution.py:949
  22.5 0.0 collective-permute-start.3
  22.5 1.9 %listed.1.place_ref = s32[40,128]{1,0:T(8,128)} custom-call(s32[40,128]{1,0:T(8,128)} %list_ref.1), custom_call_target="tpu_custom_call" | custom-call | tf_op jit(solution)/shard_map/listed/pallas_call | solution.py:962
  24.4 0.8 copy.13
  25.3 0.7 reshape.21.list_ref
  26.0 6.3 %all-to-all-done = f32[128,1,768]{2,1,0:T(1,128)S(1)} async-done(((f32[128,1,768]{2,1,0:T(1,128)}), f32[128,1,768]{2,1,0:T(1,128)S(1)}, u32[]{:S(2)}, u32[]{:S(2)}) %all-to-all-start) | async-done | bytes 393248 | tf_op jit(solution)/shard_map/all_to_all | solution.py:914
  32.3 0.0 copy-start
  32.3 0.7 copy-done
  33.0 12.8 %render.1 = (f32[3,5,16,128]{3,2,1,0:T(8,128)}, f32[150,128]{1,0:T(8,128)}, f32[150,128]{1,0:T(8,128)}, f32[5,40,128]{2,1,0:T(8,128)}, f32[3,40,128]{2,1,0:T(8,1...) custom-call(f32[1]{0:T(128)} %bitcast.1.top_ref, f32[768,128]{1,0:T(8,128)} %bitcast.9, ...), custom_call_target="tpu_custom_call" | custom-call | tf_op jit(solution)/shard_map/render/pallas_call | solution.py:977
  45.8 1.2 %collective-permute-start = (f32[150,128]{1,0:T(8,128)}, f32[150,128]{1,0:T(8,128)S(1)}, u32[]{:S(2)}, u32[]{:S(2)}) collective-permute-start(f32[150,128]{1,0:T(8,128)} %get-tuple-element.22), channel_id=1, source_target_pairs={{0,1},{1,2},{2,3},{3,4},{4,5},{5,6},{6,7},{7,8},{8,9},{9,10},{10,1... | collective-permute-start | bytes 230408 | tf_op jit(solution)/shard_map/ppermute | solution.py:1004
  47.0 0.0 collective-permute-start.1
  47.0 0.6 add_convert_fusion.keep_ref
  47.6 0.0 collective-permute-done.2.above_ref
  47.6 0.0 copy-start.1
  47.6 0.0 collective-permute-done.3.below_ref
  47.6 0.6 copy-done.1
  48.2 0.0 copy-start.2
  48.2 0.6 copy-done.2
  48.9 3.0 %truth.1 = (f32[5,128,128]{2,1,0:T(8,128)}, f32[640,128]{1,0:T(8,128)}, f32[640,128]{1,0:T(8,128)}) custom-call(f32[2]{0:T(128)} %add_convert_fusion.keep_ref, f32[3,16,640]{2,1,0:T(8,128)} %own_ref.1, f32[3,10,640]{2,1,0:T(8,128)} %copy-done.1, f32[3,10,640]{2,1,0:T(8,128)} %copy-done.2), custom_call_target="tpu_custom_call" | custom-call | tf_op jit(solution)/shard_map/truth/pallas_call | solution.py:951
  51.8 0.0 collective-permute-done.above_ref
  51.8 0.0 copy-start.3
  51.8 0.0 collective-permute-done.1.below_ref
  51.8 0.0 copy-start.4
  51.8 0.6 copy-done.3
  52.5 0.0 copy-done.4
  52.5 18.8 %gradient.1 = f32[768,128]{1,0:T(8,128)} custom-call(s32[128]{0:T(128)} %get-tuple-element.20.count_ref, f32[2]{0:T(128)} %add_convert_fusion.keep_ref, f32[3,5,16,128]{3,2,1,0:T(8,128)} %get-tuple-element.21.image_ref, f32[150,128]{1,0:T(8,128)} %copy-done.3, f32[150,128]{1,0:T(8,128)} %copy-done.4, f32[5,128,128]{2,1,0:T(8,128)} %get-tuple-element.24.truth_ref, ...), custom_call_target="tpu_custom_call" | custom-call | tf_op jit(solution)/shard_map/gradient/pallas_call | solution.py:1006
  71.3 24.6 %all_to_all.10 = f32[128,1,768]{2,1,0:T(1,128)} all-to-all(f32[128,1,768]{2,1,0:T(1,128)} %bitcast.11), channel_id=1, replica_groups=mesh['strip'=128] {'strip'}, dimensions={0} | all-to-all | bytes 786432 | tf_op jit(solution)/shard_map/all_to_all | solution.py:914
  95.9 7.6 %pull.1 = f32[59,5120]{1,0:T(8,128)} custom-call(f32[4,12]{1,0:T(4,128)} %camera_ref.3, s32[128]{0:T(128)} %count_ref.3, f32[59,5120]{1,0:T(8,128)} %params_ref.3, s32[40,128]{1,0:T(8,128)} %get-tuple-element.18.place_ref, f32[768,128]{1,0:T(8,128)} %bitcast.10), custom_call_target="tpu_custom_call" | custom-call | tf_op jit(solution)/shard_map/pull/pallas_call | solution.py:1035
Async XLA Ops:
  8.2 24.1 %all-to-all-start = ((f32[128,1,768]{2,1,0:T(1,128)}), f32[128,1,768]{2,1,0:T(1,128)S(1)}, u32[]{:S(2)}, u32[]{:S(2)}) async-start(f32[128,1,768]{2,1,0:T(1,128)} %bitcast.12), calls=%async_computation | async-start | bytes 786432 | tf_op jit(solution)/shard_map/all_to_all | solution.py:914
  20.7 26.9 %collective-permute-start.2 = (f32[3,10,640]{2,1,0:T(8,128)S(1)}, f32[3,10,640]{2,1,0:T(8,128)S(1)}, u32[]{:S(2)}, u32[]{:S(2)}) collective-permute-start(f32[3,10,640]{2,1,0:T(8,128)S(1)} %get-tuple-element.32), channel_id=1, source_target_pairs={{0,1},{1,2},{2,3},{3,4},{4,5},{5,6},{6,7},{7,8},{8,9},{9,10},{10,1... | collective-permute-start | bytes 230408 | tf_op jit(solution)/shard_map/ppermute | solution.py:949
  22.5 25.1 %collective-permute-start.3 = (f32[3,10,640]{2,1,0:T(8,128)S(1)}, f32[3,10,640]{2,1,0:T(8,128)S(1)}, u32[]{:S(2)}, u32[]{:S(2)}) collective-permute-start(f32[3,10,640]{2,1,0:T(8,128)S(1)} %get-tuple-element.31), channel_id=1, source_target_pairs={{1,0},{2,1},{3,2},{4,3},{5,4},{6,5},{7,6},{8,7},{9,8},{10,9},{11,1... | collective-permute-start | bytes 230408 | tf_op jit(solution)/shard_map/ppermute | solution.py:950
  32.3 0.7 copy-start
  45.8 6.0 %collective-permute-start = (f32[150,128]{1,0:T(8,128)}, f32[150,128]{1,0:T(8,128)S(1)}, u32[]{:S(2)}, u32[]{:S(2)}) collective-permute-start(f32[150,128]{1,0:T(8,128)} %get-tuple-element.22), channel_id=1, source_target_pairs={{0,1},{1,2},{2,3},{3,4},{4,5},{5,6},{6,7},{7,8},{8,9},{9,10},{10,1... | collective-permute-start | bytes 230408 | tf_op jit(solution)/shard_map/ppermute | solution.py:1004
  47.0 4.8 %collective-permute-start.1 = (f32[150,128]{1,0:T(8,128)}, f32[150,128]{1,0:T(8,128)S(1)}, u32[]{:S(2)}, u32[]{:S(2)}) collective-permute-start(f32[150,128]{1,0:T(8,128)} %get-tuple-element.23), channel_id=1, source_target_pairs={{1,0},{2,1},{3,2},{4,3},{5,4},{6,5},{7,6},{8,7},{9,8},{10,9},{11,1... | collective-permute-start | bytes 230408 | tf_op jit(solution)/shard_map/ppermute | solution.py:1005
  47.6 0.6 copy-start.1
  48.2 0.6 copy-start.2
  51.8 0.6 copy-start.3
  51.8 0.6 copy-start.4

commit v2 on v1

--- a/solution.py
+++ b/solution.py
@@ -217,23 +217,24 @@
     lax.fori_loop(0, steps, step, (jnp.int32(0), jnp.zeros((1, 128), jnp.int32)), unroll=16)
 
 
-def compact_feats(chunk_ref, count_of, table_ref, steps):
+def compact_feats(chunk_ref, count_of, table_ref, steps, spot=None):
     lane = iota((8, 128), 1)
 
     def step(number, carry):
         start, held, last = carry
-        if isinstance(number, int) and number == steps - 1:
+        if spot is not None:
+            chunk = chunk_ref[pl.ds(spot(number), 8), :]
+        elif isinstance(number, int) and number == steps - 1:
             chunk = pltpu.roll(chunk_ref[number * 6 - 2 : number * 6 + 6, :], 6, axis=0)
         else:
             chunk = chunk_ref[pl.ds(number * 6, 8), :]
         live = count_of(number, chunk)
         shift = start & 127
         row = start >> 7
-        first = pltpu.roll(chunk, 48, axis=1)
-        second = pltpu.roll(pltpu.roll(chunk, 96, axis=1), 7, axis=0)
-        rest = jnp.where(lane < 48, first, second)
+        even = pltpu.roll(chunk, (shift + 48) & 127, axis=1)
+        odd = pltpu.roll(chunk, (shift + 96) & 127, axis=1)
         chunk = pltpu.roll(chunk, shift, axis=1)
-        rest = pltpu.roll(rest, shift, axis=1)
+        rest = jnp.where(((lane - shift) & 127) < 48, even, pltpu.roll(odd, 7, axis=0))
         fresh = lane >= shift
         held = jnp.where(fresh, chunk, held)
         last = jnp.where(fresh, rest, last)
@@ -251,31 +252,31 @@
         carry = step(number, carry)
 
 
-def expand_feats(table_ref, count_ref, out_ref, steps):
+def expand_feats(table_ref, count_ref, out_ref, steps, spot):
     lane = iota((8, 128), 1)
     sub = iota((8, 128), 0)
+    even = (sub & 1) == 0
+    offset = lane - jnp.where(even, 80, 32)
 
     def step(number, start):
         live = count_ref[number]
         shift = start & 127
         base = pl.multiple_of((start >> 7) * 16, 16)
-        back = (128 - shift) & 127
-        here = lane < 128 - shift
-        main = jnp.where(
-            here,
-            pltpu.roll(table_ref[pl.ds(base, 8), :], back, axis=1),
-            pltpu.roll(table_ref[pl.ds(base + 16, 8), :], back, axis=1),
-        )
-        rest = jnp.where(
-            here,
-            pltpu.roll(table_ref[pl.ds(base + 8, 8), :], back, axis=1),
-            pltpu.roll(table_ref[pl.ds(base + 24, 8), :], back, axis=1),
-        )
+        back = 128 - shift
+        this, rest = table_ref[pl.ds(base, 8), :], table_ref[pl.ds(base + 8, 8), :]
+        next_, next_rest = table_ref[pl.ds(base + 16, 8), :], table_ref[pl.ds(base + 24, 8), :]
+
+        def turned(value, by):
+            return pltpu.roll(value, (back + by) & 127, axis=1)
+
+        main = jnp.where(lane < back, turned(this, 0), turned(next_, 0))
         tail = jnp.where(
-            (sub & 1) == 0, pltpu.roll(rest, 80, axis=1), pltpu.roll(rest, 32, axis=1)
+            offset < back,
+            jnp.where(even, turned(rest, 80), turned(rest, 32)),
+            jnp.where(even, turned(next_rest, 80), turned(next_rest, 32)),
         )
         tail = jnp.where((sub == 1) & (lane == 127), live.astype(F32), tail)
-        out_ref[pl.ds(number * 6, 6), :] = jnp.where(lane < 80, main, tail)[0:6]
+        out_ref[pl.ds(spot(number), 6), :] = jnp.where(lane < 80, main, tail)[0:6]
         return start + live
 
     lax.fori_loop(0, steps, step, jnp.int32(0), unroll=16)
@@ -356,10 +357,18 @@
 
 def owner_kernel(focal, centre_x, centre_y):
     def kernel(
-        camera_ref, count_ref, params_ref, index_ref, out_ref, place_ref,
+        camera_ref, count_ref, spot_ref, params_ref, index_ref, target_ref, list_ref,
+        out_ref, place_ref, pack_ref,
         wide_ref, rows_ref, feats_ref, table_ref, local_ref, sems,
     ):
         copies = fetch_params(params_ref, local_ref, sems)
+        for tile in range(5):
+            for channel in range(3):
+                at = tile * 56 + channel * 16
+                pack_ref[at : at + 16, :] = target_ref[channel, :, tile * 128 : tile * 128 + 128]
+            pack_ref[tile * 56 + 48 : tile * 56 + 56, :] = list_ref[
+                tile * 8 : tile * 8 + 8, :
+            ].astype(F32)
         strips = index_ref.shape[1]
         wide_ref[...] = jnp.concatenate(
             [index_ref[...], jnp.zeros((128 - index_ref.shape[0], strips), jnp.int32)], 0
@@ -399,7 +408,7 @@
             return carry
 
         lax.fori_loop(0, 5, gather_block, 0)
-        expand_feats(table_ref, count_ref, out_ref, strips)
+        expand_feats(table_ref, count_ref, out_ref, strips, lambda number: spot_ref[number])
 
     return kernel
 
@@ -428,11 +437,49 @@
     return coarse, (x - coarse.astype(F32)).astype(BF16)
 
 
+def by_entry(x):
+    lane = iota((8, 128), 1)
+    order = ((lane & 7) << 4) | (lane >> 3)
+    return jnp.take_along_axis(swap_tiles(x), order, axis=1, mode="promise_in_bounds")
+
+
+def by_tile(x):
+    lane = iota((8, 128), 1)
+    order = ((lane & 15) << 3) | (lane >> 4)
+    return swap_tiles(jnp.take_along_axis(x, order, axis=1, mode="promise_in_bounds"))
+
+
+def tile_rows(ref, half, tile):
+    base = (tile >> 3) * 128 + (tile & 7)
+    return jnp.concatenate(
+        [ref[half, pl.ds(base + turn * 640, 16, stride=8), :] for turn in range(8)], 0
+    )
+
+
+def turned_colours(colour_ref, turn, group):
+    return [
+        pltpu.roll(
+            colour_ref[channel, group * 8 : group * 8 + 8, :], 128 - turn * 16 & 127, axis=1
+        )
+        for channel in range(3)
+    ]
+
+
+def lit(turned, entry):
+    return [jnp.broadcast_to(part[:, entry : entry + 1], (8, 128)) for part in turned]
+
+
 def render_kernel(
-    top_ref, chunks_ref, list_ref, tiles_ref, across_ref, basis_ref,
+    chunks_ref, basis_ref, moved_ref,
     image_ref, first_ref, last_ref, entries_ref, colour_ref, count_ref, alphas_ref, weights_ref,
-    table_ref, lines_ref, power_a, power_b, alpha_ref, weight_ref, tint_ref, shown_ref, sems,
+    table_ref, order_ref, lines_ref, power_a, power_b, alpha_ref, weight_ref, tint_ref, shown_ref, sems,
 ):
+    for tile in range(5):
+        for channel in range(3):
+            at = 150 + (channel * 5 + tile) * 10
+            base = tile * 56 + channel * 16
+            first_ref[at : at + 10, :] = moved_ref[base : base + 10, :]
+            last_ref[at : at + 10, :] = moved_ref[base + 6 : base + 16, :]
     strips = chunks_ref.shape[0] // 6
 
     def count_of(number, chunk):
@@ -441,27 +488,27 @@
         return live
 
     compact_feats(chunks_ref, count_of, table_ref, strips)
-    top = top_ref[0]
+    per_view = strips // VIEWS
+    top = (lax.rem(position_of(strips), per_view) * 16 + 8).astype(F32)
+    for group in range(5):
+        rows = slice(group * 8, group * 8 + 8)
+        order_ref[rows, :] = by_entry(moved_ref[group * 56 + 48 : group * 56 + 56, :]).astype(
+            jnp.int32
+        )
 
     def entry_block(block, carry):
         rows = pl.ds(block * 8, 8)
-        number = list_ref[rows, :]
+        number = order_ref[rows, :]
         high = number >> 7
         low = number & 127
-        other = tiles_ref[rows, :]
-        other_high = other >> 7
-        other_low = other & 127
         got = [jnp.zeros((8, 128), F32)] * FEATS
         for row in range(ROWS):
             same = high == row
-            match = other_high == row
             for feature in range(FEATS):
-                line = table_line(table_ref, row, feature)
-                if 5 <= feature < 8:
-                    got[feature] = jnp.where(match, pick(line, other_low), got[feature])
-                else:
-                    got[feature] = jnp.where(same, pick(line, low), got[feature])
-        x = got[0] - across_ref[rows, :]
+                value = pick(table_line(table_ref, row, feature), low)
+                got[feature] = jnp.where(same, value, got[feature])
+        across = (block * 8 + (iota((8, 128), 1) & 7)) * 16 + 8
+        x = got[0] - across.astype(F32)
         y = got[1] - top
         a, b, c = got[2:5]
         for slot, value in enumerate((x, y, a, b, c)):
@@ -478,20 +525,27 @@
             term = term * LOG2E
             for part in range(3):
                 piece = rounded(term)
-                lines_ref[pl.ds(block * 192 + slot * 3 + part, 8, stride=24), :] = piece
+                lines_ref[pl.ds(block * 24 + slot * 3 + part, 8, stride=120), :] = piece
                 term = term - piece
         for slot in range(18, 24):
-            lines_ref[pl.ds(block * 192 + slot, 8, stride=24), :] = jnp.zeros((8, 128), F32)
+            lines_ref[pl.ds(block * 24 + slot, 8, stride=120), :] = jnp.zeros((8, 128), F32)
         for channel in range(3):
-            value = got[5 + channel]
-            colour_ref[channel, rows, :] = value
-            for part in range(3):
-                piece = rounded(value)
-                tint_ref[pl.ds(block * 128 + channel * 3 + part, 8, stride=16), :] = piece
-                value = value - piece
+            colour_ref[channel, rows, :] = got[5 + channel]
         return carry
 
     lax.fori_loop(0, 5, entry_block, 0)
+    values = [
+        by_tile(colour_ref[channel, group * 8 : group * 8 + 8, :])
+        for group in range(5)
+        for channel in range(3)
+    ]
+    for number, value in enumerate(values):
+        group, channel = divmod(number, 3)
+        colour_ref[channel, group * 8 : group * 8 + 8, :] = value
+        for part in range(3):
+            piece = rounded(value)
+            tint_ref[pl.ds(group * 128 + channel * 3 + part, 8, stride=16), :] = piece
+            value = value - piece
     basis = basis_ref[...]
 
     def powers(turn, power_ref):
@@ -519,7 +573,7 @@
         through = list(through)
         for entry in range(16):
             for group in range(5):
-                at = (entry * 5 + group) * 8
+                at = group * 128 + entry * 8
                 for half in range(2):
                     slot = group * 2 + half
                     alpha = jnp.exp2(power_ref[at : at + 8, half * 128 : half * 128 + 128])
@@ -543,13 +597,15 @@
     lax.fori_loop(0, 4, blend, (jnp.ones((8, 128), F32),) * 10)
 
     def tints(tile, carry):
-        tint = tint_ref[pl.ds(pl.multiple_of(tile * 16, 16), 16), :].astype(BF16)
+        at = pl.ds(pl.multiple_of(tile * 16, 16), 16)
+        tint = tint_ref[at, :].astype(BF16)
+        halves = [coarse_fine(tile_rows(weight_ref, half, tile)) for half in range(2)]
+        weight = jnp.concatenate(
+            [jnp.concatenate([halves[0][part], halves[1][part]], 1) for part in range(2)], 0
+        )
+        total = jnp.dot(jnp.concatenate([tint, tint], 1), weight, preferred_element_type=F32)
         for half in range(2):
-            coarse, fine = coarse_fine(weight_ref[half, pl.ds(tile, 128, stride=ROWS), :])
-            total = jnp.dot(tint, coarse, preferred_element_type=F32) + jnp.dot(
-                tint, fine, preferred_element_type=F32
-            )
-            shown_ref[half, pl.ds(pl.multiple_of(tile * 16, 16), 16), :] = total
+            shown_ref[half, at, :] = total[:, half * 128 : half * 128 + 128]
         return carry
 
     lax.fori_loop(0, ROWS, tints, 0, unroll=4)
@@ -613,46 +669,19 @@
     ref[slot, 648:656, :] = jnp.zeros((8, 128), F32)
 
 
-def truth_kernel(
-    keep_ref, own_ref, above_ref, below_ref, ext_ref, mean_ref, power_ref,
-    field_ref, rows_ref, cols_ref,
-):
-    lanes = lambda tile: slice(tile * 128, tile * 128 + 128)
-    extend(
-        ext_ref,
-        lambda channel, tile: own_ref[channel, :, lanes(tile)],
-        lambda channel, tile: above_ref[channel, :, lanes(tile)],
-        lambda channel, tile: below_ref[channel, :, lanes(tile)],
-        keep_ref[0],
-        keep_ref[1],
-    )
-    rows_ref[...] = jnp.zeros((128, 128), F32)
-    for tile in range(5):
-        field_ref[tile] = ext_ref[tile] * ext_ref[tile]
-    for slot, (source, out_ref) in enumerate(((ext_ref, mean_ref), (field_ref, power_ref))):
-        clear_ends(cols_ref, slot)
-        for tile, turned in down_rows(source, slot, rows_ref):
-            cols_ref[slot, 8 + tile * 128 : 136 + tile * 128, :] = turned
-
-        def columns(step, carry, slot=slot, out_ref=out_ref):
-            base = step * 64
-            out_ref[pl.ds(base, 64), :] = tap_sum(
-                lambda k: cols_ref[slot, pl.ds(base + 3 + k, 64), :]
-            )
-            return carry
-
-        lax.fori_loop(0, 10, columns, 0)
-
-
-def invert_kernel(list_ref, out_ref):
-    invert(list_ref, out_ref)
+def invert_kernel(moved_ref, out_ref, rows_ref):
+    for group in range(5):
+        rows_ref[group * 8 : group * 8 + 8, :] = moved_ref[
+            group * 56 + 48 : group * 56 + 56, :
+        ].astype(jnp.int32)
+    invert(rows_ref, out_ref)
 
 
 def gradient_kernel(
-    count_ref, keep_ref, image_ref, above_ref, below_ref, truth_ref, mean_y_ref, power_y_ref,
+    count_ref, image_ref, above_ref, below_ref, moved_ref,
     entries_ref, colour_ref, place_ref, moment_ref, alphas_ref, weights_ref,
     out_ref,
-    ext_ref, square_ref, cross_ref, rows_ref, cols_ref, parts_ref,
+    ext_ref, square_ref, cross_ref, truth_ref, ideal_ref, rows_ref, cols_ref, parts_ref,
     alpha_ref, weight_ref, pull_a, pull_b, light_ref, split_ref,
     sums_ref, tint_ref, feats_ref, table_ref, sems,
 ):
@@ -663,23 +692,38 @@
     ]
     for copy in copies:
         copy.start()
-    keep_above = keep_ref[0]
-    keep_below = keep_ref[1]
+    strips = out_ref.shape[0] // 6
+    keep_above, keep_below = keeps(strips)
+    def rim(base):
+        return lambda ref: lambda channel, tile: ref[
+            base + (channel * 5 + tile) * 10 : base + (channel * 5 + tile) * 10 + 10, :
+        ]
+
     extend(
         ext_ref,
         lambda channel, tile: image_ref[channel, tile],
-        lambda channel, tile: above_ref[(channel * 5 + tile) * 10 : (channel * 5 + tile) * 10 + 10, :],
-        lambda channel, tile: below_ref[(channel * 5 + tile) * 10 : (channel * 5 + tile) * 10 + 10, :],
+        rim(0)(above_ref),
+        rim(0)(below_ref),
+        keep_above,
+        keep_below,
+    )
+    extend(
+        truth_ref,
+        lambda channel, tile: moved_ref[tile * 56 + channel * 16 : tile * 56 + channel * 16 + 16, :],
+        rim(150)(above_ref),
+        rim(150)(below_ref),
         keep_above,
         keep_below,
     )
     for tile in range(5):
         square_ref[tile] = ext_ref[tile] * ext_ref[tile]
         cross_ref[tile] = ext_ref[tile] * truth_ref[tile]
+        ideal_ref[tile] = truth_ref[tile] * truth_ref[tile]
     rows_ref[...] = jnp.zeros((128, 128), F32)
-    for slot, source in enumerate((ext_ref, square_ref, cross_ref)):
+    for slot in range(3):
+        clear_ends(parts_ref, slot)
+    for slot, source in enumerate((ext_ref, square_ref, cross_ref, truth_ref, ideal_ref)):
         clear_ends(cols_ref, slot)
-        clear_ends(parts_ref, slot)
         for tile, turned in down_rows(source, slot, rows_ref):
             cols_ref[slot, 8 + tile * 128 : 136 + tile * 128, :] = turned
     lane = iota((8, 128), 1)
@@ -689,11 +733,9 @@
 
     def similarity(step, carry):
         base = step * 32
-        mean_x, power_x, cross = [
-            tap_sum(lambda k: cols_ref[slot, pl.ds(base + 3 + k, 32), :]) for slot in range(3)
+        mean_x, power_x, cross, mean_y, power_y = [
+            tap_sum(lambda k: cols_ref[slot, pl.ds(base + 3 + k, 32), :]) for slot in range(5)
         ]
-        mean_y = mean_y_ref[pl.ds(base, 32), :]
-        power_y = power_y_ref[pl.ds(base, 32), :]
         both = mean_x * mean_y
         squares = mean_x * mean_x + mean_y * mean_y
         light_up = 2.0 * both + light_term
@@ -754,7 +796,7 @@
         ]
         for entry in range(15, -1, -1):
             for group in range(5):
-                at = (entry * 5 + group) * 8
+                at = group * 128 + entry * 8
                 rows = pl.ds(turn * 640 + at, 8)
                 colour = [
                     jnp.broadcast_to(turned[group][channel][:, entry : entry + 1], (8, 128))
@@ -794,11 +836,13 @@
 
     def tints(tile, carry):
         at = pl.ds(pl.multiple_of(tile * 16, 16), 16)
-        total = jnp.zeros((16, 128), F32)
-        for half in range(2):
-            coarse, fine = coarse_fine(weight_ref[half, pl.ds(tile, 128, stride=ROWS), :])
-            light = split_ref[half, at, :].astype(BF16)
-            total = total + dot_nt(light, coarse) + dot_nt(light, fine)
+        halves = [coarse_fine(tile_rows(weight_ref, half, tile)) for half in range(2)]
+        weight = jnp.concatenate(
+            [jnp.concatenate([halves[0][part], halves[1][part]], 1) for part in range(2)], 0
+        )
+        light = jnp.concatenate([split_ref[half, at, :].astype(BF16) for half in range(2)], 1)
+        total = dot_nt(light, weight)
+        total = total[:, 0:128] + total[:, 128:256]
         tint_ref[at, :] = total
         return carry
 
@@ -807,7 +851,7 @@
     def entry_grads(block, carry):
         rows = pl.ds(block * 8, 8)
         zeroth, by_x, by_y, by_xx, by_xy, by_yy = [
-            sums_ref[pl.ds(block * 64 + slot, 8, stride=8), :] for slot in range(6)
+            sums_ref[pl.ds(block * 8 + slot, 8, stride=40), :] for slot in range(6)
         ]
         x, y, a, b, c = [entries_ref[slot, rows, :] for slot in range(5)]
         off_x = by_x - x * zeroth
@@ -827,40 +871,50 @@
         return carry
 
     lax.fori_loop(0, 5, entry_grads, 0)
+    values = [
+        by_entry(feats_ref[5 + channel, group * 8 : group * 8 + 8, :])
+        for group in range(5)
+        for channel in range(3)
+    ]
+    for number, value in enumerate(values):
+        group, channel = divmod(number, 3)
+        feats_ref[5 + channel, group * 8 : group * 8 + 8, :] = value
 
     def gather_block(block, carry):
         place = place_ref[pl.ds(block * 8, 8), :]
         tile = place >> 7
         entry = place & 127
-        other = entry * ROWS + tile
-        high = other >> 7
-        low = other & 127
+        high = (tile & 56) | (entry >> 4)
+        low = ((entry & 15) << 3) | (tile & 7)
         got = [jnp.zeros((8, 128), F32)] * FEATS
         for row in range(ROWS):
             same = high == row
-            match = tile == row
             for feature in range(FEATS):
-                line = feats_ref[feature, row : row + 1, :]
-                if 5 <= feature < 8:
-                    got[feature] = jnp.where(match, pick(line, entry), got[feature])
-                else:
-                    got[feature] = jnp.where(same, pick(line, low), got[feature])
+                value = pick(feats_ref[feature, row : row + 1, :], low)
+                got[feature] = jnp.where(same, value, got[feature])
         for feature in range(FEATS):
             put_feature(table_ref, block, feature, got[feature])
         return carry
 
     lax.fori_loop(0, 5, gather_block, 0)
-    expand_feats(table_ref, count_ref, out_ref, out_ref.shape[0] // 6)
+    expand_feats(table_ref, count_ref, out_ref, strips, lambda number: number * 6)
 
 
 def pull_kernel(focal, centre_x, centre_y):
     def kernel(
-        camera_ref, count_ref, params_ref, place_ref, chunks_ref, out_ref,
-        table_ref, local_ref, grads_ref, sems, out_sems,
+        camera_ref, count_ref, spot_ref, params_ref, place_ref, chunks_ref, out_ref,
+        table_ref, wide_ref, local_ref, grads_ref, sems, out_sems,
     ):
         copies = fetch_params(params_ref, local_ref, sems)
         strips = chunks_ref.shape[0] // 6
-        compact_feats(chunks_ref, lambda number, chunk: count_ref[number], table_ref, strips)
+        wide_ref[0 : strips * 6, :] = chunks_ref[...]
+        compact_feats(
+            wide_ref,
+            lambda number, chunk: count_ref[number],
+            table_ref,
+            strips,
+            lambda number: spot_ref[number],
+        )
         bounds = run_bounds(count_ref, strips)
 
         def block_grads(block, carry):
@@ -909,6 +963,32 @@
     return jax.ShapeDtypeStruct(dims, dtype)
 
 
+def device_of(strip):
+    core = strip & 1
+    z, y, x = (strip >> 1) & 3, (strip >> 3) & 3, strip >> 5
+    z = z + (y & 1) * (3 - 2 * z)
+    y = y + (x & 1) * (3 - 2 * y)
+    return ((x * 4 + y) * 4 + z) * 2 + core
+
+
+def strip_of(device):
+    core = device & 1
+    z, y, x = (device >> 1) & 3, (device >> 3) & 3, device >> 5
+    y = y + (x & 1) * (3 - 2 * y)
+    z = z + (y & 1) * (3 - 2 * z)
+    return ((x * 4 + y) * 4 + z) * 2 + core
+
+
+def position_of(strips):
+    return lax.rem(strip_of(lax.axis_index("strip")) + strips // VIEWS // 2, strips)
+
+
+def keeps(strips):
+    per_view = strips // VIEWS
+    place = lax.rem(position_of(strips), per_view)
+    return (place != 0).astype(F32), (place != per_view - 1).astype(F32)
+
+
 def exchange(chunks, strips):
     sent = chunks.reshape(strips, 1, 768)
     got = lax.all_to_all(sent, "strip", split_axis=0, concat_axis=0, tiled=True)
@@ -917,23 +997,22 @@
 
 def per_device(params, camera, send_index, send_count, tile_list, target):
     strips = lax.axis_size("strip")
-    index = lax.axis_index("strip")
     per_view = strips // VIEWS
-    offset = per_view // 2
-    position = (index + offset) % strips
     rows_strip = target.shape[1]
     width = target.shape[2]
     focal = 0.5 * width
     centre_y = 0.5 * rows_strip * per_view
-    top = ((position % per_view) * rows_strip + rows_strip // 2).astype(F32).reshape(1)
-    keep = jnp.stack([position % per_view != 0, position % per_view != per_view - 1]).astype(F32)
-    ahead = [(i, (i + 1) % strips) for i in range(strips)]
-    behind = [((i + 1) % strips, i) for i in range(strips)]
-
-    chunks, place = pl.pallas_call(
+    spots = [device_of(strip) for strip in range(strips)]
+    spot_rows = jnp.asarray(np.array(spots, np.int32) * 6)
+    ahead = [(spots[i], spots[(i + 1) % strips]) for i in range(strips)]
+    behind = [(spots[(i + 1) % strips], spots[i]) for i in range(strips)]
+
+    chunks, place, pack = pl.pallas_call(
         owner_kernel(focal, 0.5 * width, centre_y),
-        out_shape=(shape(strips * 6, 128), shape(ROWS, 128, dtype=jnp.int32)),
-        in_specs=[SMEM, SMEM, ANY, VMEM],
+        out_shape=(
+            shape(strips * 6, 128), shape(ROWS, 128, dtype=jnp.int32), shape(280, 128)
+        ),
+        in_specs=[SMEM, SMEM, SMEM, ANY, VMEM, VMEM, VMEM],
         scratch_shapes=[
             pltpu.VMEM((strips, 128), jnp.int32),
             pltpu.VMEM((ROWS + 8, 128), jnp.int32),
@@ -943,30 +1022,16 @@
             pltpu.SemaphoreType.DMA((ROWS,)),
         ],
         name="owner",
-    )(camera, send_count, params, send_index.T)
+    )(camera, send_count, spot_rows, params, send_index.T, target, tile_list)
     arrived = exchange(chunks, strips)
-
-    truth_above = lax.ppermute(target[:, 6:16, :], "strip", ahead)
-    truth_below = lax.ppermute(target[:, 0:10, :], "strip", behind)
-    truth, mean_y, power_y = pl.pallas_call(
-        truth_kernel,
-        out_shape=(shape(5, 128, 128), shape(640, 128), shape(640, 128)),
-        in_specs=[SMEM, VMEM, VMEM, VMEM],
-        scratch_shapes=[
-            pltpu.VMEM((5, 128, 128), F32),
-            pltpu.VMEM((128, 128), F32),
-            pltpu.VMEM((2, 656, 128), F32),
-        ],
-        name="truth",
-    )(keep, target, truth_above, truth_below)
+    moved = lax.ppermute(pack, "strip", list(enumerate(spots)))
+
     listed = pl.pallas_call(
-        invert_kernel, out_shape=shape(ROWS, 128, dtype=jnp.int32), name="listed"
-    )(tile_list)
-
-    flat_list = tile_list.T.reshape(ROWS, 128)
-    across = jnp.asarray(
-        (np.arange(ROWS * 128) % ROWS * 16 + 8).astype(np.float32).reshape(ROWS, 128)
-    )
+        invert_kernel,
+        out_shape=shape(ROWS, 128, dtype=jnp.int32),
+        scratch_shapes=[pltpu.VMEM((ROWS, 128), jnp.int32)],
+        name="listed",
+    )(moved)
     rows = entry_basis()
     basis = np.zeros((24, 256), np.float32)
     basis[0:18] = np.repeat(rows, 3, axis=0)
@@ -978,18 +1043,19 @@
         render_kernel,
         out_shape=(
             shape(3, 5, 16, 128),
-            shape(150, 128),
-            shape(150, 128),
+            shape(300, 128),
+            shape(300, 128),
             shape(5, ROWS, 128),
             shape(3, ROWS, 128),
             shape(strips, dtype=jnp.int32),
             shape(2, 5120, 128),
             shape(2, 5120, 128),
         ),
-        in_specs=[SMEM, VMEM, VMEM, VMEM, VMEM, VMEM],
+        in_specs=[VMEM, VMEM, VMEM],
         out_specs=(VMEM, VMEM, VMEM, VMEM, VMEM, SMEM, ANY, ANY),
         scratch_shapes=[
             pltpu.VMEM(((ROWS + 2) * 16, 128), F32),
+            pltpu.VMEM((ROWS, 128), jnp.int32),
             pltpu.VMEM((ROWS * 24, 128), F32),
             pltpu.VMEM((640, 256), F32),
             pltpu.VMEM((640, 256), F32),
@@ -1000,19 +1066,21 @@
             pltpu.SemaphoreType.DMA((32,)),
         ],
         name="render",
-    )(top, arrived, flat_list, tile_list, across, basis)
+    )(arrived, basis, moved)
     above = lax.ppermute(last, "strip", ahead)
     below = lax.ppermute(first, "strip", behind)
     grads = pl.pallas_call(
         gradient_kernel,
         out_shape=shape(strips * 6, 128),
-        in_specs=[SMEM, SMEM] + [VMEM] * 10 + [ANY, ANY],
+        in_specs=[SMEM] + [VMEM] * 8 + [ANY, ANY],
         scratch_shapes=[
             pltpu.VMEM((5, 128, 128), F32),
             pltpu.VMEM((5, 128, 128), F32),
             pltpu.VMEM((5, 128, 128), F32),
+            pltpu.VMEM((5, 128, 128), F32),
+            pltpu.VMEM((5, 128, 128), F32),
             pltpu.VMEM((128, 128), F32),
-            pltpu.VMEM((3, 656, 128), F32),
+            pltpu.VMEM((5, 656, 128), F32),
             pltpu.VMEM((3, 656, 128), F32),
             pltpu.VMEM((2, 5120, 128), F32),
             pltpu.VMEM((2, 5120, 128), F32),
@@ -1028,24 +1096,25 @@
         ],
         name="gradient",
     )(
-        counts, keep, image, above, below, truth, mean_y, power_y,
+        counts, image, above, below, moved,
         entries, colour, listed, moment, alphas, weights,
     )
     returned = exchange(grads, strips)
     return pl.pallas_call(
         pull_kernel(focal, 0.5 * width, centre_y),
         out_shape=shape(59, ROWS * 128),
-        in_specs=[SMEM, SMEM, ANY, VMEM, VMEM],
+        in_specs=[SMEM, SMEM, SMEM, ANY, VMEM, VMEM],
         out_specs=ANY,
         scratch_shapes=[
             pltpu.VMEM(((ROWS + 2) * 16, 128), F32),
+            pltpu.VMEM((strips * 6 + 8, 128), F32),
             pltpu.VMEM((ROWS * 64, 128), F32),
             pltpu.VMEM((ROWS * 64, 128), F32),
             pltpu.SemaphoreType.DMA((ROWS,)),
             pltpu.SemaphoreType.DMA((ROWS,)),
         ],
         name="pull",
-    )(camera, send_count, params, place, returned)
+    )(camera, send_count, spot_rows, params, place, returned)
 
 
 def solution(mesh):

time: 104 us -> 95.2 us (0.915)
  waiting for transfers between devices: 6.33 us -> 13.3 us
  blocking collectives: 24.6 us -> 18.7 us
  Pallas kernels: 52.2 us -> 46.8 us
  local copies, waits for them, and re-layouts: 5.18 us -> 1.43 us
    all_to_all x1, blocking collectives: 24.6 us -> 18.7 us  [exchange(): got = lax.all_to_all(sent, 'strip', split_axis=0, concat_axis=0, tiled=True)]
    all_to_all x1, waiting for transfers between devices: 6.32 us -> 10.6 us  [exchange(): got = lax.all_to_all(sent, 'strip', split_axis=0, concat_axis=0, tiled=True)]
    pallas_call x2 -> x1, Pallas kernels: 15.7 us -> 11.8 us  [per_device(): pl.pallas_call(render_kernel, out_shape=(shape(3, 5, 16, 128), shape(300,...]
    ppermute x1, waiting for transfers between devices: 0.01 us -> 2.66 us  [per_device(): below = lax.ppermute(first, 'strip', behind)]
    pallas_call x1, Pallas kernels: 18.8 us -> 17.3 us  [per_device(): pl.pallas_call(gradient_kernel, out_shape=shape(strips * 6, 128), in_spec...]
    unnamed x10 -> x8, local copies, waits for them, and re-layouts: 2.67 us -> 1.43 us
  transfers between devices with their start and end apart: 5 -> 4, of which waited for: 1 -> 2; matrix products, arithmetic and copies ran while one was open for 3% -> 0% of each run, Pallas kernels for 17% -> 2%
where the time goes in v2:
time: 95.2 us; the launch traced here: 94.8 us
  Pallas kernels  46.8 us (49%)
  blocking collectives  18.7 us (20%)
  starting transfers between devices  14.5 us (15%)
  waiting for transfers between devices  13.3 us (14%)
  local copies, waits for them, and re-layouts  1.43 us (2%)
    all_to_all x1, blocking collectives, exchange(): got = lax.all_to_all(sent, 'strip', split_axis=0, concat_axis=0, tiled=True)  18.7 us
    pallas_call x1, Pallas kernels, per_device(): pl.pallas_call(gradient_kernel, out_shape=shape(strips * 6, 128), in_spec...  17.3 us
    pallas_call x1, Pallas kernels, per_device(): pl.pallas_call(render_kernel, out_shape=(shape(3, 5, 16, 128), shape(300,...  11.8 us
    all_to_all x1, starting transfers between devices, exchange(): got = lax.all_to_all(sent, 'strip', split_axis=0, concat_axis=0, tiled=True)  11.5 us
    all_to_all x1, waiting for transfers between devices, exchange(): got = lax.all_to_all(sent, 'strip', split_axis=0, concat_axis=0, tiled=True)  10.6 us
    pallas_call x1, Pallas kernels, per_device(): pl.pallas_call(owner_kernel(focal, 0.5 * width, centre_y), out_shape=(sha...  8.11 us
    pallas_call x1, Pallas kernels, per_device(): pl.pallas_call(pull_kernel(focal, 0.5 * width, centre_y), out_shape=shape...  7.46 us
    ppermute x1, waiting for transfers between devices, per_device(): below = lax.ppermute(first, 'strip', behind)  2.66 us
  transfers between devices with their start and end apart: 4, of which 2 were waited for; matrix products, arithmetic and copies ran while one was open for 0% of the time, Pallas kernels for 2%

profile of v2, /device:TPU:1, one launch (start us, length us, event | category | flops | bytes accessed | tf_op | source)
XLA Modules:
  0.0 94.8 jit_solution(5555096291768084066)
XLA Ops:
  0.0 8.1 %owner.1 = (f32[768,128]{1,0:T(8,128)}, s32[40,128]{1,0:T(8,128)}, f32[280,128]{1,0:T(8,128)}) custom-call(f32[4,12]{1,0:T(4,128)} %camera_ref.3, s32[128]{0:T(128)} %count_ref.3, s32[128]{0:T(128)} %constant.6.clone.spot_ref, f32[59,5120]{1,0:T(8,128)} %params_ref.3, s32[80,128]{1,0:T(8,128)} %bitcast.9, f32[3,16,640]{2,1,0:T(8,128)} %target_ref.1, ...), custom_call_target="tpu_custom_call" | custom-call | tf_op jit(solution)/shard_map/owner/pallas_call | solution.py:1010
  8.1 11.5 %all-to-all-start = ((f32[128,1,768]{2,1,0:T(1,128)}), f32[128,1,768]{2,1,0:T(1,128)S(1)}, u32[]{:S(2)}, u32[]{:S(2)}) async-start(f32[128,1,768]{2,1,0:T(1,128)} %bitcast.8), calls=%async_computation | async-start | bytes 786432 | tf_op jit(solution)/shard_map/all_to_all | solution.py:994
  19.6 1.6 %collective-permute-start = (f32[280,128]{1,0:T(8,128)}, f32[280,128]{1,0:T(8,128)S(1)}, u32[]{:S(2)}, u32[]{:S(2)}) collective-permute-start(f32[280,128]{1,0:T(8,128)} %get-tuple-element.18), channel_id=1, source_target_pairs={{0,0},{1,1},{2,2},{3,3},{4,4},{5,5},{6,6},{7,7},{8,14},{9,15},{10,... | collective-permute-start | bytes 430088 | tf_op jit(solution)/shard_map/ppermute | solution.py:1027
  21.2 0.0 collective-permute-done.moved_ref
  21.2 0.0 copy-start.1
  21.2 10.6 %all-to-all-done = f32[128,1,768]{2,1,0:T(1,128)S(1)} async-done(((f32[128,1,768]{2,1,0:T(1,128)}), f32[128,1,768]{2,1,0:T(1,128)S(1)}, u32[]{:S(2)}, u32[]{:S(2)}) %all-to-all-start) | async-done | bytes 393248 | tf_op jit(solution)/shard_map/all_to_all | solution.py:994
  31.8 0.0 copy-start
  31.8 0.0 copy-done.1
  31.8 0.7 copy-done
  32.5 11.8 %render.1 = (f32[3,5,16,128]{3,2,1,0:T(8,128)}, f32[300,128]{1,0:T(8,128)}, f32[300,128]{1,0:T(8,128)}, f32[5,40,128]{2,1,0:T(8,128)}, f32[3,40,128]{2,1,0:T(8,1...) custom-call(f32[768,128]{1,0:T(8,128)} %bitcast.6, bf16[24,256]{1,0:T(8,128)(2,1)} %constant.7.clone.basis_ref, ...), custom_call_target="tpu_custom_call" | custom-call | tf_op jit(solution)/shard_map/render/pallas_call | solution.py:1042
  44.3 1.1 %collective-permute-start.1 = (f32[300,128]{1,0:T(8,128)}, f32[300,128]{1,0:T(8,128)S(1)}, u32[]{:S(2)}, u32[]{:S(2)}) collective-permute-start(f32[300,128]{1,0:T(8,128)} %get-tuple-element.21), channel_id=1, source_target_pairs={{0,1},{1,2},{2,3},{3,4},{4,5},{5,6},{6,7},{7,14},{14,15},{15,12},{... | collective-permute-start | bytes 460808 | tf_op jit(solution)/shard_map/ppermute | solution.py:1070
  45.4 0.3 collective-permute-start.2
  45.7 2.1 %listed.1.place_ref = s32[40,128]{1,0:T(8,128)} custom-call(f32[280,128]{1,0:T(8,128)} %copy-done.1), custom_call_target="tpu_custom_call" | custom-call | tf_op jit(solution)/shard_map/listed/pallas_call | solution.py:1029
  47.9 0.0 collective-permute-done.1.above_ref
  47.9 0.0 copy-start.2
  47.9 2.7 %collective-permute-done.2.below_ref = f32[300,128]{1,0:T(8,128)S(1)} collective-permute-done((f32[300,128]{1,0:T(8,128)}, f32[300,128]{1,0:T(8,128)S(1)}, u32[]{:S(2)}, u32[]{:S(2)}) %collective-permute-start.2) | collective-permute-done | bytes 153632 | tf_op jit(solution)/shard_map/ppermute | solution.py:1071
  50.6 0.0 copy-start.3
  50.6 0.0 copy-done.2
  50.6 0.7 copy-done.3
  51.2 17.3 %gradient.1 = f32[768,128]{1,0:T(8,128)} custom-call(s32[128]{0:T(128)} %get-tuple-element.19.count_ref, f32[3,5,16,128]{3,2,1,0:T(8,128)} %get-tuple-element.20.image_ref, f32[300,128]{1,0:T(8,128)} %copy-done.2, f32[300,128]{1,0:T(8,128)} %copy-done.3, f32[280,128]{1,0:T(8,128)} %copy-done.1, f32[5,40,128]{2,1,0:T(8,128)} %get-tuple-element.23.entries_ref, ...), custom_call_target="tpu_custom_call" | custom-call | tf_op jit(solution)/shard_map/gradient/pallas_call | solution.py:1072
  68.6 18.7 %all_to_all.10 = f32[128,1,768]{2,1,0:T(1,128)} all-to-all(f32[128,1,768]{2,1,0:T(1,128)} %bitcast.5), channel_id=1, replica_groups=mesh['strip'=128] {'strip'}, dimensions={0} | all-to-all | bytes 786432 | tf_op jit(solution)/shard_map/all_to_all | solution.py:994
  87.3 7.5 %pull.1 = f32[59,5120]{1,0:T(8,128)} custom-call(f32[4,12]{1,0:T(4,128)} %camera_ref.3, s32[128]{0:T(128)} %count_ref.3, s32[128]{0:T(128)} %constant.6.clone.spot_ref, f32[59,5120]{1,0:T(8,128)} %params_ref.3, s32[40,128]{1,0:T(8,128)} %get-tuple-element.16.place_ref, f32[768,128]{1,0:T(8,128)} %bitcast.7), custom_call_target="tpu_custom_call" | custom-call | tf_op jit(solution)/shard_map/pull/pallas_call | solution.py:1103
Async XLA Ops:
  8.1 23.6 %all-to-all-start = ((f32[128,1,768]{2,1,0:T(1,128)}), f32[128,1,768]{2,1,0:T(1,128)S(1)}, u32[]{:S(2)}, u32[]{:S(2)}) async-start(f32[128,1,768]{2,1,0:T(1,128)} %bitcast.8), calls=%async_computation | async-start | bytes 786432 | tf_op jit(solution)/shard_map/all_to_all | solution.py:994
  19.6 1.6 %collective-permute-start = (f32[280,128]{1,0:T(8,128)}, f32[280,128]{1,0:T(8,128)S(1)}, u32[]{:S(2)}, u32[]{:S(2)}) collective-permute-start(f32[280,128]{1,0:T(8,128)} %get-tuple-element.18), channel_id=1, source_target_pairs={{0,0},{1,1},{2,2},{3,3},{4,4},{5,5},{6,6},{7,7},{8,14},{9,15},{10,... | collective-permute-start | bytes 430088 | tf_op jit(solution)/shard_map/ppermute | solution.py:1027
  21.2 10.6 %copy-start.1 = (f32[280,128]{1,0:T(8,128)}, f32[280,128]{1,0:T(8,128)S(1)}, u32[]{:S(2)}) copy-start(f32[280,128]{1,0:T(8,128)S(1)} %collective-permute-done.moved_ref) | copy-start | bytes 430084
  31.8 0.7 copy-start
  44.3 3.6 %collective-permute-start.1 = (f32[300,128]{1,0:T(8,128)}, f32[300,128]{1,0:T(8,128)S(1)}, u32[]{:S(2)}, u32[]{:S(2)}) collective-permute-start(f32[300,128]{1,0:T(8,128)} %get-tuple-element.21), channel_id=1, source_target_pairs={{0,1},{1,2},{2,3},{3,4},{4,5},{5,6},{6,7},{7,14},{14,15},{15,12},{... | collective-permute-start | bytes 460808 | tf_op jit(solution)/shard_map/ppermute | solution.py:1070
  45.4 5.2 %collective-permute-start.2 = (f32[300,128]{1,0:T(8,128)}, f32[300,128]{1,0:T(8,128)S(1)}, u32[]{:S(2)}, u32[]{:S(2)}) collective-permute-start(f32[300,128]{1,0:T(8,128)} %get-tuple-element.22), channel_id=1, source_target_pairs={{1,0},{2,1},{3,2},{4,3},{5,4},{6,5},{7,6},{14,7},{15,14},{12,15},{... | collective-permute-start | bytes 460808 | tf_op jit(solution)/shard_map/ppermute | solution.py:1071
  47.9 2.7 %copy-start.2 = (f32[300,128]{1,0:T(8,128)}, f32[300,128]{1,0:T(8,128)S(1)}, u32[]{:S(2)}) copy-start(f32[300,128]{1,0:T(8,128)S(1)} %collective-permute-done.1.above_ref) | copy-start | bytes 460804
  50.6 0.7 copy-start.3

commit v3 on v2

--- a/solution.py
+++ b/solution.py
@@ -10,6 +10,7 @@
 VIEWS = 4
 ROWS = 40
 FEATS = 9
+STEP = 9
 LOG2E = 1.4426950408889634
 harmonic_zero = 0.28209479177387814
 harmonic_one = 0.4886025119029199
@@ -200,7 +201,7 @@
     return runs
 
 
-def compact_ints(chunk_ref, count_ref, out_ref, steps):
+def compact_ints(chunk_ref, count_ref, out_ref, steps, shift_ref, line_ref):
     lane = iota((1, 128), 1)
 
     def step(number, carry):
@@ -208,6 +209,8 @@
         live = count_ref[number]
         shift = start & 127
         row = start >> 7
+        shift_ref[number] = shift
+        line_ref[number] = row * 16
         chunk = pltpu.roll(chunk_ref[pl.ds(number, 1), :], shift, axis=1)
         held = jnp.where(lane >= shift, chunk, held)
         out_ref[pl.ds(row, 1), :] = held
@@ -217,7 +220,7 @@
     lax.fori_loop(0, steps, step, (jnp.int32(0), jnp.zeros((1, 128), jnp.int32)), unroll=16)
 
 
-def compact_feats(chunk_ref, count_of, table_ref, steps, spot=None):
+def compact_feats(chunk_ref, place_of, table_ref, steps, spot=None):
     lane = iota((8, 128), 1)
 
     def step(number, carry):
@@ -228,9 +231,7 @@
             chunk = pltpu.roll(chunk_ref[number * 6 - 2 : number * 6 + 6, :], 6, axis=0)
         else:
             chunk = chunk_ref[pl.ds(number * 6, 8), :]
-        live = count_of(number, chunk)
-        shift = start & 127
-        row = start >> 7
+        shift, line, crossed, start = place_of(number, chunk, start)
         even = pltpu.roll(chunk, (shift + 48) & 127, axis=1)
         odd = pltpu.roll(chunk, (shift + 96) & 127, axis=1)
         chunk = pltpu.roll(chunk, shift, axis=1)
@@ -238,13 +239,12 @@
         fresh = lane >= shift
         held = jnp.where(fresh, chunk, held)
         last = jnp.where(fresh, rest, last)
-        base = pl.multiple_of(row * 16, 16)
+        base = pl.multiple_of(line, 16)
         table_ref[pl.ds(base, 8), :] = held
         table_ref[pl.ds(base + 8, 8), :] = last
-        crossed = shift + live >= 128
         held = jnp.where(crossed, chunk, held)
         last = jnp.where(crossed, rest, last)
-        return start + live, held, last
+        return start, held, last
 
     zero = jnp.zeros((8, 128), F32)
     carry = lax.fori_loop(0, steps - 16, step, (jnp.int32(0), zero, zero), unroll=16)
@@ -252,34 +252,33 @@
         carry = step(number, carry)
 
 
-def expand_feats(table_ref, count_ref, out_ref, steps, spot):
+def expand_feats(table_ref, shift_ref, line_ref, out_ref, steps, spot, count_ref=None):
     lane = iota((8, 128), 1)
     sub = iota((8, 128), 0)
     even = (sub & 1) == 0
-    offset = lane - jnp.where(even, 80, 32)
-
-    def step(number, start):
-        live = count_ref[number]
-        shift = start & 127
-        base = pl.multiple_of((start >> 7) * 16, 16)
-        back = 128 - shift
-        this, rest = table_ref[pl.ds(base, 8), :], table_ref[pl.ds(base + 8, 8), :]
-        next_, next_rest = table_ref[pl.ds(base + 16, 8), :], table_ref[pl.ds(base + 24, 8), :]
-
-        def turned(value, by):
-            return pltpu.roll(value, (back + by) & 127, axis=1)
-
-        main = jnp.where(lane < back, turned(this, 0), turned(next_, 0))
-        tail = jnp.where(
-            offset < back,
-            jnp.where(even, turned(rest, 80), turned(rest, 32)),
-            jnp.where(even, turned(next_rest, 80), turned(next_rest, 32)),
+    mark = (sub == 1) & (lane == 127)
+
+    def step(number, carry):
+        back = 128 - shift_ref[number]
+        base = pl.multiple_of(line_ref[number], 16)
+        here = lane < back
+        main = jnp.where(
+            here,
+            pltpu.roll(table_ref[pl.ds(base, 8), :], back, axis=1),
+            pltpu.roll(table_ref[pl.ds(base + 16, 8), :], back, axis=1),
         )
-        tail = jnp.where((sub == 1) & (lane == 127), live.astype(F32), tail)
+        rest = jnp.where(
+            here,
+            pltpu.roll(table_ref[pl.ds(base + 8, 8), :], back, axis=1),
+            pltpu.roll(table_ref[pl.ds(base + 24, 8), :], back, axis=1),
+        )
+        tail = jnp.where(even, pltpu.roll(rest, 80, axis=1), pltpu.roll(rest, 32, axis=1))
+        if count_ref is not None:
+            tail = jnp.where(mark, count_ref[number].astype(F32), tail)
         out_ref[pl.ds(spot(number), 6), :] = jnp.where(lane < 80, main, tail)[0:6]
-        return start + live
-
-    lax.fori_loop(0, steps, step, jnp.int32(0), unroll=16)
+        return carry
+
+    lax.fori_loop(0, steps, step, 0, unroll=16)
 
 
 def line_of(feature):
@@ -358,7 +357,7 @@
 def owner_kernel(focal, centre_x, centre_y):
     def kernel(
         camera_ref, count_ref, spot_ref, params_ref, index_ref, target_ref, list_ref,
-        out_ref, place_ref, pack_ref,
+        out_ref, place_ref, pack_ref, shift_ref, line_ref,
         wide_ref, rows_ref, feats_ref, table_ref, local_ref, sems,
     ):
         copies = fetch_params(params_ref, local_ref, sems)
@@ -373,7 +372,7 @@
         wide_ref[...] = jnp.concatenate(
             [index_ref[...], jnp.zeros((128 - index_ref.shape[0], strips), jnp.int32)], 0
         ).T
-        compact_ints(wide_ref, count_ref, rows_ref, strips)
+        compact_ints(wide_ref, count_ref, rows_ref, strips, shift_ref, line_ref)
         invert(rows_ref, place_ref)
         bounds = run_bounds(count_ref, strips)
         for copy in copies:
@@ -408,16 +407,23 @@
             return carry
 
         lax.fori_loop(0, 5, gather_block, 0)
-        expand_feats(table_ref, count_ref, out_ref, strips, lambda number: spot_ref[number])
+        expand_feats(
+            table_ref, shift_ref, line_ref, out_ref, strips,
+            lambda number: spot_ref[number], count_ref,
+        )
 
     return kernel
 
 
-def entry_basis():
-    pixel = np.arange(256)
-    x = pixel % 16 - 7.5
-    y = pixel // 16 - 7.5
-    return np.stack([np.ones(256), x, y, x * x, x * y, y * y]).astype(np.float32)
+def pixel_basis(rows, times):
+    row = iota((rows, 256), 0)
+    pixel = iota((rows, 256), 1)
+    x = (pixel & 15).astype(F32) - 7.5
+    y = (pixel >> 4).astype(F32) - 7.5
+    value = jnp.where(row < 6 * times, y * y, 0.0)
+    for number, term in ((5, x * y), (4, x * x), (3, y), (2, x), (1, 1.0)):
+        value = jnp.where(row < number * times, term, value)
+    return value.astype(BF16)
 
 
 def swap_tiles(x):
@@ -450,9 +456,9 @@
 
 
 def tile_rows(ref, half, tile):
-    base = (tile >> 3) * 128 + (tile & 7)
+    base = (tile >> 3) * (16 * STEP) + (tile & 7)
     return jnp.concatenate(
-        [ref[half, pl.ds(base + turn * 640, 16, stride=8), :] for turn in range(8)], 0
+        [ref[half, pl.ds(base + turn * (80 * STEP), 16, stride=STEP), :] for turn in range(8)], 0
     )
 
 
@@ -470,9 +476,10 @@
 
 
 def render_kernel(
-    chunks_ref, basis_ref, moved_ref,
-    image_ref, first_ref, last_ref, entries_ref, colour_ref, count_ref, alphas_ref, weights_ref,
-    table_ref, order_ref, lines_ref, power_a, power_b, alpha_ref, weight_ref, tint_ref, shown_ref, sems,
+    chunks_ref, moved_ref,
+    image_ref, first_ref, last_ref, entries_ref, colour_ref, shift_ref, line_ref,
+    alpha_ref, weight_ref,
+    table_ref, order_ref, lines_ref, power_a, power_b, tint_ref, shown_ref,
 ):
     for tile in range(5):
         for channel in range(3):
@@ -482,12 +489,15 @@
             last_ref[at : at + 10, :] = moved_ref[base + 6 : base + 16, :]
     strips = chunks_ref.shape[0] // 6
 
-    def count_of(number, chunk):
+    def place_of(number, chunk, start):
         live = chunk[1, 127].astype(jnp.int32)
-        count_ref[number] = live
-        return live
-
-    compact_feats(chunks_ref, count_of, table_ref, strips)
+        shift = start & 127
+        line = (start >> 7) * 16
+        shift_ref[number] = shift
+        line_ref[number] = line
+        return shift, line, shift + live >= 128, start + live
+
+    compact_feats(chunks_ref, place_of, table_ref, strips)
     per_view = strips // VIEWS
     top = (lax.rem(position_of(strips), per_view) * 16 + 8).astype(F32)
     for group in range(5):
@@ -546,7 +556,7 @@
             piece = rounded(value)
             tint_ref[pl.ds(group * 128 + channel * 3 + part, 8, stride=16), :] = piece
             value = value - piece
-    basis = basis_ref[...]
+    basis = pixel_basis(24, 3)
 
     def powers(turn, power_ref):
         for part in range(5):
@@ -554,20 +564,6 @@
             power_ref[part * 128 : part * 128 + 128, :] = jnp.dot(
                 lines.T.astype(BF16), basis, preferred_element_type=F32
             )
-
-    def copies(turn):
-        rows = pl.ds(turn * 640, 640)
-        found = []
-        for half in range(2):
-            for slot, (near, far) in enumerate(((alpha_ref, alphas_ref), (weight_ref, weights_ref))):
-                found.append(
-                    pltpu.make_async_copy(
-                        near.at[half, rows, :],
-                        far.at[half, rows, :],
-                        sems.at[turn * 4 + slot * 2 + half],
-                    )
-                )
-        return found
 
     def scan(turn, power_ref, through):
         through = list(through)
@@ -580,7 +576,8 @@
                     weight = alpha * through[slot]
                     through[slot] = through[slot] - weight
                     alpha_ref[half, pl.ds(turn * 640 + at, 8), :] = alpha
-                    weight_ref[half, pl.ds(turn * 640 + at, 8), :] = weight
+                    spot = pl.ds(turn * (80 * STEP) + (group * 16 + entry) * STEP, 8)
+                    weight_ref[half, spot, :] = weight
         return tuple(through)
 
     def blend(pair, through):
@@ -588,9 +585,6 @@
         through = scan(2 * pair, power_a, through)
         powers(jnp.minimum(2 * pair + 2, 7), power_a)
         through = scan(2 * pair + 1, power_b, through)
-        for turn in (2 * pair, 2 * pair + 1):
-            for copy in copies(turn):
-                copy.start()
         return through
 
     powers(0, power_a)
@@ -608,7 +602,7 @@
             shown_ref[half, at, :] = total[:, half * 128 : half * 128 + 128]
         return carry
 
-    lax.fori_loop(0, ROWS, tints, 0, unroll=4)
+    lax.fori_loop(0, ROWS, tints, 0, unroll=8)
     for group in range(5):
         for channel in range(3):
             for half in range(2):
@@ -622,9 +616,6 @@
             at = (channel * 5 + group) * 10
             first_ref[at : at + 10, :] = image_ref[channel, group, 0:10, :]
             last_ref[at : at + 10, :] = image_ref[channel, group, 6:16, :]
-    for turn in range(8):
-        for copy in copies(turn):
-            copy.wait()
 
 
 def window_weights():
@@ -678,20 +669,12 @@
 
 
 def gradient_kernel(
-    count_ref, image_ref, above_ref, below_ref, moved_ref,
-    entries_ref, colour_ref, place_ref, moment_ref, alphas_ref, weights_ref,
+    shift_ref, line_ref, image_ref, above_ref, below_ref, moved_ref,
+    entries_ref, colour_ref, place_ref, alpha_ref, weight_ref,
     out_ref,
     ext_ref, square_ref, cross_ref, truth_ref, ideal_ref, rows_ref, cols_ref, parts_ref,
-    alpha_ref, weight_ref, pull_a, pull_b, light_ref, split_ref,
-    sums_ref, tint_ref, feats_ref, table_ref, sems,
+    pull_a, pull_b, light_ref, split_ref, sums_ref, tint_ref, feats_ref, table_ref,
 ):
-    copies = [
-        pltpu.make_async_copy(far.at[half], near.at[half], sems.at[slot * 2 + half])
-        for slot, (far, near) in enumerate(((alphas_ref, alpha_ref), (weights_ref, weight_ref)))
-        for half in range(2)
-    ]
-    for copy in copies:
-        copy.start()
     strips = out_ref.shape[0] // 6
     keep_above, keep_below = keeps(strips)
     def rim(base):
@@ -779,9 +762,7 @@
                     piece = rounded(value)
                     split_ref[half, pl.ds(tile * 128 + channel * 3 + part, 8, stride=16), :] = piece
                     value = value - piece
-    for copy in copies:
-        copy.wait()
-    moments = moment_ref[...]
+    moments = pixel_basis(16, 1)
 
     def scan(turn, pull_ref, behind):
         behind = list(behind)
@@ -798,6 +779,7 @@
             for group in range(5):
                 at = group * 128 + entry * 8
                 rows = pl.ds(turn * 640 + at, 8)
+                spot = pl.ds(turn * (80 * STEP) + (group * 16 + entry) * STEP, 8)
                 colour = [
                     jnp.broadcast_to(turned[group][channel][:, entry : entry + 1], (8, 128))
                     for channel in range(3)
@@ -813,7 +795,7 @@
                     delta = value - behind[slot]
                     behind[slot] = behind[slot] + alpha_ref[half, rows, :] * delta
                     pull_ref[at : at + 8, half * 128 : half * 128 + 128] = (
-                        weight_ref[half, rows, :] * delta
+                        weight_ref[half, spot, :] * delta
                     )
         return tuple(behind)
 
@@ -846,7 +828,7 @@
         tint_ref[at, :] = total
         return carry
 
-    lax.fori_loop(0, ROWS, tints, 0, unroll=4)
+    lax.fori_loop(0, ROWS, tints, 0, unroll=8)
 
     def entry_grads(block, carry):
         rows = pl.ds(block * 8, 8)
@@ -897,12 +879,13 @@
         return carry
 
     lax.fori_loop(0, 5, gather_block, 0)
-    expand_feats(table_ref, count_ref, out_ref, strips, lambda number: number * 6)
+    expand_feats(table_ref, shift_ref, line_ref, out_ref, strips, lambda number: number * 6)
 
 
 def pull_kernel(focal, centre_x, centre_y):
     def kernel(
-        camera_ref, count_ref, spot_ref, params_ref, place_ref, chunks_ref, out_ref,
+        camera_ref, count_ref, spot_ref, shift_ref, line_ref, params_ref, place_ref, chunks_ref,
+        out_ref,
         table_ref, wide_ref, local_ref, grads_ref, sems, out_sems,
     ):
         copies = fetch_params(params_ref, local_ref, sems)
@@ -910,7 +893,12 @@
         wide_ref[0 : strips * 6, :] = chunks_ref[...]
         compact_feats(
             wide_ref,
-            lambda number, chunk: count_ref[number],
+            lambda number, chunk, start: (
+                shift_ref[number],
+                line_ref[number],
+                shift_ref[number] + count_ref[number] >= 128,
+                start,
+            ),
             table_ref,
             strips,
             lambda number: spot_ref[number],
@@ -1007,11 +995,16 @@
     ahead = [(spots[i], spots[(i + 1) % strips]) for i in range(strips)]
     behind = [(spots[(i + 1) % strips], spots[i]) for i in range(strips)]
 
-    chunks, place, pack = pl.pallas_call(
+    chunks, place, pack, sent_shift, sent_line = pl.pallas_call(
         owner_kernel(focal, 0.5 * width, centre_y),
         out_shape=(
-            shape(strips * 6, 128), shape(ROWS, 128, dtype=jnp.int32), shape(280, 128)
+            shape(strips * 6, 128),
+            shape(ROWS, 128, dtype=jnp.int32),
+            shape(280, 128),
+            shape(strips, dtype=jnp.int32),
+            shape(strips, dtype=jnp.int32),
         ),
+        out_specs=(VMEM, VMEM, VMEM, SMEM, SMEM),
         in_specs=[SMEM, SMEM, SMEM, ANY, VMEM, VMEM, VMEM],
         scratch_shapes=[
             pltpu.VMEM((strips, 128), jnp.int32),
@@ -1030,16 +1023,10 @@
         invert_kernel,
         out_shape=shape(ROWS, 128, dtype=jnp.int32),
         scratch_shapes=[pltpu.VMEM((ROWS, 128), jnp.int32)],
+        compiler_params=pltpu.CompilerParams(vmem_limit_bytes=8 << 20),
         name="listed",
     )(moved)
-    rows = entry_basis()
-    basis = np.zeros((24, 256), np.float32)
-    basis[0:18] = np.repeat(rows, 3, axis=0)
-    moment = np.zeros((16, 256), np.float32)
-    moment[0:6] = rows
-    basis = jnp.asarray(basis, BF16)
-    moment = jnp.asarray(moment, BF16)
-    image, first, last, entries, colour, counts, alphas, weights = pl.pallas_call(
+    image, first, last, entries, colour, shifts, places, alphas, weights = pl.pallas_call(
         render_kernel,
         out_shape=(
             shape(3, 5, 16, 128),
@@ -1048,31 +1035,30 @@
             shape(5, ROWS, 128),
             shape(3, ROWS, 128),
             shape(strips, dtype=jnp.int32),
+            shape(strips, dtype=jnp.int32),
             shape(2, 5120, 128),
-            shape(2, 5120, 128),
+            shape(2, 640 * STEP, 128),
         ),
-        in_specs=[VMEM, VMEM, VMEM],
-        out_specs=(VMEM, VMEM, VMEM, VMEM, VMEM, SMEM, ANY, ANY),
+        in_specs=[VMEM, VMEM],
+        out_specs=(VMEM, VMEM, VMEM, VMEM, VMEM, SMEM, SMEM, VMEM, VMEM),
         scratch_shapes=[
             pltpu.VMEM(((ROWS + 2) * 16, 128), F32),
             pltpu.VMEM((ROWS, 128), jnp.int32),
             pltpu.VMEM((ROWS * 24, 128), F32),
             pltpu.VMEM((640, 256), F32),
             pltpu.VMEM((640, 256), F32),
-            pltpu.VMEM((2, 5120, 128), F32),
-            pltpu.VMEM((2, 5120, 128), F32),
             pltpu.VMEM((ROWS * 16, 128), F32),
             pltpu.VMEM((2, ROWS * 16, 128), F32),
-            pltpu.SemaphoreType.DMA((32,)),
         ],
+        compiler_params=pltpu.CompilerParams(vmem_limit_bytes=24 << 20),
         name="render",
-    )(arrived, basis, moved)
+    )(arrived, moved)
     above = lax.ppermute(last, "strip", ahead)
     below = lax.ppermute(first, "strip", behind)
     grads = pl.pallas_call(
         gradient_kernel,
         out_shape=shape(strips * 6, 128),
-        in_specs=[SMEM] + [VMEM] * 8 + [ANY, ANY],
+        in_specs=[SMEM, SMEM] + [VMEM] * 9,
         scratch_shapes=[
             pltpu.VMEM((5, 128, 128), F32),
             pltpu.VMEM((5, 128, 128), F32),
@@ -1082,8 +1068,6 @@
             pltpu.VMEM((128, 128), F32),
             pltpu.VMEM((5, 656, 128), F32),
             pltpu.VMEM((3, 656, 128), F32),
-            pltpu.VMEM((2, 5120, 128), F32),
-            pltpu.VMEM((2, 5120, 128), F32),
             pltpu.VMEM((640, 256), F32),
             pltpu.VMEM((640, 256), F32),
             pltpu.VMEM((30, 8, 128), F32),
@@ -1092,18 +1076,18 @@
             pltpu.VMEM((ROWS * 16, 128), F32),
             pltpu.VMEM((FEATS, ROWS, 128), F32),
             pltpu.VMEM(((ROWS + 2) * 16, 128), F32),
-            pltpu.SemaphoreType.DMA((4,)),
         ],
+        compiler_params=pltpu.CompilerParams(vmem_limit_bytes=24 << 20),
         name="gradient",
     )(
-        counts, image, above, below, moved,
-        entries, colour, listed, moment, alphas, weights,
+        shifts, places, image, above, below, moved,
+        entries, colour, listed, alphas, weights,
     )
     returned = exchange(grads, strips)
     return pl.pallas_call(
         pull_kernel(focal, 0.5 * width, centre_y),
         out_shape=shape(59, ROWS * 128),
-        in_specs=[SMEM, SMEM, SMEM, ANY, VMEM, VMEM],
+        in_specs=[SMEM] * 5 + [ANY, VMEM, VMEM],
         out_specs=ANY,
         scratch_shapes=[
             pltpu.VMEM(((ROWS + 2) * 16, 128), F32),
@@ -1113,8 +1097,9 @@
             pltpu.SemaphoreType.DMA((ROWS,)),
             pltpu.SemaphoreType.DMA((ROWS,)),
         ],
+        compiler_params=pltpu.CompilerParams(vmem_limit_bytes=16 << 20),
         name="pull",
-    )(camera, send_count, spot_rows, params, place, returned)
+    )(camera, send_count, spot_rows, sent_shift, sent_line, params, place, returned)
 
 
 def solution(mesh):

time: 95.2 us -> 87.5 us (0.919)
  Pallas kernels: 46.8 us -> 39.7 us
  local copies, waits for them, and re-layouts: 1.43 us -> 0.03 us
  waiting for transfers between devices: 13.3 us -> 14.6 us
    pallas_call x1, Pallas kernels: 11.8 us -> 8.35 us  [per_device(): pl.pallas_call(render_kernel, out_shape=(shape(3, 5, 16, 128), shape(300,...]
    pallas_call x1, Pallas kernels: 17.3 us -> 15.2 us  [per_device(): pl.pallas_call(gradient_kernel, out_shape=shape(strips * 6, 128), in_spec...]
    pallas_call x1, Pallas kernels: 2.13 us -> 0.61 us  [per_device(): pl.pallas_call(invert_kernel, out_shape=shape(ROWS, 128, dtype=jnp.int32)...]
    unnamed x8 -> x14, local copies, waits for them, and re-layouts: 1.43 us -> 0.03 us
    ppermute x1, waiting for transfers between devices: 0.04 us -> 1.24 us  [per_device(): above = lax.ppermute(last, 'strip', ahead)]
  transfers between devices with their start and end apart: 4 -> 4, of which waited for: 2 -> 3; matrix products, arithmetic and copies ran while one was open for 0% -> 0% of each run, Pallas kernels for 2% -> 1%
where the time goes in v3:
time: 87.5 us; the launch traced here: 87.3 us
  Pallas kernels  39.7 us (45%)
  blocking collectives  18.4 us (21%)
  waiting for transfers between devices  14.6 us (17%)
  starting transfers between devices  14.5 us (17%)
    all_to_all x1, blocking collectives, exchange(): got = lax.all_to_all(sent, 'strip', split_axis=0, concat_axis=0, tiled=True)  18.4 us
    pallas_call x1, Pallas kernels, per_device(): pl.pallas_call(gradient_kernel, out_shape=shape(strips * 6, 128), in_spec...  15.2 us
    all_to_all x1, starting transfers between devices, exchange(): got = lax.all_to_all(sent, 'strip', split_axis=0, concat_axis=0, tiled=True)  11.5 us
    all_to_all x1, waiting for transfers between devices, exchange(): got = lax.all_to_all(sent, 'strip', split_axis=0, concat_axis=0, tiled=True)  10.6 us
    pallas_call x1, Pallas kernels, per_device(): pl.pallas_call(owner_kernel(focal, 0.5 * width, centre_y), out_shape=(sha...  8.49 us
    pallas_call x1, Pallas kernels, per_device(): pl.pallas_call(render_kernel, out_shape=(shape(3, 5, 16, 128), shape(300,...  8.35 us
    pallas_call x1, Pallas kernels, per_device(): pl.pallas_call(pull_kernel(focal, 0.5 * width, centre_y), out_shape=shape...  7.06 us
    ppermute x1, waiting for transfers between devices, per_device(): below = lax.ppermute(first, 'strip', behind)  2.77 us
  transfers between devices with their start and end apart: 4, of which 3 were waited for; matrix products, arithmetic and copies ran while one was open for 0% of the time, Pallas kernels for 1%

profile of v3, /device:TPU:1, one launch (start us, length us, event | category | flops | bytes accessed | tf_op | source)
XLA Modules:
  0.0 87.3 jit_solution(15166847831145780834)
XLA Ops:
  0.0 8.5 %owner.1 = (f32[768,128]{1,0:T(8,128)}, s32[40,128]{1,0:T(8,128)}, f32[280,128]{1,0:T(8,128)}, s32[128]{0:T(128)}, s32[128]{0:T(128)}) custom-call(f32[4,12]{1,0:T(4,128)} %camera_ref.3, s32[128]{0:T(128)} %count_ref.3, s32[128]{0:T(128)} %constant.2.clone.spot_ref, f32[59,5120]{1,0:T(8,128)} %params_ref.3, s32[80,128]{1,0:T(8,128)} %bitcast.9, ...), custom_call_target="tpu_custom_call" | custom-call | tf_op jit(solution)/shard_map/owner/pallas_call | solution.py:998
  8.5 11.5 %all-to-all-start = ((f32[128,1,768]{2,1,0:T(1,128)}), f32[128,1,768]{2,1,0:T(1,128)S(1)}, u32[]{:S(2)}, u32[]{:S(2)}) async-start(f32[128,1,768]{2,1,0:T(1,128)} %bitcast.8), calls=%async_computation | async-start | bytes 786432 | tf_op jit(solution)/shard_map/all_to_all | solution.py:982
  20.0 1.6 %collective-permute-start = (f32[280,128]{1,0:T(8,128)}, f32[280,128]{1,0:T(8,128)S(1)}, u32[]{:S(2)}, u32[]{:S(2)}) collective-permute-start(f32[280,128]{1,0:T(8,128)} %get-tuple-element.23), channel_id=1, source_target_pairs={{0,0},{1,1},{2,2},{3,3},{4,4},{5,5},{6,6},{7,7},{8,14},{9,15},{10,... | collective-permute-start | bytes 430088 | tf_op jit(solution)/shard_map/ppermute | solution.py:1020
  21.6 0.0 collective-permute-done.moved_ref
  21.6 10.6 %all-to-all-done = f32[128,1,768]{2,1,0:T(1,128)S(1)} async-done(((f32[128,1,768]{2,1,0:T(1,128)}), f32[128,1,768]{2,1,0:T(1,128)S(1)}, u32[]{:S(2)}, u32[]{:S(2)}) %all-to-all-start) | async-done | bytes 393248 | tf_op jit(solution)/shard_map/all_to_all | solution.py:982
  32.1 8.3 %render.1 = (f32[3,5,16,128]{3,2,1,0:T(8,128)S(1)}, f32[300,128]{1,0:T(8,128)S(1)}, f32[300,128]{1,0:T(8,128)S(1)}, f32[5,40,128]{2,1,0:T(8,128)S(1)}, f32[3,40,...) custom-call(f32[768,128]{1,0:T(8,128)S(1)} %bitcast.6, ...), custom_call_target="tpu_custom_call" | custom-call | tf_op jit(solution)/shard_map/render/pallas_call | solution.py:1029
  40.5 1.1 %collective-permute-start.1 = (f32[300,128]{1,0:T(8,128)S(1)}, f32[300,128]{1,0:T(8,128)S(1)}, u32[]{:S(2)}, u32[]{:S(2)}) collective-permute-start(f32[300,128]{1,0:T(8,128)S(1)} %get-tuple-element.27), channel_id=1, source_target_pairs={{0,1},{1,2},{2,3},{3,4},{4,5},{5,6},{6,7},{7,14},{14,15},{15,12},{... | collective-permute-start | bytes 460808 | tf_op jit(solution)/shard_map/ppermute | solution.py:1056
  41.6 0.3 collective-permute-start.2
  41.9 0.6 listed.1.place_ref
  42.5 1.2 %collective-permute-done.1.above_ref = f32[300,128]{1,0:T(8,128)S(1)} collective-permute-done((f32[300,128]{1,0:T(8,128)S(1)}, f32[300,128]{1,0:T(8,128)S(1)}, u32[]{:S(2)}, u32[]{:S(2)}) %collective-permute-start.1) | collective-permute-done | bytes 153632 | tf_op jit(solution)/shard_map/ppermute | solution.py:1056
  43.8 2.8 %collective-permute-done.2.below_ref = f32[300,128]{1,0:T(8,128)S(1)} collective-permute-done((f32[300,128]{1,0:T(8,128)S(1)}, f32[300,128]{1,0:T(8,128)S(1)}, u32[]{:S(2)}, u32[]{:S(2)}) %collective-permute-start.2) | collective-permute-done | bytes 153632 | tf_op jit(solution)/shard_map/ppermute | solution.py:1057
  46.5 0.0 copy-start
  46.5 0.0 copy-start.1
  46.5 0.0 copy-start.2
  46.5 0.0 copy-start.3
  46.5 0.0 copy-start.4
  46.6 0.0 copy-start.5
  46.6 0.0 copy-start.6
  46.6 15.2 %gradient.1 = f32[768,128]{1,0:T(8,128)S(1)} custom-call(s32[128]{0:T(128)S(1)} %get-tuple-element.24.shift_ref, s32[128]{0:T(128)S(1)} %get-tuple-element.25.line_ref, f32[3,5,16,128]{3,2,1,0:T(8,128)S(1)} %get-tuple-element.26.image_ref, f32[300,128]{1,0:T(8,128)S(1)} %collective-permute-done.1.above_ref, f32[300,128]{1,0:T(8,128)S(1)} %collective-permute-done.2.below_ref, ...), custom_call_target="tpu_custom_call" | custom-call | tf_op jit(solution)/shard_map/gradient/pallas_call | solution.py:1058
  61.8 18.4 %all_to_all.10 = f32[128,1,768]{2,1,0:T(1,128)S(1)} all-to-all(f32[128,1,768]{2,1,0:T(1,128)S(1)} %bitcast.5), channel_id=1, replica_groups=mesh['strip'=128] {'strip'}, dimensions={0} | all-to-all | bytes 786432 | tf_op jit(solution)/shard_map/all_to_all | solution.py:982
  80.1 0.0 copy-done
  80.1 0.0 copy-done.1
  80.1 0.0 copy-done.2
  80.1 0.0 copy-done.3
  80.2 0.0 copy-done.4
  80.2 0.0 copy-done.5
  80.2 0.0 copy-done.6
  80.2 7.1 %pull.1 = f32[59,5120]{1,0:T(8,128)} custom-call(f32[4,12]{1,0:T(4,128)S(1)} %copy-done.2, s32[128]{0:T(128)S(1)} %copy-done.3, s32[128]{0:T(128)S(1)} %copy-done.4, s32[128]{0:T(128)S(1)} %copy-done.5, s32[128]{0:T(128)S(1)} %copy-done.6, f32[59,5120]{1,0:T(8,128)S(1)} %copy-done, s32[40,128]{1,0:T(8,128)S(1)} %copy-done.1, f32[768,128]{1,0:T(8,128)S(1)} %bitcast.7), custom_call_target="tpu_custom_call" | custom-call | tf_op jit(solution)/shard_map/pull/pallas_call | solution.py:1087
Async XLA Ops:
  8.5 23.6 %all-to-all-start = ((f32[128,1,768]{2,1,0:T(1,128)}), f32[128,1,768]{2,1,0:T(1,128)S(1)}, u32[]{:S(2)}, u32[]{:S(2)}) async-start(f32[128,1,768]{2,1,0:T(1,128)} %bitcast.8), calls=%async_computation | async-start | bytes 786432 | tf_op jit(solution)/shard_map/all_to_all | solution.py:982
  20.0 1.6 %collective-permute-start = (f32[280,128]{1,0:T(8,128)}, f32[280,128]{1,0:T(8,128)S(1)}, u32[]{:S(2)}, u32[]{:S(2)}) collective-permute-start(f32[280,128]{1,0:T(8,128)} %get-tuple-element.23), channel_id=1, source_target_pairs={{0,0},{1,1},{2,2},{3,3},{4,4},{5,5},{6,6},{7,7},{8,14},{9,15},{10,... | collective-permute-start | bytes 430088 | tf_op jit(solution)/shard_map/ppermute | solution.py:1020
  40.5 3.3 %collective-permute-start.1 = (f32[300,128]{1,0:T(8,128)S(1)}, f32[300,128]{1,0:T(8,128)S(1)}, u32[]{:S(2)}, u32[]{:S(2)}) collective-permute-start(f32[300,128]{1,0:T(8,128)S(1)} %get-tuple-element.27), channel_id=1, source_target_pairs={{0,1},{1,2},{2,3},{3,4},{4,5},{5,6},{6,7},{7,14},{14,15},{15,12},{... | collective-permute-start | bytes 460808 | tf_op jit(solution)/shard_map/ppermute | solution.py:1056
  41.6 5.0 %collective-permute-start.2 = (f32[300,128]{1,0:T(8,128)S(1)}, f32[300,128]{1,0:T(8,128)S(1)}, u32[]{:S(2)}, u32[]{:S(2)}) collective-permute-start(f32[300,128]{1,0:T(8,128)S(1)} %get-tuple-element.28), channel_id=1, source_target_pairs={{1,0},{2,1},{3,2},{4,3},{5,4},{6,5},{7,6},{14,7},{15,14},{12,15},{... | collective-permute-start | bytes 460808 | tf_op jit(solution)/shard_map/ppermute | solution.py:1057
  46.5 33.6 %copy-start = (f32[59,5120]{1,0:T(8,128)S(1)}, f32[59,5120]{1,0:T(8,128)}, u32[]{:S(2)}) copy-start(f32[59,5120]{1,0:T(8,128)} %params_ref.3) | copy-start | bytes 3624964
  46.5 33.6 %copy-start.1 = (s32[40,128]{1,0:T(8,128)S(1)}, s32[40,128]{1,0:T(8,128)}, u32[]{:S(2)}) copy-start(s32[40,128]{1,0:T(8,128)} %get-tuple-element.21.place_ref) | copy-start | bytes 61444
  46.5 33.6 %copy-start.2 = (f32[4,12]{1,0:T(4,128)S(1)}, f32[4,12]{1,0:T(4,128)}, u32[]{:S(2)}) copy-start(f32[4,12]{1,0:T(4,128)} %camera_ref.3) | copy-start | bytes 580
  46.5 33.6 %copy-start.3 = (s32[128]{0:T(128)S(1)}, s32[128]{0:T(128)}, u32[]{:S(2)}) copy-start(s32[128]{0:T(128)} %count_ref.3) | copy-start | bytes 1540
  46.5 33.6 %copy-start.4 = (s32[128]{0:T(128)S(1)}, s32[128]{0:T(128)}, u32[]{:S(2)}) copy-start(s32[128]{0:T(128)} %constant.2.clone.spot_ref) | copy-start | bytes 1540
  46.6 33.6 %copy-start.5 = (s32[128]{0:T(128)S(1)}, s32[128]{0:T(128)}, u32[]{:S(2)}) copy-start(s32[128]{0:T(128)} %get-tuple-element.19.shift_ref) | copy-start | bytes 1540
  46.6 33.6 %copy-start.6 = (s32[128]{0:T(128)S(1)}, s32[128]{0:T(128)}, u32[]{:S(2)}) copy-start(s32[128]{0:T(128)} %get-tuple-element.20.line_ref) | copy-start | bytes 1540

commit v4 on v3

--- a/solution.py
+++ b/solution.py
@@ -10,6 +10,8 @@
 VIEWS = 4
 ROWS = 40
 FEATS = 9
+GAP = 24
+PLACE = 72
 STEP = 9
 LOG2E = 1.4426950408889634
 harmonic_zero = 0.28209479177387814
@@ -201,7 +203,7 @@
     return runs
 
 
-def compact_ints(chunk_ref, count_ref, out_ref, steps, shift_ref, line_ref):
+def compact_ints(chunk_ref, count_ref, out_ref, steps):
     lane = iota((1, 128), 1)
 
     def step(number, carry):
@@ -209,8 +211,6 @@
         live = count_ref[number]
         shift = start & 127
         row = start >> 7
-        shift_ref[number] = shift
-        line_ref[number] = row * 16
         chunk = pltpu.roll(chunk_ref[pl.ds(number, 1), :], shift, axis=1)
         held = jnp.where(lane >= shift, chunk, held)
         out_ref[pl.ds(row, 1), :] = held
@@ -239,7 +239,7 @@
         fresh = lane >= shift
         held = jnp.where(fresh, chunk, held)
         last = jnp.where(fresh, rest, last)
-        base = pl.multiple_of(line, 16)
+        base = pl.multiple_of(line, 8)
         table_ref[pl.ds(base, 8), :] = held
         table_ref[pl.ds(base + 8, 8), :] = last
         held = jnp.where(crossed, chunk, held)
@@ -252,33 +252,34 @@
         carry = step(number, carry)
 
 
-def expand_feats(table_ref, shift_ref, line_ref, out_ref, steps, spot, count_ref=None):
+def expand_feats(table_ref, place_of, out_ref, steps, spot, count_ref=None):
     lane = iota((8, 128), 1)
     sub = iota((8, 128), 0)
     even = (sub & 1) == 0
     mark = (sub == 1) & (lane == 127)
 
-    def step(number, carry):
-        back = 128 - shift_ref[number]
-        base = pl.multiple_of(line_ref[number], 16)
+    def step(number, start):
+        shift, line, start = place_of(number, start)
+        back = 128 - shift
+        base = pl.multiple_of(line, 8)
         here = lane < back
         main = jnp.where(
             here,
             pltpu.roll(table_ref[pl.ds(base, 8), :], back, axis=1),
-            pltpu.roll(table_ref[pl.ds(base + 16, 8), :], back, axis=1),
+            pltpu.roll(table_ref[pl.ds(base + GAP, 8), :], back, axis=1),
         )
         rest = jnp.where(
             here,
             pltpu.roll(table_ref[pl.ds(base + 8, 8), :], back, axis=1),
-            pltpu.roll(table_ref[pl.ds(base + 24, 8), :], back, axis=1),
+            pltpu.roll(table_ref[pl.ds(base + GAP + 8, 8), :], back, axis=1),
         )
         tail = jnp.where(even, pltpu.roll(rest, 80, axis=1), pltpu.roll(rest, 32, axis=1))
         if count_ref is not None:
             tail = jnp.where(mark, count_ref[number].astype(F32), tail)
         out_ref[pl.ds(spot(number), 6), :] = jnp.where(lane < 80, main, tail)[0:6]
-        return carry
-
-    lax.fori_loop(0, steps, step, 0, unroll=16)
+        return start
+
+    lax.fori_loop(0, steps, step, jnp.int32(0), unroll=16)
 
 
 def line_of(feature):
@@ -287,13 +288,13 @@
 
 def put_feature(table_ref, block, feature, value):
     line = line_of(feature)
-    table_ref[pl.ds(block * 128 + line, 8, stride=16), :] = value
+    table_ref[pl.ds(block * (8 * GAP) + line, 8, stride=GAP), :] = value
     if feature >= 6:
-        table_ref[pl.ds(block * 128 + line + 1, 8, stride=16), :] = value
+        table_ref[pl.ds(block * (8 * GAP) + line + 1, 8, stride=GAP), :] = value
 
 
 def table_line(table_ref, row, feature):
-    line = row * 16 + line_of(feature)
+    line = row * GAP + line_of(feature)
     return table_ref[line : line + 1, :]
 
 
@@ -301,7 +302,7 @@
     copies = [
         pltpu.make_async_copy(
             params_ref.at[:, pl.ds(tile * 128, 128)],
-            local_ref.at[pl.ds(tile * 64, 59), :],
+            local_ref.at[pl.ds(tile * PLACE, 59), :],
             sems.at[tile],
         )
         for tile in range(ROWS)
@@ -357,7 +358,7 @@
 def owner_kernel(focal, centre_x, centre_y):
     def kernel(
         camera_ref, count_ref, spot_ref, params_ref, index_ref, target_ref, list_ref,
-        out_ref, place_ref, pack_ref, shift_ref, line_ref,
+        out_ref, place_ref, pack_ref,
         wide_ref, rows_ref, feats_ref, table_ref, local_ref, sems,
     ):
         copies = fetch_params(params_ref, local_ref, sems)
@@ -372,7 +373,7 @@
         wide_ref[...] = jnp.concatenate(
             [index_ref[...], jnp.zeros((128 - index_ref.shape[0], strips), jnp.int32)], 0
         ).T
-        compact_ints(wide_ref, count_ref, rows_ref, strips, shift_ref, line_ref)
+        compact_ints(wide_ref, count_ref, rows_ref, strips)
         invert(rows_ref, place_ref)
         bounds = run_bounds(count_ref, strips)
         for copy in copies:
@@ -382,7 +383,8 @@
             rows = pl.ds(block * 8, 8)
             camera = select_camera(camera_ref, place_ref[rows, :], bounds)
             params = [
-                local_ref[pl.ds(block * 512 + number, 8, stride=64), :] for number in range(59)
+                local_ref[pl.ds(block * (8 * PLACE) + number, 8, stride=PLACE), :]
+                for number in range(59)
             ]
             feats = project(params, camera, focal, centre_x, centre_y)
             feats.append(log_sigmoid(params[10]))
@@ -408,8 +410,12 @@
 
         lax.fori_loop(0, 5, gather_block, 0)
         expand_feats(
-            table_ref, shift_ref, line_ref, out_ref, strips,
-            lambda number: spot_ref[number], count_ref,
+            table_ref,
+            lambda number, start: (start & 127, (start >> 7) * GAP, start + count_ref[number]),
+            out_ref,
+            strips,
+            lambda number: spot_ref[number],
+            count_ref,
         )
 
     return kernel
@@ -492,7 +498,7 @@
     def place_of(number, chunk, start):
         live = chunk[1, 127].astype(jnp.int32)
         shift = start & 127
-        line = (start >> 7) * 16
+        line = (start >> 7) * GAP
         shift_ref[number] = shift
         line_ref[number] = line
         return shift, line, shift + live >= 128, start + live
@@ -554,7 +560,7 @@
         colour_ref[channel, group * 8 : group * 8 + 8, :] = value
         for part in range(3):
             piece = rounded(value)
-            tint_ref[pl.ds(group * 128 + channel * 3 + part, 8, stride=16), :] = piece
+            tint_ref[pl.ds(group * (8 * GAP) + channel * 3 + part, 8, stride=GAP), :] = piece
             value = value - piece
     basis = pixel_basis(24, 3)
 
@@ -591,7 +597,7 @@
     lax.fori_loop(0, 4, blend, (jnp.ones((8, 128), F32),) * 10)
 
     def tints(tile, carry):
-        at = pl.ds(pl.multiple_of(tile * 16, 16), 16)
+        at = pl.ds(pl.multiple_of(tile * GAP, 8), 16)
         tint = tint_ref[at, :].astype(BF16)
         halves = [coarse_fine(tile_rows(weight_ref, half, tile)) for half in range(2)]
         weight = jnp.concatenate(
@@ -607,7 +613,7 @@
         for channel in range(3):
             for half in range(2):
                 parts = [
-                    shown_ref[half, pl.ds(group * 128 + channel * 3 + part, 8, stride=16), :]
+                    shown_ref[half, pl.ds(group * (8 * GAP) + channel * 3 + part, 8, stride=GAP), :]
                     for part in range(3)
                 ]
                 image_ref[channel, group, half * 8 : half * 8 + 8, :] = swap_tiles(
@@ -760,7 +766,7 @@
                 light_ref[tile * 6 + half * 3 + channel] = value
                 for part in range(3):
                     piece = rounded(value)
-                    split_ref[half, pl.ds(tile * 128 + channel * 3 + part, 8, stride=16), :] = piece
+                    split_ref[half, pl.ds(tile * (8 * GAP) + channel * 3 + part, 8, stride=GAP), :] = piece
                     value = value - piece
     moments = pixel_basis(16, 1)
 
@@ -817,7 +823,7 @@
     reduce(0, pull_b)
 
     def tints(tile, carry):
-        at = pl.ds(pl.multiple_of(tile * 16, 16), 16)
+        at = pl.ds(pl.multiple_of(tile * GAP, 8), 16)
         halves = [coarse_fine(tile_rows(weight_ref, half, tile)) for half in range(2)]
         weight = jnp.concatenate(
             [jnp.concatenate([halves[0][part], halves[1][part]], 1) for part in range(2)], 0
@@ -846,9 +852,9 @@
         feats_ref[8, rows, :] = zeroth
         for channel in range(3):
             feats_ref[5 + channel, rows, :] = (
-                tint_ref[pl.ds(block * 128 + channel * 3, 8, stride=16), :]
-                + tint_ref[pl.ds(block * 128 + channel * 3 + 1, 8, stride=16), :]
-                + tint_ref[pl.ds(block * 128 + channel * 3 + 2, 8, stride=16), :]
+                tint_ref[pl.ds(block * (8 * GAP) + channel * 3, 8, stride=GAP), :]
+                + tint_ref[pl.ds(block * (8 * GAP) + channel * 3 + 1, 8, stride=GAP), :]
+                + tint_ref[pl.ds(block * (8 * GAP) + channel * 3 + 2, 8, stride=GAP), :]
             )
         return carry
 
@@ -879,13 +885,18 @@
         return carry
 
     lax.fori_loop(0, 5, gather_block, 0)
-    expand_feats(table_ref, shift_ref, line_ref, out_ref, strips, lambda number: number * 6)
+    expand_feats(
+        table_ref,
+        lambda number, start: (shift_ref[number], line_ref[number], start),
+        out_ref,
+        strips,
+        lambda number: number * 6,
+    )
 
 
 def pull_kernel(focal, centre_x, centre_y):
     def kernel(
-        camera_ref, count_ref, spot_ref, shift_ref, line_ref, params_ref, place_ref, chunks_ref,
-        out_ref,
+        camera_ref, count_ref, spot_ref, params_ref, place_ref, chunks_ref, out_ref,
         table_ref, wide_ref, local_ref, grads_ref, sems, out_sems,
     ):
         copies = fetch_params(params_ref, local_ref, sems)
@@ -894,10 +905,10 @@
         compact_feats(
             wide_ref,
             lambda number, chunk, start: (
-                shift_ref[number],
-                line_ref[number],
-                shift_ref[number] + count_ref[number] >= 128,
-                start,
+                start & 127,
+                (start >> 7) * GAP,
+                (start & 127) + count_ref[number] >= 128,
+                start + count_ref[number],
             ),
             table_ref,
             strips,
@@ -918,7 +929,8 @@
                     got[feature] = jnp.where(same, value, got[feature])
             camera = select_camera(camera_ref, place, bounds)
             params = [
-                local_ref[pl.ds(block * 512 + number, 8, stride=64), :] for number in range(59)
+                local_ref[pl.ds(block * (8 * PLACE) + number, 8, stride=PLACE), :]
+                for number in range(59)
             ]
             ignored, pull = jax.vjp(
                 lambda values: project(values, camera, focal, centre_x, centre_y), params
@@ -926,14 +938,14 @@
             for number, grad in enumerate(pull(got[:8])[0]):
                 if number == 10:
                     grad = got[8] / (1.0 + jnp.exp(params[10]))
-                grads_ref[pl.ds(block * 512 + number, 8, stride=64), :] = grad
+                grads_ref[pl.ds(block * (8 * PLACE) + number, 8, stride=PLACE), :] = grad
             for tile in range(8):
                 result(block * 8 + tile).start()
             return carry
 
         def result(tile):
             return pltpu.make_async_copy(
-                grads_ref.at[pl.ds(pl.multiple_of(tile * 64, 64), 59), :],
+                grads_ref.at[pl.ds(pl.multiple_of(tile * PLACE, 8), 59), :],
                 out_ref.at[:, pl.ds(pl.multiple_of(tile * 128, 128), 128)],
                 out_sems.at[tile],
             )
@@ -995,23 +1007,20 @@
     ahead = [(spots[i], spots[(i + 1) % strips]) for i in range(strips)]
     behind = [(spots[(i + 1) % strips], spots[i]) for i in range(strips)]
 
-    chunks, place, pack, sent_shift, sent_line = pl.pallas_call(
+    chunks, place, pack = pl.pallas_call(
         owner_kernel(focal, 0.5 * width, centre_y),
         out_shape=(
             shape(strips * 6, 128),
             shape(ROWS, 128, dtype=jnp.int32),
             shape(280, 128),
-            shape(strips, dtype=jnp.int32),
-            shape(strips, dtype=jnp.int32),
         ),
-        out_specs=(VMEM, VMEM, VMEM, SMEM, SMEM),
         in_specs=[SMEM, SMEM, SMEM, ANY, VMEM, VMEM, VMEM],
         scratch_shapes=[
             pltpu.VMEM((strips, 128), jnp.int32),
             pltpu.VMEM((ROWS + 8, 128), jnp.int32),
             pltpu.VMEM((FEATS, ROWS, 128), F32),
-            pltpu.VMEM(((ROWS + 2) * 16, 128), F32),
-            pltpu.VMEM((ROWS * 64, 128), F32),
+            pltpu.VMEM(((ROWS + 2) * GAP, 128), F32),
+            pltpu.VMEM((ROWS * PLACE, 128), F32),
             pltpu.SemaphoreType.DMA((ROWS,)),
         ],
         name="owner",
@@ -1042,13 +1051,13 @@
         in_specs=[VMEM, VMEM],
         out_specs=(VMEM, VMEM, VMEM, VMEM, VMEM, SMEM, SMEM, VMEM, VMEM),
         scratch_shapes=[
-            pltpu.VMEM(((ROWS + 2) * 16, 128), F32),
+            pltpu.VMEM(((ROWS + 2) * GAP, 128), F32),
             pltpu.VMEM((ROWS, 128), jnp.int32),
             pltpu.VMEM((ROWS * 24, 128), F32),
             pltpu.VMEM((640, 256), F32),
             pltpu.VMEM((640, 256), F32),
-            pltpu.VMEM((ROWS * 16, 128), F32),
-            pltpu.VMEM((2, ROWS * 16, 128), F32),
+            pltpu.VMEM((ROWS * GAP, 128), F32),
+            pltpu.VMEM((2, ROWS * GAP, 128), F32),
         ],
         compiler_params=pltpu.CompilerParams(vmem_limit_bytes=24 << 20),
         name="render",
@@ -1071,11 +1080,11 @@
             pltpu.VMEM((640, 256), F32),
             pltpu.VMEM((640, 256), F32),
             pltpu.VMEM((30, 8, 128), F32),
-            pltpu.VMEM((2, ROWS * 16, 128), F32),
+            pltpu.VMEM((2, ROWS * GAP, 128), F32),
             pltpu.VMEM((ROWS * 8 + 40, 128), F32),
-            pltpu.VMEM((ROWS * 16, 128), F32),
+            pltpu.VMEM((ROWS * GAP, 128), F32),
             pltpu.VMEM((FEATS, ROWS, 128), F32),
-            pltpu.VMEM(((ROWS + 2) * 16, 128), F32),
+            pltpu.VMEM(((ROWS + 2) * GAP, 128), F32),
         ],
         compiler_params=pltpu.CompilerParams(vmem_limit_bytes=24 << 20),
         name="gradient",
@@ -1087,19 +1096,19 @@
     return pl.pallas_call(
         pull_kernel(focal, 0.5 * width, centre_y),
         out_shape=shape(59, ROWS * 128),
-        in_specs=[SMEM] * 5 + [ANY, VMEM, VMEM],
+        in_specs=[SMEM] * 3 + [ANY, VMEM, VMEM],
         out_specs=ANY,
         scratch_shapes=[
-            pltpu.VMEM(((ROWS + 2) * 16, 128), F32),
+            pltpu.VMEM(((ROWS + 2) * GAP, 128), F32),
             pltpu.VMEM((strips * 6 + 8, 128), F32),
-            pltpu.VMEM((ROWS * 64, 128), F32),
-            pltpu.VMEM((ROWS * 64, 128), F32),
+            pltpu.VMEM((ROWS * PLACE, 128), F32),
+            pltpu.VMEM((ROWS * PLACE, 128), F32),
             pltpu.SemaphoreType.DMA((ROWS,)),
             pltpu.SemaphoreType.DMA((ROWS,)),
         ],
         compiler_params=pltpu.CompilerParams(vmem_limit_bytes=16 << 20),
         name="pull",
-    )(camera, send_count, spot_rows, sent_shift, sent_line, params, place, returned)
+    )(camera, send_count, spot_rows, params, place, returned)
 
 
 def solution(mesh):

time: 87.5 us -> 85.7 us (0.979)
  Pallas kernels: 39.7 us -> 38 us
    pallas_call x1, Pallas kernels: 7.06 us -> 6.15 us  [per_device(): pl.pallas_call(pull_kernel(focal, 0.5 * width, centre_y), out_shape=shape...]
where the time goes in v4:
time: 85.7 us; the launch traced here: 85.5 us
  Pallas kernels  38 us (44%)
  blocking collectives  18.4 us (21%)
  waiting for transfers between devices  14.6 us (17%)
  starting transfers between devices  14.5 us (17%)
    all_to_all x1, blocking collectives, exchange(): got = lax.all_to_all(sent, 'strip', split_axis=0, concat_axis=0, tiled=True)  18.4 us
    pallas_call x1, Pallas kernels, per_device(): pl.pallas_call(gradient_kernel, out_shape=shape(strips * 6, 128), in_spec...  15.1 us
    all_to_all x1, starting transfers between devices, exchange(): got = lax.all_to_all(sent, 'strip', split_axis=0, concat_axis=0, tiled=True)  11.5 us
    all_to_all x1, waiting for transfers between devices, exchange(): got = lax.all_to_all(sent, 'strip', split_axis=0, concat_axis=0, tiled=True)  10.6 us
    pallas_call x1, Pallas kernels, per_device(): pl.pallas_call(render_kernel, out_shape=(shape(3, 5, 16, 128), shape(300,...  8.36 us
    pallas_call x1, Pallas kernels, per_device(): pl.pallas_call(owner_kernel(focal, 0.5 * width, centre_y), out_shape=(sha...  7.78 us
    pallas_call x1, Pallas kernels, per_device(): pl.pallas_call(pull_kernel(focal, 0.5 * width, centre_y), out_shape=shape...  6.15 us
    ppermute x1, waiting for transfers between devices, per_device(): below = lax.ppermute(first, 'strip', behind)  2.77 us
  transfers between devices with their start and end apart: 4, of which 3 were waited for; matrix products, arithmetic and copies ran while one was open for 0% of the time, Pallas kernels for 1%

profile of v4, /device:TPU:1, one launch (start us, length us, event | category | flops | bytes accessed | tf_op | source)
XLA Modules:
  0.0 85.5 jit_solution(3411634972514170848)
XLA Ops:
  0.0 7.8 %owner.1 = (f32[768,128]{1,0:T(8,128)}, s32[40,128]{1,0:T(8,128)}, f32[280,128]{1,0:T(8,128)}) custom-call(f32[4,12]{1,0:T(4,128)} %camera_ref.3, s32[128]{0:T(128)} %count_ref.3, s32[128]{0:T(128)} %constant.2.clone.spot_ref, f32[59,5120]{1,0:T(8,128)} %params_ref.3, s32[80,128]{1,0:T(8,128)} %bitcast.9, f32[3,16,640]{2,1,0:T(8,128)} %target_ref.1, ...), custom_call_target="tpu_custom_call" | custom-call | tf_op jit(solution)/shard_map/owner/pallas_call | solution.py:1010
  7.8 11.5 %all-to-all-start = ((f32[128,1,768]{2,1,0:T(1,128)}), f32[128,1,768]{2,1,0:T(1,128)S(1)}, u32[]{:S(2)}, u32[]{:S(2)}) async-start(f32[128,1,768]{2,1,0:T(1,128)} %bitcast.8), calls=%async_computation | async-start | bytes 786432 | tf_op jit(solution)/shard_map/all_to_all | solution.py:994
  19.3 1.6 %collective-permute-start = (f32[280,128]{1,0:T(8,128)}, f32[280,128]{1,0:T(8,128)S(1)}, u32[]{:S(2)}, u32[]{:S(2)}) collective-permute-start(f32[280,128]{1,0:T(8,128)} %get-tuple-element.19), channel_id=1, source_target_pairs={{0,0},{1,1},{2,2},{3,3},{4,4},{5,5},{6,6},{7,7},{8,14},{9,15},{10,... | collective-permute-start | bytes 430088 | tf_op jit(solution)/shard_map/ppermute | solution.py:1029
  20.9 0.0 collective-permute-done.moved_ref
  20.9 10.6 %all-to-all-done = f32[128,1,768]{2,1,0:T(1,128)S(1)} async-done(((f32[128,1,768]{2,1,0:T(1,128)}), f32[128,1,768]{2,1,0:T(1,128)S(1)}, u32[]{:S(2)}, u32[]{:S(2)}) %all-to-all-start) | async-done | bytes 393248 | tf_op jit(solution)/shard_map/all_to_all | solution.py:994
  31.4 8.4 %render.1 = (f32[3,5,16,128]{3,2,1,0:T(8,128)S(1)}, f32[300,128]{1,0:T(8,128)S(1)}, f32[300,128]{1,0:T(8,128)S(1)}, f32[5,40,128]{2,1,0:T(8,128)S(1)}, f32[3,40,...) custom-call(f32[768,128]{1,0:T(8,128)S(1)} %bitcast.6, ...), custom_call_target="tpu_custom_call" | custom-call | tf_op jit(solution)/shard_map/render/pallas_call | solution.py:1038
  39.8 1.1 %collective-permute-start.1 = (f32[300,128]{1,0:T(8,128)S(1)}, f32[300,128]{1,0:T(8,128)S(1)}, u32[]{:S(2)}, u32[]{:S(2)}) collective-permute-start(f32[300,128]{1,0:T(8,128)S(1)} %get-tuple-element.23), channel_id=1, source_target_pairs={{0,1},{1,2},{2,3},{3,4},{4,5},{5,6},{6,7},{7,14},{14,15},{15,12},{... | collective-permute-start | bytes 460808 | tf_op jit(solution)/shard_map/ppermute | solution.py:1065
  40.9 0.3 collective-permute-start.2
  41.2 0.6 listed.1.place_ref
  41.8 1.2 %collective-permute-done.1.above_ref = f32[300,128]{1,0:T(8,128)S(1)} collective-permute-done((f32[300,128]{1,0:T(8,128)S(1)}, f32[300,128]{1,0:T(8,128)S(1)}, u32[]{:S(2)}, u32[]{:S(2)}) %collective-permute-start.1) | collective-permute-done | bytes 153632 | tf_op jit(solution)/shard_map/ppermute | solution.py:1065
  43.1 2.8 %collective-permute-done.2.below_ref = f32[300,128]{1,0:T(8,128)S(1)} collective-permute-done((f32[300,128]{1,0:T(8,128)S(1)}, f32[300,128]{1,0:T(8,128)S(1)}, u32[]{:S(2)}, u32[]{:S(2)}) %collective-permute-start.2) | collective-permute-done | bytes 153632 | tf_op jit(solution)/shard_map/ppermute | solution.py:1066
  45.8 0.0 copy-start
  45.8 0.0 copy-start.1
  45.8 0.0 copy-start.2
  45.8 0.0 copy-start.3
  45.8 0.0 copy-start.4
  45.9 15.1 %gradient.1 = f32[768,128]{1,0:T(8,128)S(1)} custom-call(s32[128]{0:T(128)S(1)} %get-tuple-element.20.shift_ref, s32[128]{0:T(128)S(1)} %get-tuple-element.21.line_ref, f32[3,5,16,128]{3,2,1,0:T(8,128)S(1)} %get-tuple-element.22.image_ref, f32[300,128]{1,0:T(8,128)S(1)} %collective-permute-done.1.above_ref, f32[300,128]{1,0:T(8,128)S(1)} %collective-permute-done.2.below_ref, ...), custom_call_target="tpu_custom_call" | custom-call | tf_op jit(solution)/shard_map/gradient/pallas_call | solution.py:1067
  61.0 18.4 %all_to_all.10 = f32[128,1,768]{2,1,0:T(1,128)S(1)} all-to-all(f32[128,1,768]{2,1,0:T(1,128)S(1)} %bitcast.5), channel_id=1, replica_groups=mesh['strip'=128] {'strip'}, dimensions={0} | all-to-all | bytes 786432 | tf_op jit(solution)/shard_map/all_to_all | solution.py:994
  79.4 0.0 copy-done
  79.4 0.0 copy-done.1
  79.4 0.0 copy-done.2
  79.4 0.0 copy-done.3
  79.4 0.0 copy-done.4
  79.4 6.1 %pull.1 = f32[59,5120]{1,0:T(8,128)} custom-call(f32[4,12]{1,0:T(4,128)S(1)} %copy-done.2, s32[128]{0:T(128)S(1)} %copy-done.3, s32[128]{0:T(128)S(1)} %copy-done.4, f32[59,5120]{1,0:T(8,128)S(1)} %copy-done, s32[40,128]{1,0:T(8,128)S(1)} %copy-done.1, f32[768,128]{1,0:T(8,128)S(1)} %bitcast.7), custom_call_target="tpu_custom_call" | custom-call | tf_op jit(solution)/shard_map/pull/pallas_call | solution.py:1096
Async XLA Ops:
  7.8 23.6 %all-to-all-start = ((f32[128,1,768]{2,1,0:T(1,128)}), f32[128,1,768]{2,1,0:T(1,128)S(1)}, u32[]{:S(2)}, u32[]{:S(2)}) async-start(f32[128,1,768]{2,1,0:T(1,128)} %bitcast.8), calls=%async_computation | async-start | bytes 786432 | tf_op jit(solution)/shard_map/all_to_all | solution.py:994
  19.3 1.6 %collective-permute-start = (f32[280,128]{1,0:T(8,128)}, f32[280,128]{1,0:T(8,128)S(1)}, u32[]{:S(2)}, u32[]{:S(2)}) collective-permute-start(f32[280,128]{1,0:T(8,128)} %get-tuple-element.19), channel_id=1, source_target_pairs={{0,0},{1,1},{2,2},{3,3},{4,4},{5,5},{6,6},{7,7},{8,14},{9,15},{10,... | collective-permute-start | bytes 430088 | tf_op jit(solution)/shard_map/ppermute | solution.py:1029
  39.8 3.3 %collective-permute-start.1 = (f32[300,128]{1,0:T(8,128)S(1)}, f32[300,128]{1,0:T(8,128)S(1)}, u32[]{:S(2)}, u32[]{:S(2)}) collective-permute-start(f32[300,128]{1,0:T(8,128)S(1)} %get-tuple-element.23), channel_id=1, source_target_pairs={{0,1},{1,2},{2,3},{3,4},{4,5},{5,6},{6,7},{7,14},{14,15},{15,12},{... | collective-permute-start | bytes 460808 | tf_op jit(solution)/shard_map/ppermute | solution.py:1065
  40.9 5.0 %collective-permute-start.2 = (f32[300,128]{1,0:T(8,128)S(1)}, f32[300,128]{1,0:T(8,128)S(1)}, u32[]{:S(2)}, u32[]{:S(2)}) collective-permute-start(f32[300,128]{1,0:T(8,128)S(1)} %get-tuple-element.24), channel_id=1, source_target_pairs={{1,0},{2,1},{3,2},{4,3},{5,4},{6,5},{7,6},{14,7},{15,14},{12,15},{... | collective-permute-start | bytes 460808 | tf_op jit(solution)/shard_map/ppermute | solution.py:1066
  45.8 33.5 %copy-start = (f32[59,5120]{1,0:T(8,128)S(1)}, f32[59,5120]{1,0:T(8,128)}, u32[]{:S(2)}) copy-start(f32[59,5120]{1,0:T(8,128)} %params_ref.3) | copy-start | bytes 3624964
  45.8 33.5 %copy-start.1 = (s32[40,128]{1,0:T(8,128)S(1)}, s32[40,128]{1,0:T(8,128)}, u32[]{:S(2)}) copy-start(s32[40,128]{1,0:T(8,128)} %get-tuple-element.17.place_ref) | copy-start | bytes 61444
  45.8 33.5 %copy-start.2 = (f32[4,12]{1,0:T(4,128)S(1)}, f32[4,12]{1,0:T(4,128)}, u32[]{:S(2)}) copy-start(f32[4,12]{1,0:T(4,128)} %camera_ref.3) | copy-start | bytes 580
  45.8 33.5 %copy-start.3 = (s32[128]{0:T(128)S(1)}, s32[128]{0:T(128)}, u32[]{:S(2)}) copy-start(s32[128]{0:T(128)} %count_ref.3) | copy-start | bytes 1540
  45.8 33.5 %copy-start.4 = (s32[128]{0:T(128)S(1)}, s32[128]{0:T(128)}, u32[]{:S(2)}) copy-start(s32[128]{0:T(128)} %constant.2.clone.spot_ref) | copy-start | bytes 1540

commit v5 on v4

--- a/solution.py
+++ b/solution.py
@@ -247,7 +247,7 @@
         return start, held, last
 
     zero = jnp.zeros((8, 128), F32)
-    carry = lax.fori_loop(0, steps - 16, step, (jnp.int32(0), zero, zero), unroll=16)
+    carry = lax.fori_loop(0, steps - 16, step, (jnp.int32(0), zero, zero), unroll=56)
     for number in range(steps - 16, steps):
         carry = step(number, carry)
 
@@ -916,9 +916,8 @@
         )
         bounds = run_bounds(count_ref, strips)
 
-        def block_grads(block, carry):
-            rows = pl.ds(block * 8, 8)
-            place = place_ref[rows, :]
+        def gather(block):
+            place = place_ref[pl.ds(block * 8, 8), :]
             high = place >> 7
             low = place & 127
             got = [jnp.zeros((8, 128), F32)] * FEATS
@@ -927,7 +926,10 @@
                 for feature in range(FEATS):
                     value = pick(table_line(table_ref, row, feature), low)
                     got[feature] = jnp.where(same, value, got[feature])
-            camera = select_camera(camera_ref, place, bounds)
+            return tuple(got)
+
+        def grads(block, got):
+            camera = select_camera(camera_ref, place_ref[pl.ds(block * 8, 8), :], bounds)
             params = [
                 local_ref[pl.ds(block * (8 * PLACE) + number, 8, stride=PLACE), :]
                 for number in range(59)
@@ -935,13 +937,17 @@
             ignored, pull = jax.vjp(
                 lambda values: project(values, camera, focal, centre_x, centre_y), params
             )
-            for number, grad in enumerate(pull(got[:8])[0]):
+            for number, grad in enumerate(pull(list(got[:8]))[0]):
                 if number == 10:
                     grad = got[8] / (1.0 + jnp.exp(params[10]))
                 grads_ref[pl.ds(block * (8 * PLACE) + number, 8, stride=PLACE), :] = grad
             for tile in range(8):
                 result(block * 8 + tile).start()
-            return carry
+
+        def block_grads(block, got):
+            coming = gather(block + 1)
+            grads(block, got)
+            return coming
 
         def result(tile):
             return pltpu.make_async_copy(
@@ -952,7 +958,7 @@
 
         for copy in copies:
             copy.wait()
-        lax.fori_loop(0, 5, block_grads, 0)
+        grads(4, lax.fori_loop(0, 4, block_grads, gather(0)))
         for tile in range(ROWS):
             result(tile).wait()
 
@@ -1020,7 +1026,7 @@
             pltpu.VMEM((ROWS + 8, 128), jnp.int32),
             pltpu.VMEM((FEATS, ROWS, 128), F32),
             pltpu.VMEM(((ROWS + 2) * GAP, 128), F32),
-            pltpu.VMEM((ROWS * PLACE, 128), F32),
+            pltpu.VMEM(((ROWS + 1) * PLACE, 128), F32),
             pltpu.SemaphoreType.DMA((ROWS,)),
         ],
         name="owner",
@@ -1046,18 +1052,18 @@
             shape(strips, dtype=jnp.int32),
             shape(strips, dtype=jnp.int32),
             shape(2, 5120, 128),
-            shape(2, 640 * STEP, 128),
+            shape(2, 640 * STEP + 16, 128),
         ),
         in_specs=[VMEM, VMEM],
         out_specs=(VMEM, VMEM, VMEM, VMEM, VMEM, SMEM, SMEM, VMEM, VMEM),
         scratch_shapes=[
             pltpu.VMEM(((ROWS + 2) * GAP, 128), F32),
             pltpu.VMEM((ROWS, 128), jnp.int32),
-            pltpu.VMEM((ROWS * 24, 128), F32),
+            pltpu.VMEM(((ROWS + 5) * 24, 128), F32),
             pltpu.VMEM((640, 256), F32),
             pltpu.VMEM((640, 256), F32),
-            pltpu.VMEM((ROWS * GAP, 128), F32),
-            pltpu.VMEM((2, ROWS * GAP, 128), F32),
+            pltpu.VMEM(((ROWS + 1) * GAP, 128), F32),
+            pltpu.VMEM((2, (ROWS + 1) * GAP, 128), F32),
         ],
         compiler_params=pltpu.CompilerParams(vmem_limit_bytes=24 << 20),
         name="render",
@@ -1080,9 +1086,9 @@
             pltpu.VMEM((640, 256), F32),
             pltpu.VMEM((640, 256), F32),
             pltpu.VMEM((30, 8, 128), F32),
-            pltpu.VMEM((2, ROWS * GAP, 128), F32),
+            pltpu.VMEM((2, (ROWS + 1) * GAP, 128), F32),
             pltpu.VMEM((ROWS * 8 + 40, 128), F32),
-            pltpu.VMEM((ROWS * GAP, 128), F32),
+            pltpu.VMEM(((ROWS + 1) * GAP, 128), F32),
             pltpu.VMEM((FEATS, ROWS, 128), F32),
             pltpu.VMEM(((ROWS + 2) * GAP, 128), F32),
         ],
@@ -1101,8 +1107,8 @@
         scratch_shapes=[
             pltpu.VMEM(((ROWS + 2) * GAP, 128), F32),
             pltpu.VMEM((strips * 6 + 8, 128), F32),
-            pltpu.VMEM((ROWS * PLACE, 128), F32),
-            pltpu.VMEM((ROWS * PLACE, 128), F32),
+            pltpu.VMEM(((ROWS + 1) * PLACE, 128), F32),
+            pltpu.VMEM(((ROWS + 1) * PLACE, 128), F32),
             pltpu.SemaphoreType.DMA((ROWS,)),
             pltpu.SemaphoreType.DMA((ROWS,)),
         ],

time: 85.7 us -> 84.9 us (level)
  Pallas kernels: 38 us -> 37.1 us
where the time goes in v5:
time: 84.9 us; the launch traced here: 84.6 us
  Pallas kernels  37.1 us (44%)
  blocking collectives  18.4 us (22%)
  waiting for transfers between devices  14.6 us (17%)
  starting transfers between devices  14.4 us (17%)
    all_to_all x1, blocking collectives, exchange(): got = lax.all_to_all(sent, 'strip', split_axis=0, concat_axis=0, tiled=True)  18.4 us
    pallas_call x1, Pallas kernels, per_device(): pl.pallas_call(gradient_kernel, out_shape=shape(strips * 6, 128), in_spec...  15.2 us
    all_to_all x1, starting transfers between devices, exchange(): got = lax.all_to_all(sent, 'strip', split_axis=0, concat_axis=0, tiled=True)  11.5 us
    all_to_all x1, waiting for transfers between devices, exchange(): got = lax.all_to_all(sent, 'strip', split_axis=0, concat_axis=0, tiled=True)  10.6 us
    pallas_call x1, Pallas kernels, per_device(): pl.pallas_call(owner_kernel(focal, 0.5 * width, centre_y), out_shape=(sha...  7.78 us
    pallas_call x1, Pallas kernels, per_device(): pl.pallas_call(render_kernel, out_shape=(shape(3, 5, 16, 128), shape(300,...  7.76 us
    pallas_call x1, Pallas kernels, per_device(): pl.pallas_call(pull_kernel(focal, 0.5 * width, centre_y), out_shape=shape...  5.8 us
    ppermute x1, waiting for transfers between devices, per_device(): below = lax.ppermute(first, 'strip', behind)  2.77 us
  transfers between devices with their start and end apart: 4, of which 3 were waited for; matrix products, arithmetic and copies ran while one was open for 0% of the time, Pallas kernels for 1%

profile of v5, /device:TPU:1, one launch (start us, length us, event | category | flops | bytes accessed | tf_op | source)
XLA Modules:
  0.0 84.6 jit_solution(6701769259628572189)
XLA Ops:
  0.0 7.8 %owner.1 = (f32[768,128]{1,0:T(8,128)}, s32[40,128]{1,0:T(8,128)}, f32[280,128]{1,0:T(8,128)}) custom-call(f32[4,12]{1,0:T(4,128)} %camera_ref.3, s32[128]{0:T(128)} %count_ref.3, s32[128]{0:T(128)} %constant.2.clone.spot_ref, f32[59,5120]{1,0:T(8,128)} %params_ref.3, s32[80,128]{1,0:T(8,128)} %bitcast.9, f32[3,16,640]{2,1,0:T(8,128)} %target_ref.1, ...), custom_call_target="tpu_custom_call" | custom-call | tf_op jit(solution)/shard_map/owner/pallas_call | solution.py:1016
  7.8 11.5 %all-to-all-start = ((f32[128,1,768]{2,1,0:T(1,128)}), f32[128,1,768]{2,1,0:T(1,128)S(1)}, u32[]{:S(2)}, u32[]{:S(2)}) async-start(f32[128,1,768]{2,1,0:T(1,128)} %bitcast.8), calls=%async_computation | async-start | bytes 786432 | tf_op jit(solution)/shard_map/all_to_all | solution.py:1000
  19.3 1.6 %collective-permute-start = (f32[280,128]{1,0:T(8,128)}, f32[280,128]{1,0:T(8,128)S(1)}, u32[]{:S(2)}, u32[]{:S(2)}) collective-permute-start(f32[280,128]{1,0:T(8,128)} %get-tuple-element.19), channel_id=1, source_target_pairs={{0,0},{1,1},{2,2},{3,3},{4,4},{5,5},{6,6},{7,7},{8,14},{9,15},{10,... | collective-permute-start | bytes 430088 | tf_op jit(solution)/shard_map/ppermute | solution.py:1035
  20.9 0.0 collective-permute-done.moved_ref
  20.9 10.6 %all-to-all-done = f32[128,1,768]{2,1,0:T(1,128)S(1)} async-done(((f32[128,1,768]{2,1,0:T(1,128)}), f32[128,1,768]{2,1,0:T(1,128)S(1)}, u32[]{:S(2)}, u32[]{:S(2)}) %all-to-all-start) | async-done | bytes 393248 | tf_op jit(solution)/shard_map/all_to_all | solution.py:1000
  31.4 7.8 %render.1 = (f32[3,5,16,128]{3,2,1,0:T(8,128)S(1)}, f32[300,128]{1,0:T(8,128)S(1)}, f32[300,128]{1,0:T(8,128)S(1)}, f32[5,40,128]{2,1,0:T(8,128)S(1)}, f32[3,40,...) custom-call(f32[768,128]{1,0:T(8,128)S(1)} %bitcast.6, ...), custom_call_target="tpu_custom_call" | custom-call | tf_op jit(solution)/shard_map/render/pallas_call | solution.py:1044
  39.2 1.1 %collective-permute-start.1 = (f32[300,128]{1,0:T(8,128)S(1)}, f32[300,128]{1,0:T(8,128)S(1)}, u32[]{:S(2)}, u32[]{:S(2)}) collective-permute-start(f32[300,128]{1,0:T(8,128)S(1)} %get-tuple-element.23), channel_id=1, source_target_pairs={{0,1},{1,2},{2,3},{3,4},{4,5},{5,6},{6,7},{7,14},{14,15},{15,12},{... | collective-permute-start | bytes 460808 | tf_op jit(solution)/shard_map/ppermute | solution.py:1071
  40.3 0.3 collective-permute-start.2
  40.6 0.6 listed.1.place_ref
  41.2 1.2 %collective-permute-done.1.above_ref = f32[300,128]{1,0:T(8,128)S(1)} collective-permute-done((f32[300,128]{1,0:T(8,128)S(1)}, f32[300,128]{1,0:T(8,128)S(1)}, u32[]{:S(2)}, u32[]{:S(2)}) %collective-permute-start.1) | collective-permute-done | bytes 153632 | tf_op jit(solution)/shard_map/ppermute | solution.py:1071
  42.5 2.8 %collective-permute-done.2.below_ref = f32[300,128]{1,0:T(8,128)S(1)} collective-permute-done((f32[300,128]{1,0:T(8,128)S(1)}, f32[300,128]{1,0:T(8,128)S(1)}, u32[]{:S(2)}, u32[]{:S(2)}) %collective-permute-start.2) | collective-permute-done | bytes 153632 | tf_op jit(solution)/shard_map/ppermute | solution.py:1072
  45.2 0.0 copy-start
  45.2 0.0 copy-start.1
  45.2 0.0 copy-start.2
  45.2 0.0 copy-start.3
  45.3 0.0 copy-start.4
  45.3 15.2 %gradient.1 = f32[768,128]{1,0:T(8,128)S(1)} custom-call(s32[128]{0:T(128)S(1)} %get-tuple-element.20.shift_ref, s32[128]{0:T(128)S(1)} %get-tuple-element.21.line_ref, f32[3,5,16,128]{3,2,1,0:T(8,128)S(1)} %get-tuple-element.22.image_ref, f32[300,128]{1,0:T(8,128)S(1)} %collective-permute-done.1.above_ref, f32[300,128]{1,0:T(8,128)S(1)} %collective-permute-done.2.below_ref, ...), custom_call_target="tpu_custom_call" | custom-call | tf_op jit(solution)/shard_map/gradient/pallas_call | solution.py:1073
  60.4 18.4 %all_to_all.10 = f32[128,1,768]{2,1,0:T(1,128)S(1)} all-to-all(f32[128,1,768]{2,1,0:T(1,128)S(1)} %bitcast.5), channel_id=1, replica_groups=mesh['strip'=128] {'strip'}, dimensions={0} | all-to-all | bytes 786432 | tf_op jit(solution)/shard_map/all_to_all | solution.py:1000
  78.8 0.0 copy-done
  78.8 0.0 copy-done.1
  78.8 0.0 copy-done.2
  78.8 0.0 copy-done.3
  78.8 0.0 copy-done.4
  78.8 5.8 %pull.1 = f32[59,5120]{1,0:T(8,128)} custom-call(f32[4,12]{1,0:T(4,128)S(1)} %copy-done.2, s32[128]{0:T(128)S(1)} %copy-done.3, s32[128]{0:T(128)S(1)} %copy-done.4, f32[59,5120]{1,0:T(8,128)S(1)} %copy-done, s32[40,128]{1,0:T(8,128)S(1)} %copy-done.1, f32[768,128]{1,0:T(8,128)S(1)} %bitcast.7), custom_call_target="tpu_custom_call" | custom-call | tf_op jit(solution)/shard_map/pull/pallas_call | solution.py:1102
Async XLA Ops:
  7.8 23.6 %all-to-all-start = ((f32[128,1,768]{2,1,0:T(1,128)}), f32[128,1,768]{2,1,0:T(1,128)S(1)}, u32[]{:S(2)}, u32[]{:S(2)}) async-start(f32[128,1,768]{2,1,0:T(1,128)} %bitcast.8), calls=%async_computation | async-start | bytes 786432 | tf_op jit(solution)/shard_map/all_to_all | solution.py:1000
  19.3 1.6 %collective-permute-start = (f32[280,128]{1,0:T(8,128)}, f32[280,128]{1,0:T(8,128)S(1)}, u32[]{:S(2)}, u32[]{:S(2)}) collective-permute-start(f32[280,128]{1,0:T(8,128)} %get-tuple-element.19), channel_id=1, source_target_pairs={{0,0},{1,1},{2,2},{3,3},{4,4},{5,5},{6,6},{7,7},{8,14},{9,15},{10,... | collective-permute-start | bytes 430088 | tf_op jit(solution)/shard_map/ppermute | solution.py:1035
  39.2 3.3 %collective-permute-start.1 = (f32[300,128]{1,0:T(8,128)S(1)}, f32[300,128]{1,0:T(8,128)S(1)}, u32[]{:S(2)}, u32[]{:S(2)}) collective-permute-start(f32[300,128]{1,0:T(8,128)S(1)} %get-tuple-element.23), channel_id=1, source_target_pairs={{0,1},{1,2},{2,3},{3,4},{4,5},{5,6},{6,7},{7,14},{14,15},{15,12},{... | collective-permute-start | bytes 460808 | tf_op jit(solution)/shard_map/ppermute | solution.py:1071
  40.3 5.0 %collective-permute-start.2 = (f32[300,128]{1,0:T(8,128)S(1)}, f32[300,128]{1,0:T(8,128)S(1)}, u32[]{:S(2)}, u32[]{:S(2)}) collective-permute-start(f32[300,128]{1,0:T(8,128)S(1)} %get-tuple-element.24), channel_id=1, source_target_pairs={{1,0},{2,1},{3,2},{4,3},{5,4},{6,5},{7,6},{14,7},{15,14},{12,15},{... | collective-permute-start | bytes 460808 | tf_op jit(solution)/shard_map/ppermute | solution.py:1072
  45.2 33.6 %copy-start = (f32[59,5120]{1,0:T(8,128)S(1)}, f32[59,5120]{1,0:T(8,128)}, u32[]{:S(2)}) copy-start(f32[59,5120]{1,0:T(8,128)} %params_ref.3) | copy-start | bytes 3624964
  45.2 33.6 %copy-start.1 = (s32[40,128]{1,0:T(8,128)S(1)}, s32[40,128]{1,0:T(8,128)}, u32[]{:S(2)}) copy-start(s32[40,128]{1,0:T(8,128)} %get-tuple-element.17.place_ref) | copy-start | bytes 61444
  45.2 33.6 %copy-start.2 = (f32[4,12]{1,0:T(4,128)S(1)}, f32[4,12]{1,0:T(4,128)}, u32[]{:S(2)}) copy-start(f32[4,12]{1,0:T(4,128)} %camera_ref.3) | copy-start | bytes 580
  45.2 33.6 %copy-start.3 = (s32[128]{0:T(128)S(1)}, s32[128]{0:T(128)}, u32[]{:S(2)}) copy-start(s32[128]{0:T(128)} %count_ref.3) | copy-start | bytes 1540
  45.3 33.6 %copy-start.4 = (s32[128]{0:T(128)S(1)}, s32[128]{0:T(128)}, u32[]{:S(2)}) copy-start(s32[128]{0:T(128)} %constant.2.clone.spot_ref) | copy-start | bytes 1540

commit v6 on v5

--- a/solution.py
+++ b/solution.py
@@ -217,7 +217,7 @@
         held = jnp.where(shift + live >= 128, chunk, held)
         return start + live, held
 
-    lax.fori_loop(0, steps, step, (jnp.int32(0), jnp.zeros((1, 128), jnp.int32)), unroll=16)
+    lax.fori_loop(0, steps, step, (jnp.int32(0), jnp.zeros((1, 128), jnp.int32)), unroll=64)
 
 
 def compact_feats(chunk_ref, place_of, table_ref, steps, spot=None):
@@ -745,7 +745,7 @@
         parts_ref[2, at, :] = cross_grad
         return carry
 
-    lax.fori_loop(0, 20, similarity, 0)
+    lax.fori_loop(0, 20, similarity, 0, unroll=5)
     for tile in range(5):
         for slot in range(3):
             turned = tap_sum(

time: 84.9 us -> 84.6 us (level)
  no operation moved by 1% of the time
where the time goes in v6:
time: 84.6 us; the launch traced here: 84.2 us
  Pallas kernels  36.7 us (43%)
  blocking collectives  18.4 us (22%)
  waiting for transfers between devices  14.6 us (17%)
  starting transfers between devices  14.4 us (17%)
    all_to_all x1, blocking collectives, exchange(): got = lax.all_to_all(sent, 'strip', split_axis=0, concat_axis=0, tiled=True)  18.4 us
    pallas_call x1, Pallas kernels, per_device(): pl.pallas_call(gradient_kernel, out_shape=shape(strips * 6, 128), in_spec...  14.9 us
    all_to_all x1, starting transfers between devices, exchange(): got = lax.all_to_all(sent, 'strip', split_axis=0, concat_axis=0, tiled=True)  11.5 us
    all_to_all x1, waiting for transfers between devices, exchange(): got = lax.all_to_all(sent, 'strip', split_axis=0, concat_axis=0, tiled=True)  10.6 us
    pallas_call x1, Pallas kernels, per_device(): pl.pallas_call(render_kernel, out_shape=(shape(3, 5, 16, 128), shape(300,...  7.75 us
    pallas_call x1, Pallas kernels, per_device(): pl.pallas_call(owner_kernel(focal, 0.5 * width, centre_y), out_shape=(sha...  7.68 us
    pallas_call x1, Pallas kernels, per_device(): pl.pallas_call(pull_kernel(focal, 0.5 * width, centre_y), out_shape=shape...  5.8 us
    ppermute x1, waiting for transfers between devices, per_device(): below = lax.ppermute(first, 'strip', behind)  2.77 us
  transfers between devices with their start and end apart: 4, of which 3 were waited for; matrix products, arithmetic and copies ran while one was open for 0% of the time, Pallas kernels for 1%

profile of v6, /device:TPU:1, one launch (start us, length us, event | category | flops | bytes accessed | tf_op | source)
XLA Modules:
  0.0 84.2 jit_solution(13262430559027035425)
XLA Ops:
  0.0 7.7 %owner.1 = (f32[768,128]{1,0:T(8,128)}, s32[40,128]{1,0:T(8,128)}, f32[280,128]{1,0:T(8,128)}) custom-call(f32[4,12]{1,0:T(4,128)} %camera_ref.3, s32[128]{0:T(128)} %count_ref.3, s32[128]{0:T(128)} %constant.2.clone.spot_ref, f32[59,5120]{1,0:T(8,128)} %params_ref.3, s32[80,128]{1,0:T(8,128)} %bitcast.9, f32[3,16,640]{2,1,0:T(8,128)} %target_ref.1, ...), custom_call_target="tpu_custom_call" | custom-call | tf_op jit(solution)/shard_map/owner/pallas_call | solution.py:1016
  7.7 11.5 %all-to-all-start = ((f32[128,1,768]{2,1,0:T(1,128)}), f32[128,1,768]{2,1,0:T(1,128)S(1)}, u32[]{:S(2)}, u32[]{:S(2)}) async-start(f32[128,1,768]{2,1,0:T(1,128)} %bitcast.8), calls=%async_computation | async-start | bytes 786432 | tf_op jit(solution)/shard_map/all_to_all | solution.py:1000
  19.2 1.6 %collective-permute-start = (f32[280,128]{1,0:T(8,128)}, f32[280,128]{1,0:T(8,128)S(1)}, u32[]{:S(2)}, u32[]{:S(2)}) collective-permute-start(f32[280,128]{1,0:T(8,128)} %get-tuple-element.19), channel_id=1, source_target_pairs={{0,0},{1,1},{2,2},{3,3},{4,4},{5,5},{6,6},{7,7},{8,14},{9,15},{10,... | collective-permute-start | bytes 430088 | tf_op jit(solution)/shard_map/ppermute | solution.py:1035
  20.8 0.0 collective-permute-done.moved_ref
  20.8 10.6 %all-to-all-done = f32[128,1,768]{2,1,0:T(1,128)S(1)} async-done(((f32[128,1,768]{2,1,0:T(1,128)}), f32[128,1,768]{2,1,0:T(1,128)S(1)}, u32[]{:S(2)}, u32[]{:S(2)}) %all-to-all-start) | async-done | bytes 393248 | tf_op jit(solution)/shard_map/all_to_all | solution.py:1000
  31.3 7.8 %render.1 = (f32[3,5,16,128]{3,2,1,0:T(8,128)S(1)}, f32[300,128]{1,0:T(8,128)S(1)}, f32[300,128]{1,0:T(8,128)S(1)}, f32[5,40,128]{2,1,0:T(8,128)S(1)}, f32[3,40,...) custom-call(f32[768,128]{1,0:T(8,128)S(1)} %bitcast.6, ...), custom_call_target="tpu_custom_call" | custom-call | tf_op jit(solution)/shard_map/render/pallas_call | solution.py:1044
  39.1 1.1 %collective-permute-start.1 = (f32[300,128]{1,0:T(8,128)S(1)}, f32[300,128]{1,0:T(8,128)S(1)}, u32[]{:S(2)}, u32[]{:S(2)}) collective-permute-start(f32[300,128]{1,0:T(8,128)S(1)} %get-tuple-element.23), channel_id=1, source_target_pairs={{0,1},{1,2},{2,3},{3,4},{4,5},{5,6},{6,7},{7,14},{14,15},{15,12},{... | collective-permute-start | bytes 460808 | tf_op jit(solution)/shard_map/ppermute | solution.py:1071
  40.2 0.3 collective-permute-start.2
  40.5 0.6 listed.1.place_ref
  41.1 1.2 %collective-permute-done.1.above_ref = f32[300,128]{1,0:T(8,128)S(1)} collective-permute-done((f32[300,128]{1,0:T(8,128)S(1)}, f32[300,128]{1,0:T(8,128)S(1)}, u32[]{:S(2)}, u32[]{:S(2)}) %collective-permute-start.1) | collective-permute-done | bytes 153632 | tf_op jit(solution)/shard_map/ppermute | solution.py:1071
  42.4 2.8 %collective-permute-done.2.below_ref = f32[300,128]{1,0:T(8,128)S(1)} collective-permute-done((f32[300,128]{1,0:T(8,128)S(1)}, f32[300,128]{1,0:T(8,128)S(1)}, u32[]{:S(2)}, u32[]{:S(2)}) %collective-permute-start.2) | collective-permute-done | bytes 153632 | tf_op jit(solution)/shard_map/ppermute | solution.py:1072
  45.1 0.0 copy-start
  45.1 0.0 copy-start.1
  45.1 0.0 copy-start.2
  45.1 0.0 copy-start.3
  45.1 0.0 copy-start.4
  45.2 14.9 %gradient.1 = f32[768,128]{1,0:T(8,128)S(1)} custom-call(s32[128]{0:T(128)S(1)} %get-tuple-element.20.shift_ref, s32[128]{0:T(128)S(1)} %get-tuple-element.21.line_ref, f32[3,5,16,128]{3,2,1,0:T(8,128)S(1)} %get-tuple-element.22.image_ref, f32[300,128]{1,0:T(8,128)S(1)} %collective-permute-done.1.above_ref, f32[300,128]{1,0:T(8,128)S(1)} %collective-permute-done.2.below_ref, ...), custom_call_target="tpu_custom_call" | custom-call | tf_op jit(solution)/shard_map/gradient/pallas_call | solution.py:1073
  60.0 18.4 %all_to_all.10 = f32[128,1,768]{2,1,0:T(1,128)S(1)} all-to-all(f32[128,1,768]{2,1,0:T(1,128)S(1)} %bitcast.5), channel_id=1, replica_groups=mesh['strip'=128] {'strip'}, dimensions={0} | all-to-all | bytes 786432 | tf_op jit(solution)/shard_map/all_to_all | solution.py:1000
  78.4 0.0 copy-done
  78.4 0.0 copy-done.1
  78.4 0.0 copy-done.2
  78.4 0.0 copy-done.3
  78.4 0.0 copy-done.4
  78.4 5.8 %pull.1 = f32[59,5120]{1,0:T(8,128)} custom-call(f32[4,12]{1,0:T(4,128)S(1)} %copy-done.2, s32[128]{0:T(128)S(1)} %copy-done.3, s32[128]{0:T(128)S(1)} %copy-done.4, f32[59,5120]{1,0:T(8,128)S(1)} %copy-done, s32[40,128]{1,0:T(8,128)S(1)} %copy-done.1, f32[768,128]{1,0:T(8,128)S(1)} %bitcast.7), custom_call_target="tpu_custom_call" | custom-call | tf_op jit(solution)/shard_map/pull/pallas_call | solution.py:1102
Async XLA Ops:
  7.7 23.6 %all-to-all-start = ((f32[128,1,768]{2,1,0:T(1,128)}), f32[128,1,768]{2,1,0:T(1,128)S(1)}, u32[]{:S(2)}, u32[]{:S(2)}) async-start(f32[128,1,768]{2,1,0:T(1,128)} %bitcast.8), calls=%async_computation | async-start | bytes 786432 | tf_op jit(solution)/shard_map/all_to_all | solution.py:1000
  19.2 1.6 %collective-permute-start = (f32[280,128]{1,0:T(8,128)}, f32[280,128]{1,0:T(8,128)S(1)}, u32[]{:S(2)}, u32[]{:S(2)}) collective-permute-start(f32[280,128]{1,0:T(8,128)} %get-tuple-element.19), channel_id=1, source_target_pairs={{0,0},{1,1},{2,2},{3,3},{4,4},{5,5},{6,6},{7,7},{8,14},{9,15},{10,... | collective-permute-start | bytes 430088 | tf_op jit(solution)/shard_map/ppermute | solution.py:1035
  39.1 3.3 %collective-permute-start.1 = (f32[300,128]{1,0:T(8,128)S(1)}, f32[300,128]{1,0:T(8,128)S(1)}, u32[]{:S(2)}, u32[]{:S(2)}) collective-permute-start(f32[300,128]{1,0:T(8,128)S(1)} %get-tuple-element.23), channel_id=1, source_target_pairs={{0,1},{1,2},{2,3},{3,4},{4,5},{5,6},{6,7},{7,14},{14,15},{15,12},{... | collective-permute-start | bytes 460808 | tf_op jit(solution)/shard_map/ppermute | solution.py:1071
  40.2 5.0 %collective-permute-start.2 = (f32[300,128]{1,0:T(8,128)S(1)}, f32[300,128]{1,0:T(8,128)S(1)}, u32[]{:S(2)}, u32[]{:S(2)}) collective-permute-start(f32[300,128]{1,0:T(8,128)S(1)} %get-tuple-element.24), channel_id=1, source_target_pairs={{1,0},{2,1},{3,2},{4,3},{5,4},{6,5},{7,6},{14,7},{15,14},{12,15},{... | collective-permute-start | bytes 460808 | tf_op jit(solution)/shard_map/ppermute | solution.py:1072
  45.1 33.3 %copy-start = (f32[59,5120]{1,0:T(8,128)S(1)}, f32[59,5120]{1,0:T(8,128)}, u32[]{:S(2)}) copy-start(f32[59,5120]{1,0:T(8,128)} %params_ref.3) | copy-start | bytes 3624964
  45.1 33.3 %copy-start.1 = (s32[40,128]{1,0:T(8,128)S(1)}, s32[40,128]{1,0:T(8,128)}, u32[]{:S(2)}) copy-start(s32[40,128]{1,0:T(8,128)} %get-tuple-element.17.place_ref) | copy-start | bytes 61444
  45.1 33.3 %copy-start.2 = (f32[4,12]{1,0:T(4,128)S(1)}, f32[4,12]{1,0:T(4,128)}, u32[]{:S(2)}) copy-start(f32[4,12]{1,0:T(4,128)} %camera_ref.3) | copy-start | bytes 580
  45.1 33.3 %copy-start.3 = (s32[128]{0:T(128)S(1)}, s32[128]{0:T(128)}, u32[]{:S(2)}) copy-start(s32[128]{0:T(128)} %count_ref.3) | copy-start | bytes 1540
  45.1 33.3 %copy-start.4 = (s32[128]{0:T(128)S(1)}, s32[128]{0:T(128)}, u32[]{:S(2)}) copy-start(s32[128]{0:T(128)} %constant.2.clone.spot_ref) | copy-start | bytes 1540
